TPU v7x, 32 devices: a whole 2x2x4 slice. The times are simulated.
32 devices in a mesh: batch: 16 (over z, y, core), head: 2 (over x).
Axes of the slice: x: 2, y: 2, z: 4, core: 2. Of those that a mesh axis runs over, the one named last changes fastest.
Arguments:
- tokens: bfloat16 [16384, 768], P('batch', 'head'), may hold values from -6 to 6
- w_qkv: bfloat16 [768, 3, 768], P(None, None, 'head'), may hold values from -0.21875 to 0.21875
- w_out: bfloat16 [768, 768], replicated, may hold values from -3 to 3
- gain_one: float32 [768], replicated, may hold values from 0.25 to 1.75
- attention_norm_bias: float32 [768], replicated, may hold values from -3 to 3
- w_up: bfloat16 [768, 3072], P(None, 'head'), may hold values from -0.21875 to 0.21875
- b_up: float32 [3072], P('head'), may hold values from -3 to 3
- w_down: bfloat16 [3072, 768], P('head'), may hold values from -0.109375 to 0.109375
- gain_two: float32 [768], replicated, may hold values from 0.25 to 1.75
- shift_two: float32 [768], replicated, may hold values from -3 to 3
- block_perm: int32 [12, 2], P('head'), may hold values from 0 to 1, each once within a row
- mask_index: int32 [16, 256], P('batch'), may hold values from 0 to 1023, as said below
- mask_count: int32 [16], P('batch'), may hold values from 51 to 256, as said below
- cotangent: bfloat16 [16, 256, 768], P('batch'), may hold values from -6 to 6
Outputs:
- result: bfloat16 [16384, 768], P('batch', 'head')
- grad_tokens: bfloat16 [16384, 768], P('batch', 'head')
- grad_w_qkv: float32 [768, 3, 768], P(None, None, 'head')
- grad_w_out: float32 [768, 768], P('head')
- grad_gain_one: float32 [768], replicated
- grad_shift_one: float32 [768], replicated
- grad_w_up: float32 [768, 3072], P(None, 'head')
- up_bias_gradient: float32 [3072], P('head')
- grad_w_down: float32 [3072, 768], P('head')
- grad_gain_two: float32 [768], replicated
- grad_shift_two: float32 [768], replicated
Inputs may be any that keep to these rules, and one draw needn't show every extreme that they name: `mask_index`: each row holds 256 distinct positions of one sequence; only its first mask_count entries are used. `mask_count`: some sequence has exactly 256 masked positions.
All inputs are finite; a program needn't handle non-finite values.
Results may differ from a plain program's by a relative error of at most 0.019.
Values may be sent and summed in bfloat16 or wider, within the bound.
A program may use at most 192 MiB of HBM per device.

v0:
```python
import jax
import jax.numpy as jnp
from jax import lax
from jax.sharding import PartitionSpec as P

HEAD_DIM = 64


norm_eps = 1e-06
root_half = 0.7071067811865476
inv_root_two_pi = 0.3989422804014327


def norm_forward(values, gain_vec, shift_vec):
    centered = values - jnp.mean(values, axis=-1, keepdims=True)
    inverse = lax.rsqrt(jnp.mean(centered * centered, axis=-1, keepdims=True) + norm_eps)
    normal = centered * inverse
    return (normal * gain_vec + shift_vec, normal, inverse)


def norm_backward(upstream, normal, inverse, gain_vec):
    scaled = upstream * gain_vec
    centered_gradient = (
        scaled
        - jnp.mean(scaled, axis=-1, keepdims=True)
        - normal * jnp.mean(scaled * normal, axis=-1, keepdims=True)
    )
    return (
        centered_gradient * inverse,
        jnp.sum(upstream * normal, axis=0),
        jnp.sum(upstream, axis=0),
    )


def gelu_slope_of(hidden_in):
    return 0.5 * (
        1.0 + jax.scipy.special.erf(hidden_in * root_half)
    ) + hidden_in * inv_root_two_pi * jnp.exp(-0.5 * hidden_in * hidden_in)


def pick_blocks(blocks, chosen):
    picked = jnp.zeros_like(blocks)
    for source in range(blocks.shape[2]):
        mask_here = (chosen == source)[None, :, :, None, None]
        picked = jnp.where(mask_here, blocks[:, :, source : source + 1], picked)
    return picked


def place_blocks(blocks, chosen):
    placed = []
    for target in range(blocks.shape[2]):
        mask_here = (chosen == target)[None, :, :, None, None]
        placed.append(jnp.sum(jnp.where(mask_here, blocks, 0.0), axis=2))
    return jnp.stack(placed, axis=2)


def body(
    tokens,
    w_qkv,
    w_out,
    gain_one,
    attention_norm_bias,
    w_up,
    b_up,
    w_down,
    gain_two,
    shift_two,
    block_perm,
    mask_index,
    mask_count,
    cotangent,
):
    model_width = w_out.shape[0]
    local_width = w_qkv.shape[2]
    head_size = HEAD_DIM
    groups = local_width // head_size
    seq_count = mask_count.shape[0]
    row_count = tokens.shape[0]
    seq_len = row_count // seq_count
    blocks = block_perm.shape[1]
    block_len = seq_len // blocks
    head_pos = lax.axis_index("head")
    out_width = model_width // lax.axis_size("head")
    score_scale = head_size ** (-0.5)
    full_tokens = lax.all_gather(tokens, "head", axis=1, tiled=True)
    flat_qkv = w_qkv.reshape(model_width, 3 * local_width)
    qkv_low = jnp.dot(full_tokens, flat_qkv, preferred_element_type=jnp.float32).astype(
        jnp.bfloat16
    )
    arranged = qkv_low.reshape(seq_count, blocks, block_len, 3, groups, head_size).transpose(
        3, 0, 4, 1, 2, 5
    )
    queries = arranged[0]
    key_sel = pick_blocks(arranged[1], block_perm)
    value_sel = pick_blocks(arranged[2], block_perm)
    scores = (
        jnp.einsum("sgbqd,sgbkd->sgbqk", queries, key_sel, preferred_element_type=jnp.float32)
        * score_scale
    )
    row_max = jnp.max(scores, axis=-1, keepdims=True)
    log_total = row_max + jnp.log(jnp.sum(jnp.exp(scores - row_max), axis=-1, keepdims=True))
    weights_low = jnp.exp(scores - log_total).astype(jnp.bfloat16)
    context = jnp.einsum(
        "sgbqk,sgbkd->sgbqd", weights_low, value_sel, preferred_element_type=jnp.float32
    ).astype(jnp.bfloat16)
    context_rows = context.transpose(0, 2, 3, 1, 4).reshape(row_count, local_width)
    attn_out = jnp.dot(
        lax.all_gather(context_rows, "head", axis=1, tiled=True),
        w_out,
        preferred_element_type=jnp.float32,
    )
    normed_one, normal_one, inverse_one = norm_forward(
        full_tokens.astype(jnp.float32) + attn_out, gain_one, attention_norm_bias
    )
    normed_low = normed_one.astype(jnp.bfloat16)
    hidden_in = jnp.dot(normed_low, w_up, preferred_element_type=jnp.float32) + b_up
    hidden = jax.nn.gelu(hidden_in, approximate=False).astype(jnp.bfloat16)
    partial_out = jnp.dot(hidden, w_down, preferred_element_type=jnp.float32)
    branch = lax.psum(partial_out.astype(jnp.bfloat16), "head").astype(jnp.float32)
    normed_two, normal_two, inverse_two = norm_forward(normed_one + branch, gain_two, shift_two)
    result = lax.dynamic_slice_in_dim(normed_two, head_pos * out_width, out_width, 1).astype(
        jnp.bfloat16
    )
    max_rows = mask_index.shape[1]
    live_slots = jnp.arange(max_rows, dtype=jnp.int32)[None, :] < mask_count[:, None]
    places = jnp.arange(seq_len, dtype=jnp.int32)
    block_picker = (
        (mask_index[:, :, None] == places[None, None, :]) & live_slots[:, :, None]
    ).astype(jnp.bfloat16)
    upstream = jnp.einsum(
        "otv,otg->ovg", block_picker, cotangent, preferred_element_type=jnp.float32
    ).reshape(row_count, model_width)
    grad_pre_two, grad_gain_two, grad_shift_two = norm_backward(
        upstream, normal_two, inverse_two, gain_two
    )
    grad_branch = grad_pre_two.astype(jnp.bfloat16)
    grad_w_down = jnp.dot(hidden.T, grad_branch, preferred_element_type=jnp.float32)
    hidden_gradient = jnp.dot(grad_branch, w_down.T, preferred_element_type=jnp.float32)
    grad_in = (hidden_gradient * gelu_slope_of(hidden_in)).astype(jnp.bfloat16)
    up_bias_gradient = jnp.sum(grad_in, axis=0, dtype=jnp.float32)
    grad_w_up = jnp.dot(normed_low.T, grad_in, preferred_element_type=jnp.float32)
    back_part = jnp.dot(grad_in, w_up.T, preferred_element_type=jnp.float32)
    grad_normed = grad_pre_two + lax.psum(back_part.astype(jnp.bfloat16), "head").astype(
        jnp.float32
    )
    prenorm_first_gradient, grad_gain_one, grad_shift_one = norm_backward(
        grad_normed, normal_one, inverse_one, gain_one
    )
    grad_attn = prenorm_first_gradient.astype(jnp.bfloat16)
    grad_w_out = jnp.dot(context_rows.T, grad_attn, preferred_element_type=jnp.float32)
    own_rows = lax.dynamic_slice_in_dim(w_out, head_pos * local_width, local_width, 0)
    grad_context = jnp.dot(grad_attn, own_rows.T, preferred_element_type=jnp.float32).astype(
        jnp.bfloat16
    )
    grad_ctx_blocks = grad_context.reshape(
        seq_count, blocks, block_len, groups, head_size
    ).transpose(0, 3, 1, 2, 4)
    again = (
        jnp.einsum("sgbqd,sgbkd->sgbqk", queries, key_sel, preferred_element_type=jnp.float32)
        * score_scale
    )
    probs_full = jnp.exp(again - log_total)
    grad_probs = jnp.einsum(
        "sgbqd,sgbkd->sgbqk", grad_ctx_blocks, value_sel, preferred_element_type=jnp.float32
    )
    row_inner = jnp.sum(grad_probs * probs_full, axis=-1, keepdims=True)
    grad_scores = (probs_full * (grad_probs - row_inner)).astype(jnp.bfloat16)
    grad_value_sel = jnp.einsum(
        "sgbqk,sgbqd->sgbkd",
        probs_full.astype(jnp.bfloat16),
        grad_ctx_blocks,
        preferred_element_type=jnp.float32,
    )
    grad_query = (
        jnp.einsum("sgbqk,sgbkd->sgbqd", grad_scores, key_sel, preferred_element_type=jnp.float32)
        * score_scale
    )
    grad_key_sel = (
        jnp.einsum("sgbqk,sgbqd->sgbkd", grad_scores, queries, preferred_element_type=jnp.float32)
        * score_scale
    )
    grad_key = place_blocks(grad_key_sel, block_perm)
    grad_value = place_blocks(grad_value_sel, block_perm)
    grad_qkv = jnp.stack((grad_query, grad_key, grad_value), axis=0).astype(jnp.bfloat16)
    grad_qkv_rows = grad_qkv.transpose(1, 3, 4, 0, 2, 5).reshape(row_count, 3 * local_width)
    grad_w_qkv = jnp.dot(full_tokens.T, grad_qkv_rows, preferred_element_type=jnp.float32).reshape(
        model_width, 3, local_width
    )
    input_part = jnp.dot(grad_qkv_rows, flat_qkv.T, preferred_element_type=jnp.float32)
    own_grad = lax.dynamic_slice_in_dim(prenorm_first_gradient, head_pos * out_width, out_width, 1)
    grad_tokens = (
        lax.psum_scatter(
            input_part.astype(jnp.bfloat16), "head", scatter_dimension=1, tiled=True
        ).astype(jnp.float32)
        + own_grad
    ).astype(jnp.bfloat16)
    (
        grad_w_qkv,
        grad_w_out,
        grad_gain_one,
        grad_shift_one,
        grad_w_up,
        up_bias_gradient,
        grad_w_down,
        grad_gain_two,
        grad_shift_two,
    ) = lax.psum(
        (
            grad_w_qkv,
            grad_w_out,
            grad_gain_one,
            grad_shift_one,
            grad_w_up,
            up_bias_gradient,
            grad_w_down,
            grad_gain_two,
            grad_shift_two,
        ),
        "batch",
    )
    return (
        result,
        grad_tokens,
        grad_w_qkv,
        grad_w_out,
        grad_gain_one,
        grad_shift_one,
        grad_w_up,
        up_bias_gradient,
        grad_w_down,
        grad_gain_two,
        grad_shift_two,
    )


def solution(mesh):
    return jax.shard_map(
        body,
        mesh=mesh,
        in_specs=(
            P("batch", "head"),
            P(None, None, "head"),
            P(),
            P(),
            P(),
            P(None, "head"),
            P("head"),
            P("head", None),
            P(),
            P(),
            P("head", None),
            P("batch", None),
            P("batch"),
            P("batch", None, None),
        ),
        out_specs=(
            P("batch", "head"),
            P("batch", "head"),
            P(None, None, "head"),
            P("head", None),
            P(),
            P(),
            P(None, "head"),
            P("head"),
            P("head", None),
            P(),
            P(),
        ),
        check_vma=False,
    )
```

profile of v0, /device:TPU:0, one launch (start us, length us, event | category | flops | bytes accessed | tf_op | source)
XLA Modules:
  0.0 607.5 jit_solution(10802624537217628534)
XLA Ops:
  7.2 2.4 copy.42
  9.8 0.7 broadcast_compare_fusion.1
  10.7 3.8 copy.43
  14.5 25.6 %all-gather.3.cloned.1.call-done = bf16[1024,768]{0,1:T(8,128)(2,1)} async-done(((bf16[1024,384]{0,1:T(8,128)(2,1)}), bf16[1024,768]{0,1:T(8,128)(2,1)}) %all-gather.3.cloned.1.call-update) | async-done | bytes 1572880 | tf_op jit(solution)/shard_map/all_gather | solution.py:85
  40.1 5.6 convolution_convert_fusion
  45.7 4.3 copy.44
  49.9 6.6 %reshape.333 = bf16[1,2,512,3,6,64]{2,1,5,4,3,0:T(2,128)(2,1)} reshape(bf16[1024,1152]{0,1:T(8,128)(2,1)} %copy.44) | data formatting | bytes 4718592 | tf_op jit(solution)/shard_map/reshape | solution.py:90
  56.5 2.2 copy.83
  59.0 1.1 copy-done.11
  60.1 2.4 multiply_reduce_fusion.1
  62.5 2.1 exponential_reduce_fusion
  64.7 2.4 copy-done.2
  67.0 2.7 fusion.19
  69.7 0.8 copy.49
  70.6 1.0 copy.72
  71.9 27.1 %all-gather.5.cloned.1.call-done = bf16[1024,768]{0,1:T(8,128)(2,1)} async-done(((bf16[1024,384]{0,1:T(8,128)(2,1)}), bf16[1024,768]{0,1:T(8,128)(2,1)}) %all-gather.5.cloned.1.call-update) | async-done | bytes 1572880 | tf_op jit(solution)/shard_map/all_gather | solution.py:108
  98.9 3.7 fusion.75
  103.5 19.0 %fusion.3 = (bf16[1024,1536]{1,0:T(8,128)(2,1)S(1)}, f32[1024,1536]{1,0:T(8,128)}) fusion(f32[1536]{0:T(1024)S(1)} %copy-done.37, bf16[768,1536]{1,0:T(8,128)(2,1)S(1)} %copy-done, f32[1024,768]{0,1:T(8,128)S(1)} %get-tuple-element.69, f32[768]{0:T(1024)S(1)} %copy-done.31, f32[768]{0:T(1024)S(1)} %copy-done.21, f32[1024]{0:T(1024)S(1)} %add_rsqrt_fusion.1, ...), kind=kOutput, calls=%fused_computation.10 | convolution fusion | flops 2523660288 | bytes 14962688 | tf_op jit(solution)/shard_map/dot_general | solution.py:116
  122.5 1.6 copy-done.39
  124.2 3.8 convolution_convert_fusion.3
  128.9 4.2 fusion.76
  133.1 3.8 copy.51
  136.9 42.8 %all-reduce.6.cloned.1.call-done = bf16[1024,768]{0,1:T(8,128)(2,1)} async-done(((bf16[1024,768]{0,1:T(8,128)(2,1)}), bf16[1024,768]{0,1:T(8,128)(2,1)}) %all-reduce.6.cloned.1.call-update) | async-done | bytes 1572880 | tf_op jit(solution)/shard_map/psum | solution.py:119
  179.7 3.2 fusion.74
  183.3 1.5 copy-done.9
  184.8 1.6 multiply_reduce_fusion.2
  186.4 0.6 subtract_multiply_fusion.1
  187.0 1.1 copy-done.10
  188.1 1.4 copy-done.35
  189.6 5.4 convert_reduce_fusion
  194.9 1.7 copy-done.40
  196.6 3.8 convolution_convert_fusion.2
  200.7 51.4 %all-reduce.8.cloned.1.call-done = bf16[1024,768]{0,1:T(8,128)(2,1)} async-done(((bf16[1024,768]{0,1:T(8,128)(2,1)}), bf16[1024,768]{0,1:T(8,128)(2,1)}) %all-reduce.8.cloned.1.call-update) | async-done | bytes 1572880 | tf_op jit(solution)/shard_map/psum | solution.py:143
  252.1 5.4 multiply_reduce_fusion.3
  257.7 1.0 subtract_multiply_fusion
  258.7 1.7 copy-done.6
  260.5 1.0 convolution_convert_fusion.4
  261.8 0.6 reshape.337
  262.4 11.5 %multiply_reduce_fusion = (f32[6,2,512]{2,1,0:T(2,128)S(1)}, f32[6,2,512,512]{2,3,1,0:T(8,128)}) fusion(f32[6,2,512,512]{2,3,1,0:T(8,128)} %copy-done.2, f32[6,2,512]{2,1,0:T(2,128)S(1)} %copy-done.19, pred[6,2]{1,0:T(8,128)(4,1)S(1)} %copy.47, pred[6,2]{1,0:T(8,128)(4,1)S(1)} %copy.46, bf16[6,512,64]{1,2,0:T(8,128)(2,1)S(1)} %get-tuple-element.78, ...), kind=kOutput, calls=%fused_computation.1 | convolution fusion | flops 416016384 | bytes 26787864 | tf_op jit(solution)/shard_map/sgbqd,sgbkd->sgbqk/dot_general | solution.py:163
  274.1 7.0 %multiply_convert_fusion = bf16[6,2,512,512]{2,3,1,0:T(8,128)(2,1)S(1)} fusion(f32[6,2,512,512]{2,3,1,0:T(8,128)} %get-tuple-element.73, f32[6,2,512,512]{2,3,1,0:T(8,128)S(1)} %bitcast.99, f32[6,2,512]{2,1,0:T(2,128)S(1)} %get-tuple-element.72, f32[6,2,512]{2,1,0:T(2,128)S(1)} %copy-done.19), kind=kLoop, calls=%fused_computation | loop fusion | flops 15728640 | bytes 31506432 | tf_op jit(solution)/shard_map/convert_element_type | solution.py:167
  281.1 3.1 convolution_multiply_fusion
  284.2 1.3 fusion.20
  285.5 7.4 %select_reduce_fusion.1 = (bf16[6,512,64]{1,2,0:T(8,128)(2,1)S(1)}, bf16[6,512,64]{1,2,0:T(8,128)(2,1)S(1)}, bf16[6,512,64]{1,2,0:T(8,128)(2,1)S(1)}, bf16[6,512,64]{1,2,0:T(8,128)(2,1)S(1)}) fusion(pred[6,2]{1,0:T(8,128)(4,1)S(1)} %copy.47, pred[6,2]{1,0:T(8,128)(4,1)S(1)} %copy.46, f32[6,2,512,64]{2,3,1,0:T(8,128)S(1)} %convolution_multiply_fusion, ...), kind=kOutput, calls=%fused_computation.60 | convolution fusion | flops 414449664 | bytes 16539672 | tf_op jit(solution)/shard_map/sgbqk,sgbqd->sgbkd/dot_general | solution.py:168
  293.3 2.4 copy.59
  295.7 0.6 copy.73
  296.4 0.8 copy-done.16
  297.2 3.4 convolution_convert_fusion.1
  301.0 7.8 %fusion.31 = f32[1536,768]{1,0:T(8,128)} fusion(bf16[1024,1536]{1,0:T(8,128)(2,1)} %copy-done.39, f32[1024,768]{0,1:T(8,128)} %copy-done.7), kind=kOutput, calls=%fused_computation.82 | convolution fusion | flops 2416705536 | bytes 11010048 | tf_op jit(solution)/shard_map/dot_general | solution.py:137
  308.9 4.5 fusion.70
  313.4 3.8 fusion.77
  317.3 5.2 copy.61
  322.5 3.8 fusion.28
  326.3 0.7 copy-done.25
  327.1 1.6 fusion.18
  328.7 1.2 copy.63
  329.9 64.1 %all-reduce = (f32[768]{0:T(1024)}, f32[768]{0:T(1024)}, f32[1536]{0:T(1024)}, f32[768]{0:T(1024)}, f32[768]{0:T(1024)}) all-reduce(f32[768]{0:T(1024)S(1)} %copy-done.28, f32[768]{0:T(1024)S(1)} %copy-done.29, f32[1536]{0:T(1024)S(1)} %copy-done.30, f32[768]{0:T(1024)S(1)} %copy-done.27, ...), channel_id=1, replica_groups=mesh['batch'=16,'head'=2] {'batch'}, use_global_device_ids=true, to_apply=%region_21.22 | all-reduce | flops 4608 | bytes 36864 | tf_op jit(solution)/shard_map/psum | solution.py:207
  394.0 1.9 add_convert_fusion
  395.9 1.2 copy.64
  397.0 192.2 %all-reduce.10.cloned.1.call-done = (f32[768,3,384]{2,0,1:T(8,128)}, f32[384,768]{1,0:T(8,128)}, f32[768,1536]{1,0:T(8,128)}, f32[1536,768]{1,0:T(8,128)}) async-done(((f32[768,3,384]{2,0,1:T(8,128)}, f32[384,768]{1,0:T(8,128)}, f32[768,1536]{1,0:T(8,128)}, f32[1536,768]{1,0:T(8,128)}), (f32[768,3,384]{2,0,1:T(8,128)}, f32[384,768]{1,0:T(8,128)}, f32[768,1536]{1,0:T(8,128)}, ...) | async-done | bytes 14155792 | tf_op jit(solution)/shard_map/psum | solution.py:207
  589.3 4.2 copy.91
  593.5 1.0 copy.92
  594.5 2.4 copy.93
  596.9 0.6 slice-done.3
  597.9 2.2 copy.94
  (130 shorter events, 4.7 us)
Async XLA Ops:
  7.2 96.0 %copy-start = (bf16[768,1536]{1,0:T(8,128)(2,1)S(1)}, bf16[768,1536]{1,0:T(8,128)(2,1)}, u32[]{:S(2)}) copy-start(bf16[768,1536]{1,0:T(8,128)(2,1)} %param.19) | copy-start | bytes 7077892
  7.2 32.9 %all-gather.3.cloned.1.call-start = ((), (), s32[]{:S(2)}) async-start(), calls=%async_computation.1 | async-start | bytes 2359296 | tf_op jit(solution)/shard_map/all_gather | solution.py:85
  9.7 89.2 %all-gather.5.cloned.1.call-start = ((), (), s32[]{:S(2)}) async-start(), calls=%async_computation.2 | async-start | bytes 2359296 | tf_op jit(solution)/shard_map/all_gather | solution.py:108
  58.7 1.4 copy-start.11
  59.0 5.7 copy-start.14
  62.5 4.5 copy-start.2
  64.7 5.1 copy-start.18
  71.6 108.1 %all-reduce.6.cloned.1.call-start = ((), (), s32[]{:S(2)}) async-start(), calls=%async_computation.3 | async-start | bytes 3145728 | tf_op jit(solution)/shard_map/psum | solution.py:119
  102.7 19.8 %copy-start.3 = (f32[1024,768]{0,1:T(8,128)}, f32[1024,768]{0,1:T(8,128)S(1)}, u32[]{:S(2)}) copy-start(f32[1024,768]{0,1:T(8,128)S(1)} %get-tuple-element.69) | copy-start | bytes 9437188
  102.7 0.7 copy-start.21
  102.7 0.8 copy-start.31
  102.7 0.8 copy-start.37
  103.5 20.6 %copy-start.34 = (bf16[1536,768]{1,0:T(8,128)(2,1)S(1)}, bf16[1536,768]{1,0:T(8,128)(2,1)}, u32[]{:S(2)}) copy-start(bf16[1536,768]{1,0:T(8,128)(2,1)} %param.21) | copy-start | bytes 7077892
  122.5 1.6 copy-start.39
  128.0 124.1 %all-reduce.8.cloned.1.call-start = ((), (), s32[]{:S(2)}) async-start(), calls=%async_computation.4 | async-start | bytes 3145728 | tf_op jit(solution)/shard_map/psum | solution.py:143
  182.9 1.9 copy-start.9
  182.9 1.9 copy-start.24
  182.9 5.2 slice-start.7
  184.8 3.4 slice-start.8
  186.4 1.7 copy-start.10
  186.4 3.2 copy-start.35
  186.4 3.2 copy-start.38
  188.1 6.8 %copy-start.7 = (f32[1024,768]{0,1:T(8,128)}, f32[1024,768]{0,1:T(8,128)S(1)}, u32[]{:S(2)}) copy-start(f32[1024,768]{0,1:T(8,128)S(1)} %subtract_multiply_fusion.1) | copy-start | bytes 9437188
  194.9 1.7 copy-start.40
  200.4 193.6 %reduce-scatter.2.cloned.1.call-start = ((), (), s32[]{:S(2)}) async-start(), calls=%async_computation.5 | async-start | bytes 2359296 | tf_op jit(solution)/shard_map/reduce_scatter | solution.py:192
  200.7 56.8 %copy-start.22 = (f32[768]{0:T(1024)S(1)}, f32[768]{0:T(1024)}, u32[]{:S(2)}) copy-start(f32[768]{0:T(1024)} %param.17) | copy-start | bytes 9220
  252.1 5.4 copy-start.4
  252.1 5.4 copy-start.8
  252.1 5.6 copy-start.13
  257.7 2.8 copy-start.20
  258.7 1.7 copy-start.6
  260.5 1.9 copy-start.15
  260.5 1.9 copy-start.19
  262.4 11.5 %slice-start = ((s8[12582912]{0:T(1024)(128)(4,1)}), s8[4194304]{0:T(1024)(128)(4,1)S(1)}, s32[]{:S(2)}) async-start(s8[12582912]{0:T(1024)(128)(4,1)} %bitcast.98), calls=%async_computation.7 | async-start | bytes 8388608
  262.4 11.5 %slice-start.1 = ((s8[12582912]{0:T(1024)(128)(4,1)}), s8[4194304]{0:T(1024)(128)(4,1)S(1)}, s32[]{:S(2)}) async-start(s8[12582912]{0:T(1024)(128)(4,1)} %bitcast.98), calls=%async_computation.8 | async-start | bytes 8388608
  262.4 11.7 %slice-start.2 = ((s8[12582912]{0:T(1024)(128)(4,1)}), s8[4194304]{0:T(1024)(128)(4,1)S(1)}, s32[]{:S(2)}) async-start(s8[12582912]{0:T(1024)(128)(4,1)} %bitcast.98), calls=%async_computation.9 | async-start | bytes 8388608
  295.7 1.5 copy-start.16
  300.6 8.2 %copy-start.23 = (f32[768]{0:T(1024)S(1)}, f32[768]{0:T(1024)}, u32[]{:S(2)}) copy-start(f32[768]{0:T(1024)} %param.17) | copy-start | bytes 9220
  300.6 8.2 %copy-start.32 = (f32[768]{0:T(1024)S(1)}, f32[768]{0:T(1024)}, u32[]{:S(2)}) copy-start(f32[768]{0:T(1024)} %param.18) | copy-start | bytes 9220
  300.7 288.6 %all-reduce.10.cloned.1.call-start = ((), (), s32[]{:S(2)}) async-start(), calls=%async_computation.6 | async-start | bytes 28311552 | tf_op jit(solution)/shard_map/psum | solution.py:207
  301.0 7.9 %copy-start.5 = (f32[1024,768]{0,1:T(8,128)S(1)}, f32[1024,768]{0,1:T(8,128)}, u32[]{:S(2)}) copy-start(f32[1024,768]{0,1:T(8,128)} %copy-done.3) | copy-start | bytes 9437188
  301.0 7.9 %copy-start.41 = (bf16[1024,1536]{1,0:T(8,128)(2,1)S(1)}, bf16[1024,1536]{1,0:T(8,128)(2,1)}, u32[]{:S(2)}) copy-start(bf16[1024,1536]{1,0:T(8,128)(2,1)} %copy-done.40) | copy-start | bytes 9437188
  308.9 4.5 copy-start.36
  317.3 5.2 copy-start.12
  326.3 0.7 copy-start.25
  326.3 0.8 copy-start.33
  326.9 3.0 copy-start.26
  327.0 3.0 copy-start.27
  327.0 3.0 copy-start.28
  327.0 3.0 copy-start.29
  327.0 3.0 copy-start.30
  589.3 5.2 slice-start.5
  589.3 4.2 copy-start.17
  589.3 5.2 slice-start.6
  593.5 4.1 slice-start.3
  594.5 3.4 slice-start.4
  594.5 5.6 copy-start.1
Sparse Core Ops, SparseCore 0:
  10.1 29.8 all-gather.2
  71.7 27.1 all-gather.4
  128.1 51.5 all-reduce.5
  200.5 51.5 all-reduce.7
  300.8 26.1 reduce-scatter.1
  332.5 256.7 all-reduce.9
where the time goes:
time: 617 us; the launch traced here: 607 us
  waiting for transfers between devices  339 us (55%)
  matrix products  98.2 us (16%)
  blocking collectives  64.1 us (10%)
  local copies, waits for them, and re-layouts  62.7 us (10%)
  other arithmetic  26.3 us (4%)
  between operations  15.8 us (3%)
    psum x1, waiting for transfers between devices, body(): lax.psum((grad_w_qkv, grad_w_out, grad_gain_one, grad_shift_one, grad_w_u...  192 us
    psum x1, blocking collectives, body(): lax.psum((grad_w_qkv, grad_w_out, grad_gain_one, grad_shift_one, grad_w_u...  64.1 us
    psum x1, waiting for transfers between devices, body(): lax.psum(back_part.astype(jnp.bfloat16), 'head').astype(jnp.float32)  51.4 us
    psum x1, waiting for transfers between devices, body(): lax.psum(partial_out.astype(jnp.bfloat16), 'head').astype(jnp.float32)  42.8 us
    unnamed x112, local copies, waits for them, and re-layouts  35.9 us
    all_gather x1, waiting for transfers between devices, body(): lax.all_gather(context_rows, 'head', axis=1, tiled=True)  27.1 us
    all_gather x1, waiting for transfers between devices, body(): full_tokens = lax.all_gather(tokens, 'head', axis=1, tiled=True)  25.6 us
    dot_general x1, matrix products, body(): jnp.dot(normed_low, w_up, preferred_element_type=jnp.float32) + b_up  19 us
  transfers between devices with their start and end apart: 6, of which 5 were waited for; matrix products, arithmetic and copies ran while one was open for 7% of the time, Pallas kernels for 0%

commit v1 on v0

v1 whole, which is shorter than its diff:
```python
import jax
import jax.numpy as jnp
from jax import lax
from jax.sharding import PartitionSpec as P

HEAD_DIM = 64
norm_eps = 1e-06
root_half = 0.7071067811865476
inv_root_two_pi = 0.3989422804014327
LOW = jnp.bfloat16
WIDE = jnp.float32


def dot(a, b, dims=((1,), (0,))):
    return lax.dot_general(a, b, (dims, ((), ())), preferred_element_type=WIDE)


def normalize(values):
    centered = values - jnp.mean(values, axis=-1, keepdims=True)
    inverse = lax.rsqrt(jnp.mean(centered * centered, axis=-1, keepdims=True) + norm_eps)
    return centered * inverse, inverse


def norm_backward(upstream, normal, inverse, gain_vec):
    scaled = upstream * gain_vec
    grad = inverse * (
        scaled
        - jnp.mean(scaled, axis=-1, keepdims=True)
        - normal * jnp.mean(scaled * normal, axis=-1, keepdims=True)
    )
    return grad, jnp.sum(upstream * normal, axis=0), jnp.sum(upstream, axis=0)


def swap(x, axis, bit):
    n = lax.axis_size(axis)
    return lax.ppermute(x, axis, [(i, i ^ bit) for i in range(n)])


def gather_features(x, head_pos):
    other = swap(x, "head", 1)
    first = head_pos == 0
    return jnp.concatenate((jnp.where(first, x, other), jnp.where(first, other, x)), axis=1)


def sum_batch(grad):
    n = lax.axis_size("batch")
    pos = lax.axis_index("batch")
    shape = grad.shape
    x = grad.reshape(n, shape[0] // n, shape[1])
    bits = [1 << k for k in range(n.bit_length() - 1)]
    for bit in bits:
        half = x.shape[0] // 2
        mine = lax.rem(lax.div(pos, bit), 2)
        keep = lax.dynamic_slice_in_dim(x, mine * half, half, 0)
        send = lax.dynamic_slice_in_dim(x, (1 - mine) * half, half, 0)
        x = keep + swap(send.astype(LOW), "batch", bit).astype(WIDE)
    x = x.astype(LOW)
    for bit in reversed(bits):
        mine = lax.rem(lax.div(pos, bit), 2) == 0
        other = swap(x, "batch", bit)
        x = jnp.concatenate((jnp.where(mine, x, other), jnp.where(mine, other, x)), axis=0)
    return x.reshape(shape).astype(WIDE)


def body(tokens, w_qkv, w_out, gain_one, attention_norm_bias, w_up, b_up, w_down, gain_two,
         shift_two, block_perm, mask_index, mask_count, cotangent):
    width = w_out.shape[0]
    local = w_qkv.shape[2]
    groups = local // HEAD_DIM
    rows = tokens.shape[0]
    blocks = block_perm.shape[1]
    block_len = rows // blocks
    scale = HEAD_DIM ** (-0.5)
    head_pos = lax.axis_index("head")
    slots = mask_index.shape[1]
    full = gather_features(tokens, head_pos)
    flat = w_qkv.reshape(width, 3 * local)
    qkv = dot(full, flat).astype(LOW)
    query, key, value = (qkv[:, i * local:(i + 1) * local] for i in range(3))

    places = jnp.arange(rows, dtype=jnp.int32)
    index = mask_index[0][:, None]
    live = jnp.arange(slots, dtype=jnp.int32)[:, None] < mask_count[0]
    pick = ((index == places[None, :]) & live).astype(LOW)

    def split(x):
        return x.reshape(x.shape[0], groups, HEAD_DIM).transpose(1, 0, 2)

    tokens_c = dot(pick, full).astype(LOW)
    query_c = split(dot(pick, query).astype(LOW))
    key_h, value_h, query_h = split(key), split(value), split(query)
    place_block = places // block_len
    wanted = jnp.where(index // block_len == 0, block_perm[:, 0][:, None, None], block_perm[:, 1][:, None, None])
    allowed = wanted == place_block[None, None, :]
    scores = jnp.einsum("gqd,gkd->gqk", query_c, key_h, preferred_element_type=WIDE) * scale
    scores = jnp.where(allowed, scores, -1e30)
    peak = jnp.max(scores, -1, keepdims=True)
    expd = jnp.exp(scores - peak)
    probs = expd / jnp.sum(expd, -1, keepdims=True)
    probs_low = probs.astype(LOW)
    ctx_c = jnp.einsum("gqk,gkd->gqd", probs_low, value_h, preferred_element_type=WIDE).astype(LOW)
    ctx_c = ctx_c.transpose(1, 0, 2).reshape(slots, local)
    ctx_all = gather_features(ctx_c, head_pos)
    pre_one = tokens_c.astype(WIDE) + dot(ctx_all, w_out)
    normal_one, inverse_one = normalize(pre_one)
    normed_one = normal_one * gain_one + attention_norm_bias
    low_one = normed_one.astype(LOW)
    hidden_in = dot(low_one, w_up) + b_up
    cdf = 0.5 * (1.0 + lax.erf(hidden_in * root_half))
    hidden = (hidden_in * cdf).astype(LOW)
    slope = cdf + hidden_in * inv_root_two_pi * jnp.exp(-0.5 * hidden_in * hidden_in)
    part = dot(hidden, w_down).astype(LOW)
    branch = part.astype(WIDE) + swap(part, "head", 1).astype(WIDE)
    normal_two, inverse_two = normalize(normed_one + branch)
    upstream = jnp.where(live, cotangent[0].astype(WIDE), 0.0)
    grad_two, g_gain_two, g_shift_two = norm_backward(upstream, normal_two, inverse_two, gain_two)
    grad_branch = grad_two.astype(LOW)
    g_down = dot(hidden, grad_branch, ((0,), (0,)))
    grad_in = (dot(grad_branch, w_down, ((1,), (1,))) * slope).astype(LOW)
    g_bias = jnp.sum(grad_in.astype(WIDE), axis=0)
    g_up = dot(low_one, grad_in, ((0,), (0,)))
    back = dot(grad_in, w_up, ((1,), (1,))).astype(LOW)
    grad_normed = grad_two + (back.astype(WIDE) + swap(back, "head", 1).astype(WIDE))
    grad_one, g_gain_one, g_shift_one = norm_backward(grad_normed, normal_one, inverse_one, gain_one)
    grad_attn = grad_one.astype(LOW)
    g_out = dot(ctx_c, grad_attn, ((0,), (0,)))
    own_rows = lax.dynamic_slice_in_dim(w_out, head_pos * local, local, 0)
    grad_ctx = split(dot(grad_attn, own_rows, ((1,), (1,))).astype(LOW))
    dprobs = jnp.einsum("gqd,gkd->gqk", grad_ctx, value_h, preferred_element_type=WIDE)
    inner = jnp.sum(dprobs * probs, -1, keepdims=True)
    dscores = (probs * (dprobs - inner)).astype(LOW)
    d_query = jnp.einsum("gqk,gkd->gqd", dscores, key_h, preferred_element_type=WIDE) * scale
    d_key = jnp.einsum("gqk,gqd->gkd", dscores, query_c, preferred_element_type=WIDE) * scale
    d_value = jnp.einsum("gqk,gqd->gkd", probs_low, grad_ctx, preferred_element_type=WIDE)

    def join(x):
        return x.astype(LOW).transpose(1, 0, 2).reshape(x.shape[1], local)

    d_query, d_key, d_value = join(d_query), join(d_key), join(d_value)
    d_kv = jnp.concatenate((d_key, d_value), axis=1)
    g_q = dot(tokens_c, d_query, ((0,), (0,)))
    g_kv = dot(full, d_kv, ((0,), (0,)))
    g_qkv = jnp.concatenate((g_q, g_kv), axis=1)
    dense_q = dot(pick, d_query, ((0,), (0,))).astype(LOW)
    d_all = jnp.concatenate((dense_q, d_kv), axis=1)
    own = width // 2
    flat_own = lax.dynamic_slice_in_dim(flat, head_pos * own, own, 0)
    flat_far = lax.dynamic_slice_in_dim(flat, (1 - head_pos) * own, own, 0)
    far = dot(d_all, flat_far, ((1,), (1,))).astype(LOW)
    near = dot(d_all, flat_own, ((1,), (1,)))
    got = swap(far, "head", 1)
    mine = lax.dynamic_slice_in_dim(grad_one, head_pos * own, own, 1)
    high = mine.astype(LOW)
    rest = (mine - high.astype(WIDE)).astype(LOW)
    spread = dot(pick, high, ((0,), (0,))) + dot(pick, rest, ((0,), (0,)))
    grad_tokens = (near + got.astype(WIDE) + spread).astype(LOW)

    def choose(x):
        x = x.reshape(groups, blocks, block_len, HEAD_DIM)
        picked = x
        for source in range(blocks):
            picked = jnp.where((block_perm == source)[:, :, None, None], x[:, source:source + 1], picked)
        return picked

    q4 = query_h.reshape(groups, blocks, block_len, HEAD_DIM)
    k4, v4 = choose(key_h), choose(value_h)
    sc = jnp.einsum("gbqd,gbkd->gbqk", q4, k4, preferred_element_type=WIDE) * scale
    top = jnp.max(sc, -1, keepdims=True)
    ex = jnp.exp(sc - top)
    pr = (ex / jnp.sum(ex, -1, keepdims=True)).astype(LOW)
    ctx = jnp.einsum("gbqk,gbkd->gbqd", pr, v4, preferred_element_type=WIDE).astype(LOW)
    ctx = ctx.transpose(1, 2, 0, 3).reshape(rows, local)
    pre = full.astype(WIDE) + dot(gather_features(ctx, head_pos), w_out)
    normed = normalize(pre)[0] * gain_one + attention_norm_bias
    hid_in = dot(normed.astype(LOW), w_up) + b_up
    hid = (hid_in * (0.5 * (1.0 + lax.erf(hid_in * root_half)))).astype(LOW)
    down_own = lax.dynamic_slice_in_dim(w_down, head_pos * own, own, 1)
    down_far = lax.dynamic_slice_in_dim(w_down, (1 - head_pos) * own, own, 1)
    sent = swap(dot(hid, down_far).astype(LOW), "head", 1)
    cols = lax.dynamic_slice_in_dim(normed, head_pos * own, own, 1)
    pre_two = cols + (dot(hid, down_own) + sent.astype(WIDE))
    mean_own = jnp.mean(pre_two, -1, keepdims=True)
    dev = pre_two - mean_own
    stats = jnp.concatenate((mean_own, jnp.mean(dev * dev, -1, keepdims=True)), axis=1)
    far_stats = swap(stats, "head", 1)
    mean_far, var_far = far_stats[:, :1], far_stats[:, 1:]
    mean_all = 0.5 * (mean_own + mean_far)
    gap = 0.5 * (mean_own - mean_far)
    var_all = 0.5 * (stats[:, 1:] + var_far) + gap * gap
    gain_own = lax.dynamic_slice_in_dim(gain_two, head_pos * own, own, 0)
    shift_own = lax.dynamic_slice_in_dim(shift_two, head_pos * own, own, 0)
    result = ((pre_two - mean_all) * lax.rsqrt(var_all + norm_eps) * gain_own + shift_own).astype(LOW)

    g_qkv, g_out, g_up, g_down = (sum_batch(g) for g in (g_qkv, g_out, g_up, g_down))
    small = jnp.concatenate((g_gain_one, g_shift_one, g_gain_two, g_shift_two, g_bias))
    for k in range(lax.axis_size("batch").bit_length() - 1):
        small = small + swap(small, "batch", 1 << k)
    return (result, grad_tokens, g_qkv.reshape(width, 3, local), g_out, small[:width],
            small[width:2 * width], g_up, small[4 * width:], g_down, small[2 * width:3 * width],
            small[3 * width:4 * width])


def solution(mesh):
    return jax.shard_map(
        body,
        mesh=mesh,
        in_specs=(P("batch", "head"), P(None, None, "head"), P(), P(), P(), P(None, "head"), P("head"),
                  P("head", None), P(), P(), P("head", None), P("batch", None), P("batch"),
                  P("batch", None, None)),
        out_specs=(P("batch", "head"), P("batch", "head"), P(None, None, "head"), P("head", None), P(), P(),
                   P(None, "head"), P("head"), P("head", None), P(), P()),
        check_vma=False,
    )
```

time: 617 us -> 321 us (0.52)
  waiting for transfers between devices: 339 us -> 110 us
  blocking collectives: 64.1 us -> 0 us
  starting transfers between devices: 1.14 us -> 48.9 us
  matrix products: 98.2 us -> 74 us
  local copies, waits for them, and re-layouts: 62.7 us -> 45.7 us
  between operations: 15.8 us -> 3.21 us
  other arithmetic: 26.3 us -> 33.8 us
    psum x3 -> x0, waiting for transfers between devices: 286 us -> none  [the longest x1 192 us: body(): lax.psum((grad_w_qkv, grad_w_out, grad_gain_one, grad_shift_one, grad_w_u...]
    ppermute x0 -> x44, waiting for transfers between devices: none -> 110 us  [swap(): return lax.ppermute(x, axis, [(i, i ^ bit) for i in range(n)])]
    psum x1 -> x0, blocking collectives: 64.1 us -> none  [body(): lax.psum((grad_w_qkv, grad_w_out, grad_gain_one, grad_shift_one, grad_w_u...]
    all_gather x2 -> x0, waiting for transfers between devices: 52.7 us -> none  [the longest x1 27.1 us: body(): lax.all_gather(context_rows, 'head', axis=1, tiled=True)]
    ppermute x0 -> x44, starting transfers between devices: none -> 48.9 us  [swap(): return lax.ppermute(x, axis, [(i, i ^ bit) for i in range(n)])]
    dot_general x19 -> x29, matrix products: 98.2 us -> 57.8 us  [the longest x23 38.3 us: dot(): return lax.dot_general(a, b, (dims, ((), ())), preferred_element_type=WIDE)]
    unnamed x112 -> x105, local copies, waits for them, and re-layouts: 35.9 us -> 14.4 us
    sub x0 -> x2, matrix products: none -> 16.2 us  [the longest x1 10.9 us: body(): ex = jnp.exp(sc - top)]
  transfers between devices with their start and end apart: 6 -> 44, of which waited for: 5 -> 21; matrix products, arithmetic and copies ran while one was open for 7% -> 37% of each run, Pallas kernels for 0% -> 0%
where the time goes in v1:
time: 321 us; the launch traced here: 315 us
  waiting for transfers between devices  110 us (34%)
  matrix products  74 us (23%)
  starting transfers between devices  48.9 us (15%)
  local copies, waits for them, and re-layouts  45.7 us (14%)
  other arithmetic  33.8 us (11%)
  between operations  3.21 us (1%)
    ppermute x44, waiting for transfers between devices, swap(): return lax.ppermute(x, axis, [(i, i ^ bit) for i in range(n)])  110 us
    ppermute x44, starting transfers between devices, swap(): return lax.ppermute(x, axis, [(i, i ^ bit) for i in range(n)])  48.9 us
    dot_general x23, matrix products, dot(): return lax.dot_general(a, b, (dims, ((), ())), preferred_element_type=WIDE)  38.3 us
    unnamed x105, local copies, waits for them, and re-layouts  14.4 us
    sub x1, matrix products, body(): ex = jnp.exp(sc - top)  10.9 us
    convert_element_type x4, other arithmetic, sum_batch(): return x.reshape(shape).astype(WIDE)  8.83 us
    add x12, other arithmetic, sum_batch(): x = keep + swap(send.astype(LOW), 'batch', bit).astype(WIDE)  6.53 us
  transfers between devices with their start and end apart: 44, of which 21 were waited for; matrix products, arithmetic and copies ran while one was open for 37% of the time, Pallas kernels for 0%

profile of v1, /device:TPU:0, one launch (start us, length us, event | category | flops | bytes accessed | tf_op | source)
XLA Modules:
  0.0 315.2 jit_solution(1979262620367448779)
XLA Ops:
  0.7 1.6 copy.40
  2.3 3.0 collective-permute-start
  6.7 3.8 %copy.42 = bf16[768,3,384]{0,2,1:T(8,128)(2,1)} copy(bf16[768,3,384]{2,0,1:T(8,128)(2,1)} %param.15) | data formatting | bytes 3538944 | tf_op args[1]
  14.5 8.4 %collective-permute-done = bf16[1024,384]{0,1:T(8,128)(2,1)} collective-permute-done((bf16[1024,384]{0,1:T(8,128)(2,1)S(1)}, bf16[1024,384]{0,1:T(8,128)(2,1)}, u32[]{:S(2)}, u32[]{:S(2)}) %collective-permute-start) | collective-permute-done | bytes 786464 | tf_op jit(solution)/shard_map/ppermute | solution.py:36
  24.2 2.3 convolution_convert_fusion
  32.9 2.3 copy.51
  37.3 1.6 convolution_convert_fusion.8
  39.1 5.3 %fusion.156 = (f32[6,256]{1,0:T(8,128)S(1)}, f32[6,256,1024]{2,1,0:T(8,128)}) fusion(s32[1024]{0:T(1024)} %add_select_fusion, s32[6,256]{1,0:T(8,128)} %broadcast_select_fusion.38, bf16[6,256,64]{1,2,0:T(8,128)(2,1)S(1)} %bitcast.188, bf16[6,1024,64]{1,2,0:T(8,128)(2,1)S(1)} %bitcast.169), kind=kOutput, calls=%fused_computation.302 | convolution fusion | flops 209191936 | bytes 7290880 | tf_op jit(solution)/shard_map/sub | solution.py:98
  44.4 4.1 %fusion.44 = bf16[6,256,64]{1,2,0:T(8,128)(2,1)S(1)} fusion(bf16[6,1024,64]{1,2,0:T(8,128)(2,1)} %bitcast.175, f32[6,256,1024]{2,1,0:T(8,128)} %get-tuple-element.106, f32[6,256]{1,0:T(8,128)S(1)} %get-tuple-element.105), kind=kOutput, calls=%fused_computation.90 | convolution fusion | flops 204570624 | bytes 7280640 | tf_op jit(solution)/shard_map/gqk,gkd->gqd/dot_general | solution.py:101
  48.5 1.8 collective-permute-start.4
  50.3 10.9 %fusion.149 = (f32[6,2,512]{2,1,0:T(2,128)}, f32[6,2,512,512]{2,3,1,0:T(8,128)}) fusion(bf16[6,8,2,8,512]{4,3,2,1,0:T(8,128)(2,1)} %bitcast.190, pred[6,2]{1,0:T(8,128)(4,1)} %copy.47, pred[6,2]{1,0:T(8,128)(4,1)} %copy.44, bf16[6,512,64]{1,2,0:T(8,128)(2,1)} %get-tuple-element.66, bf16[6,512,64]{1,2,0:T(8,128)(2,1)} %get-tuple-element.65, ...), kind=kOutput, calls=%fused_computation.299 | convolution fusion | flops 412877312 | bytes 14966808 | tf_op jit(solution)/shard_map/sub | solution.py:169
  61.2 2.1 convolution_convert_fusion.4
  68.2 6.1 %fusion.37 = bf16[2,512,6,64]{1,3,0,2:T(8,128)(2,1)S(1)} fusion(f32[6,2,512,512]{2,3,1,0:T(8,128)} %get-tuple-element.100, f32[6,2,512]{2,1,0:T(2,128)S(1)} %copy-done.45, pred[6,2]{1,0:T(8,128)(4,1)S(1)} %copy-done.42, pred[6,2]{1,0:T(8,128)(4,1)S(1)} %copy-done.43, bf16[6,512,64]{1,2,0:T(8,128)(2,1)S(1)} %copy-done.23, ...), kind=kOutput, calls=%fused_computation.71 | convolution fusion | flops 410124288 | bytes 14966808 | tf_op jit(solution)/shard_map/gbqk,gbkd->gbqd/dot_general | solution.py:171
  75.3 1.8 collective-permute-start.1
  77.1 1.5 collective-permute-done.5
  79.7 2.7 convert_reduce_fusion
  89.5 6.2 %collective-permute-done.1 = bf16[1024,384]{0,1:T(8,128)(2,1)S(1)} collective-permute-done((bf16[1024,384]{0,1:T(8,128)(2,1)S(1)}, bf16[1024,384]{0,1:T(8,128)(2,1)S(1)}, u32[]{:S(2)}, u32[]{:S(2)}) %collective-permute-start.1) | collective-permute-done | bytes 786464 | tf_op jit(solution)/shard_map/ppermute | solution.py:36
  95.9 1.5 fusion.154
  98.4 3.8 %multiply_convert_fusion.1 = bf16[1024,1536]{1,0:T(8,128)(2,1)S(1)} fusion(bf16[768,1536]{1,0:T(8,128)(2,1)S(1)} %copy-done, f32[1536]{0:T(1024)S(1)} %copy-done.41, f32[1024,768]{0,1:T(8,128)S(1)} %multiply_add_fusion), kind=kOutput, calls=%fused_computation.10 | convolution fusion | flops 2426142720 | bytes 8656896 | tf_op jit(solution)/shard_map/dot_general | solution.py:15
  102.2 2.4 convolution_convert_fusion.3
  104.6 1.7 collective-permute-start.2
  108.0 3.8 %fusion.33 = bf16[6,1024,64]{1,2,0:T(8,128)(2,1)S(1)} fusion(bf16[6,256,64]{1,2,0:T(8,128)(2,1)S(1)} %bitcast.196, f32[6,256,1024]{2,1,0:T(8,128)} %get-tuple-element.106, f32[6,256]{1,0:T(8,128)S(1)} %copy-done.30), kind=kOutput, calls=%fused_computation.66 | convolution fusion | flops 204865536 | bytes 7280640 | tf_op jit(solution)/shard_map/gqk,gqd->gkd/dot_general | solution.py:134
  111.8 3.7 %multiply_reduce_fusion.1 = (f32[6,256]{1,0:T(8,128)S(1)}, f32[6,256,1024]{2,1,0:T(8,128)S(1)}) fusion(f32[6,256,1024]{2,1,0:T(8,128)} %get-tuple-element.106, f32[6,256]{1,0:T(8,128)S(1)} %copy-done.30, bf16[6,256,64]{1,2,0:T(8,128)(2,1)S(1)} %bitcast.197, bf16[6,1024,64]{1,2,0:T(8,128)(2,1)S(1)} %bitcast.177), kind=kOutput, calls=%fused_computation.7 | convolution fusion | flops 206043648 | bytes 13578240 | tf_op jit(solution)/shard_map/gqd,gkd->gqk/dot_general | solution.py:129
  121.6 2.0 pad_maximum_fusion
  124.2 2.5 convolution_convert_fusion.1
  126.6 1.6 collective-permute-start.25
  128.9 2.6 fusion.54
  131.5 1.7 collective-permute-start.26
  134.0 1.6 collective-permute-start.18
  135.6 1.8 fusion.49
  137.4 5.4 %copy.60 = f32[768,1152]{1,0:T(8,128)} copy(f32[768,1152]{0,1:T(8,128)} %pad_maximum_fusion) | data formatting | bytes 7077888 | tf_op jit(solution)/shard_map/concatenate | solution.py:143
  142.8 2.7 collective-permute-start.27
  145.9 2.5 dynamic-slice_convert_fusion.2
  149.0 1.8 collective-permute-done.19
  152.9 2.9 collective-permute-done.20
  155.8 4.1 %fusion.155 = (f32[1024]{0:T(1024)S(1)}, f32[1024,384]{0,1:T(8,128)S(1)}) fusion(bf16[1024,384]{0,1:T(8,128)(2,1)} %collective-permute-done.2, bf16[1024,1536]{1,0:T(8,128)(2,1)} %copy-done.44, bf16[1536,768]{1,0:T(8,128)(2,1)S(1)} %copy-done.40, s32[]{:T(128)S(6)} %select_n.341, f32[1024,768]{0,1:T(8,128)} %copy-done.7), kind=kOutput, calls=%fused_computation.301 | convolution fusion | flops 1209531392 | bytes 8262656 | tf_op jit(solution)/shard_map/dot_general | solution.py:15
  160.7 5.6 %collective-permute-done.3 = f32[1024,2]{0,1:T(2,128)S(1)} collective-permute-done((f32[1024,2]{0,1:T(2,128)S(1)}, f32[1024,2]{0,1:T(2,128)S(1)}, u32[]{:S(2)}, u32[]{:S(2)}) %collective-permute-start.3) | collective-permute-done | bytes 8224 | tf_op jit(solution)/shard_map/ppermute | solution.py:36
  168.3 2.4 collective-permute-done.21
  171.8 2.3 convert_add_fusion.2
  175.4 2.3 convert_add_fusion.1
  178.7 2.7 add_convert_fusion
  185.4 23.9 %collective-permute-done.9 = bf16[4,48,1152]{2,1,0:T(8,128)(2,1)S(1)} collective-permute-done((bf16[4,48,1152]{2,1,0:T(8,128)(2,1)S(1)}, bf16[4,48,1152]{2,1,0:T(8,128)(2,1)S(1)}, u32[]{:S(2)}, u32[]{:S(2)}) %collective-permute-start.9) | collective-permute-done | bytes 442400 | tf_op jit(solution)/shard_map/ppermute | solution.py:36
  211.9 7.1 %collective-permute-done.10 = bf16[2,48,1152]{2,1,0:T(8,128)(2,1)S(1)} collective-permute-done((bf16[2,48,1152]{2,1,0:T(8,128)(2,1)S(1)}, bf16[2,48,1152]{2,1,0:T(8,128)(2,1)S(1)}, u32[]{:S(2)}, u32[]{:S(2)}) %collective-permute-start.10) | collective-permute-done | bytes 221216 | tf_op jit(solution)/shard_map/ppermute | solution.py:36
  219.1 1.5 collective-permute-start.11
  220.6 1.9 collective-permute-start.38
  222.5 3.5 %collective-permute-done.11 = bf16[1,48,1152]{2,1,0:T(8,128)(2,1)S(1)} collective-permute-done((bf16[1,48,1152]{2,1,0:T(8,128)(2,1)S(1)}, bf16[1,48,1152]{2,1,0:T(8,128)(2,1)S(1)}, u32[]{:S(2)}, u32[]{:S(2)}) %collective-permute-start.11) | collective-permute-done | bytes 110624 | tf_op jit(solution)/shard_map/ppermute | solution.py:36
  226.0 2.2 collective-permute-start.12
  229.2 5.3 %collective-permute-done.38 = bf16[2,96,768]{2,1,0:T(8,128)(2,1)S(1)} collective-permute-done((bf16[2,96,768]{2,1,0:T(8,128)(2,1)S(1)}, bf16[2,96,768]{2,1,0:T(8,128)(2,1)S(1)}, u32[]{:S(2)}, u32[]{:S(2)}) %collective-permute-start.38) | collective-permute-done | bytes 294944 | tf_op jit(solution)/shard_map/ppermute | solution.py:36
  235.6 7.5 %collective-permute-start.13 = (bf16[2,48,1152]{2,1,0:T(8,128)(2,1)S(1)}, bf16[2,48,1152]{2,1,0:T(8,128)(2,1)S(1)}, u32[]{:S(2)}, u32[]{:S(2)}) collective-permute-start(bf16[2,48,1152]{2,1,0:T(8,128)(2,1)S(1)} %pad_maximum_fusion.17), channel_id=1, source_target_pairs={{0,8},{2,10},{4,12},{6,14},{8,0},{10,2},{12,4},{14,6},{16,24},{18,... | collective-permute-start | bytes 663560 | tf_op jit(solution)/shard_map/ppermute | solution.py:36
  243.1 2.7 collective-permute-done.31
  246.7 2.2 collective-permute-done.39
  249.1 3.7 %collective-permute-done.32 = bf16[1,48,1536]{2,1,0:T(8,128)(2,1)S(1)} collective-permute-done((bf16[1,48,1536]{2,1,0:T(8,128)(2,1)S(1)}, bf16[1,48,1536]{2,1,0:T(8,128)(2,1)S(1)}, u32[]{:S(2)}, u32[]{:S(2)}) %collective-permute-start.32) | collective-permute-done | bytes 147488 | tf_op jit(solution)/shard_map/ppermute | solution.py:36
  252.8 2.2 collective-permute-start.33
  255.0 1.7 collective-permute-done.40
  259.1 3.8 %collective-permute-done.33 = bf16[2,48,1536]{2,1,0:T(8,128)(2,1)S(1)} collective-permute-done((bf16[2,48,1536]{2,1,0:T(8,128)(2,1)S(1)}, bf16[2,48,1536]{2,1,0:T(8,128)(2,1)S(1)}, u32[]{:S(2)}, u32[]{:S(2)}) %collective-permute-start.33) | collective-permute-done | bytes 294944 | tf_op jit(solution)/shard_map/ppermute | solution.py:36
  263.8 3.6 %collective-permute-done.41 = bf16[2,96,768]{2,1,0:T(8,128)(2,1)S(1)} collective-permute-done((bf16[2,96,768]{2,1,0:T(8,128)(2,1)S(1)}, bf16[2,96,768]{2,1,0:T(8,128)(2,1)S(1)}, u32[]{:S(2)}, u32[]{:S(2)}) %collective-permute-start.41) | collective-permute-done | bytes 294944 | tf_op jit(solution)/shard_map/ppermute | solution.py:36
  267.9 3.3 %collective-permute-done.14 = bf16[4,48,1152]{2,1,0:T(8,128)(2,1)S(1)} collective-permute-done((bf16[4,48,1152]{2,1,0:T(8,128)(2,1)S(1)}, bf16[4,48,1152]{2,1,0:T(8,128)(2,1)S(1)}, u32[]{:S(2)}, u32[]{:S(2)}) %collective-permute-start.14) | collective-permute-done | bytes 442400 | tf_op jit(solution)/shard_map/ppermute | solution.py:36
  271.5 12.3 %collective-permute-done.34 = bf16[4,48,1536]{2,1,0:T(8,128)(2,1)S(1)} collective-permute-done((bf16[4,48,1536]{2,1,0:T(8,128)(2,1)S(1)}, bf16[4,48,1536]{2,1,0:T(8,128)(2,1)S(1)}, u32[]{:S(2)}, u32[]{:S(2)}) %collective-permute-start.34) | collective-permute-done | bytes 589856 | tf_op jit(solution)/shard_map/ppermute | solution.py:36
  285.0 6.9 %collective-permute-done.42 = bf16[4,96,768]{2,1,0:T(8,128)(2,1)S(1)} collective-permute-done((bf16[4,96,768]{2,1,0:T(8,128)(2,1)S(1)}, bf16[4,96,768]{2,1,0:T(8,128)(2,1)S(1)}, u32[]{:S(2)}, u32[]{:S(2)}) %collective-permute-start.42) | collective-permute-done | bytes 589856 | tf_op jit(solution)/shard_map/ppermute | solution.py:36
  293.3 2.0 maximum_convert_fusion
  295.4 6.1 %reshape.303 = f32[768,3,384]{2,1,0:T(4,128)} reshape(f32[16,48,1152]{2,1,0:T(8,128)} %maximum_convert_fusion) | data formatting | bytes 7077888 | tf_op jit(solution)/shard_map/convert_element_type | solution.py:62
  301.5 4.4 %copy.62 = f32[768,3,384]{2,0,1:T(8,128)} copy(f32[768,3,384]{2,1,0:T(4,128)} %reshape.303) | data formatting | bytes 7077888
  307.5 3.0 bitcast_convert_fusion.1
  312.1 2.7 bitcast_convert_fusion
  (287 shorter events, 67.7 us)
Async XLA Ops:
  0.6 64.7 %copy-start = (bf16[768,1536]{1,0:T(8,128)(2,1)S(1)}, bf16[768,1536]{1,0:T(8,128)(2,1)}, u32[]{:S(2)}) copy-start(bf16[768,1536]{1,0:T(8,128)(2,1)} %param.19) | copy-start | bytes 7077892
  0.7 13.1 %copy-start.37 = (s32[6,2]{0,1:T(2,128)S(1)}, s32[6,2]{0,1:T(2,128)}, u32[]{:S(2)}) copy-start(s32[6,2]{0,1:T(2,128)} %param.24) | copy-start | bytes 148
  0.7 11.2 %copy-start.38 = (f32[768]{0:T(1024)S(1)}, f32[768]{0:T(1024)}, u32[]{:S(2)}) copy-start(f32[768]{0:T(1024)} %param.23) | copy-start | bytes 9220
  0.7 11.8 %copy-start.27 = (f32[768]{0:T(1024)S(1)}, f32[768]{0:T(1024)}, u32[]{:S(2)}) copy-start(f32[768]{0:T(1024)} %param.22) | copy-start | bytes 9220
  0.7 13.1 %copy-start.34 = (s32[1,256]{1,0:T(1,128)S(1)}, s32[1,256]{1,0:T(1,128)}, u32[]{:S(2)}) copy-start(s32[1,256]{1,0:T(1,128)} %param.25) | copy-start | bytes 3076
  2.3 20.7 %collective-permute-start = (bf16[1024,384]{0,1:T(8,128)(2,1)S(1)}, bf16[1024,384]{0,1:T(8,128)(2,1)}, u32[]{:S(2)}, u32[]{:S(2)}) collective-permute-start(bf16[1024,384]{0,1:T(8,128)(2,1)S(1)} %copy.40), channel_id=1, source_target_pairs={{0,1},{1,0},{2,3},{3,2},{4,5},{5,4},{6,7},{7,6},{8,9},{9,8},{10,11... | collective-permute-start | bytes 2359304 | tf_op jit(solution)/shard_map/ppermute | solution.py:36
  13.2 11.0 %copy-start.11 = (bf16[768,3,384]{0,2,1:T(8,128)(2,1)S(1)}, bf16[768,3,384]{0,2,1:T(8,128)(2,1)}, u32[]{:S(2)}) copy-start(bf16[768,3,384]{0,2,1:T(8,128)(2,1)} %copy.42) | copy-start | bytes 5308420
  44.4 4.1 %copy-start.29 = (f32[6,256]{1,0:T(8,128)}, f32[6,256]{1,0:T(8,128)S(1)}, u32[]{:S(2)}) copy-start(f32[6,256]{1,0:T(8,128)S(1)} %get-tuple-element.105) | copy-start | bytes 18436
  48.5 14.9 %collective-permute-start.4 = (bf16[256,384]{0,1:T(8,128)(2,1)S(1)}, bf16[256,384]{0,1:T(8,128)(2,1)}, u32[]{:S(2)}, u32[]{:S(2)}) collective-permute-start(bf16[256,384]{0,1:T(8,128)(2,1)S(1)} %bitcast.191), channel_id=1, source_target_pairs={{0,1},{1,0},{2,3},{3,2},{4,5},{5,4},{6,7},{7,6},{8,9},{9,8},{10,11... | collective-permute-start | bytes 589832 | tf_op jit(solution)/shard_map/ppermute | solution.py:36
  50.3 10.9 %copy-start.35 = (s32[1,256]{1,0:T(1,128)S(1)}, s32[1,256]{1,0:T(1,128)}, u32[]{:S(2)}) copy-start(s32[1,256]{1,0:T(1,128)} %param.25) | copy-start | bytes 3076
  67.8 10.7 %collective-permute-start.5 = (bf16[256,768]{1,0:T(8,128)(2,1)S(1)}, bf16[256,768]{1,0:T(8,128)(2,1)S(1)}, u32[]{:S(2)}, u32[]{:S(2)}) collective-permute-start(bf16[256,768]{1,0:T(8,128)(2,1)S(1)} %convolution_convert_fusion.6), channel_id=1, source_target_pairs={{0,1},{1,0},{2,3},{3,2},{4,5},{5,4},{6,7},{7,6},{8,9},{9,8},{10,11... | collective-permute-start | bytes 1179656 | tf_op jit(solution)/shard_map/ppermute | solution.py:36
  75.1 4.0 %copy-start.6 = (bf16[1,256,768]{2,1,0:T(8,128)(2,1)S(1)}, bf16[1,256,768]{2,1,0:T(8,128)(2,1)}, u32[]{:S(2)}) copy-start(bf16[1,256,768]{2,1,0:T(8,128)(2,1)} %param.27) | copy-start | bytes 1179652
  75.3 20.5 %collective-permute-start.1 = (bf16[1024,384]{0,1:T(8,128)(2,1)S(1)}, bf16[1024,384]{0,1:T(8,128)(2,1)S(1)}, u32[]{:S(2)}, u32[]{:S(2)}) collective-permute-start(bf16[1024,384]{0,1:T(8,128)(2,1)S(1)} %bitcast.181), channel_id=1, source_target_pairs={{0,1},{1,0},{2,3},{3,2},{4,5},{5,4},{6,7},{7,6},{8,9},{9,8},{10,11... | collective-permute-start | bytes 2359304 | tf_op jit(solution)/shard_map/ppermute | solution.py:36
  84.2 22.1 %collective-permute-start.6 = (bf16[256,768]{1,0:T(8,128)(2,1)S(1)}, bf16[256,768]{1,0:T(8,128)(2,1)S(1)}, u32[]{:S(2)}, u32[]{:S(2)}) collective-permute-start(bf16[256,768]{1,0:T(8,128)(2,1)S(1)} %convolution_convert_fusion.5), channel_id=1, source_target_pairs={{0,1},{1,0},{2,3},{3,2},{4,5},{5,4},{6,7},{7,6},{8,9},{9,8},{10,11... | collective-permute-start | bytes 1179656 | tf_op jit(solution)/shard_map/ppermute | solution.py:36
  86.7 85.0 %collective-permute-start.28 = (bf16[8,48,1536]{2,1,0:T(8,128)(2,1)}, bf16[8,48,1536]{2,1,0:T(8,128)(2,1)}, u32[]{:S(2)}, u32[]{:S(2)}) collective-permute-start(bf16[8,48,1536]{2,1,0:T(8,128)(2,1)} %dynamic-slice_convert_fusion.1), channel_id=1, source_target_pairs={{0,2},{2,0},{4,6},{6,4},{8,10},{10,8},{12,14},{14,12},{16,18},{18,... | collective-permute-start | bytes 3538952 | tf_op jit(solution)/shard_map/ppermute | solution.py:36
  87.8 8.1 %copy-start.2 = (f32[1536,768]{1,0:T(8,128)}, f32[1536,768]{1,0:T(8,128)S(1)}, u32[]{:S(2)}) copy-start(f32[1536,768]{1,0:T(8,128)S(1)} %fusion.116) | copy-start | bytes 14155780
  87.8 8.1 %copy-start.15 = (bf16[1024,384]{0,1:T(8,128)(2,1)S(1)}, bf16[1024,384]{0,1:T(8,128)(2,1)}, u32[]{:S(2)}) copy-start(bf16[1024,384]{0,1:T(8,128)(2,1)} %copy-done.14) | copy-start | bytes 2359300
  87.8 8.1 %copy-start.18 = (bf16[1024,384]{0,1:T(8,128)(2,1)S(1)}, bf16[1024,384]{0,1:T(8,128)(2,1)}, u32[]{:S(2)}) copy-start(bf16[1024,384]{0,1:T(8,128)(2,1)} %copy-done.17) | copy-start | bytes 2359300
  89.0 86.3 %collective-permute-start.36 = (bf16[8,96,768]{2,1,0:T(8,128)(2,1)}, bf16[8,96,768]{2,1,0:T(8,128)(2,1)}, u32[]{:S(2)}, u32[]{:S(2)}) collective-permute-start(bf16[8,96,768]{2,1,0:T(8,128)(2,1)} %dynamic-slice_convert_fusion), channel_id=1, source_target_pairs={{0,2},{2,0},{4,6},{6,4},{8,10},{10,8},{12,14},{14,12},{16,18},{18,... | collective-permute-start | bytes 3538952 | tf_op jit(solution)/shard_map/ppermute | solution.py:36
  104.6 51.2 %collective-permute-start.2 = (bf16[1024,384]{0,1:T(8,128)(2,1)}, bf16[1024,384]{0,1:T(8,128)(2,1)}, u32[]{:S(2)}, u32[]{:S(2)}) collective-permute-start(bf16[1024,384]{0,1:T(8,128)(2,1)} %convolution_convert_fusion.3), channel_id=1, source_target_pairs={{0,1},{1,0},{2,3},{3,2},{4,5},{5,4},{6,7},{7,6},{8,9},{9,8},{10,11... | collective-permute-start | bytes 2359304 | tf_op jit(solution)/shard_map/ppermute | solution.py:36
  108.0 3.8 %copy-start.9 = (bf16[1024,384]{0,1:T(8,128)(2,1)S(1)}, bf16[1024,384]{0,1:T(8,128)(2,1)}, u32[]{:S(2)}) copy-start(bf16[1024,384]{0,1:T(8,128)(2,1)} %copy.51) | copy-start | bytes 2359300
  108.0 7.6 %slice-start = ((s8[6291456]{0:T(1024)(128)(4,1)}), s8[4194304]{0:T(1024)(128)(4,1)S(1)}, s32[]{:S(2)}) async-start(s8[6291456]{0:T(1024)(128)(4,1)} %bitcast.172), calls=%async_computation | async-start | bytes 8388608
  119.4 8.8 %collective-permute-start.16 = (bf16[8,24,768]{2,1,0:T(8,128)(2,1)S(1)}, bf16[8,24,768]{2,1,0:T(8,128)(2,1)S(1)}, u32[]{:S(2)}, u32[]{:S(2)}) collective-permute-start(bf16[8,24,768]{2,1,0:T(8,128)(2,1)S(1)} %dynamic-slice_convert_fusion.8), channel_id=1, source_target_pairs={{0,2},{2,0},{4,6},{6,4},{8,10},{10,8},{12,14},{14,12},{16,18},{18,... | collective-permute-start | bytes 884744 | tf_op jit(solution)/shard_map/ppermute | solution.py:36
  119.6 7.1 %collective-permute-start.24 = (f32[4608]{0:T(1024)S(1)}, f32[4608]{0:T(1024)S(1)}, u32[]{:S(2)}, u32[]{:S(2)}) collective-permute-start(f32[4608]{0:T(1024)S(1)} %constant_dynamic-update-slice_fusion), channel_id=1, source_target_pairs={{0,2},{2,0},{4,6},{6,4},{8,10},{10,8},{12,14},{14,12},{16,18},{18,... | collective-permute-start | bytes 55304 | tf_op jit(solution)/shard_map/ppermute | solution.py:36
  126.6 4.9 %collective-permute-start.25 = (f32[4608]{0:T(1024)S(1)}, f32[4608]{0:T(1024)S(1)}, u32[]{:S(2)}, u32[]{:S(2)}) collective-permute-start(f32[4608]{0:T(1024)S(1)} %add.306), channel_id=1, source_target_pairs={{0,4},{2,6},{4,0},{6,2},{8,12},{10,14},{12,8},{14,10},{16,20},{18,... | collective-permute-start | bytes 55304 | tf_op jit(solution)/shard_map/ppermute | solution.py:36
  128.3 5.6 %collective-permute-start.17 = (bf16[4,24,768]{2,1,0:T(8,128)(2,1)S(1)}, bf16[4,24,768]{2,1,0:T(8,128)(2,1)S(1)}, u32[]{:S(2)}, u32[]{:S(2)}) collective-permute-start(bf16[4,24,768]{2,1,0:T(8,128)(2,1)S(1)} %dynamic-slice_convert_fusion.13), channel_id=1, source_target_pairs={{0,4},{2,6},{4,0},{6,2},{8,12},{10,14},{12,8},{14,10},{16,20},{18,... | collective-permute-start | bytes 442376 | tf_op jit(solution)/shard_map/ppermute | solution.py:36
  131.5 11.3 %collective-permute-start.26 = (f32[4608]{0:T(1024)S(1)}, f32[4608]{0:T(1024)S(1)}, u32[]{:S(2)}, u32[]{:S(2)}) collective-permute-start(f32[4608]{0:T(1024)S(1)} %add.307), channel_id=1, source_target_pairs={{0,8},{2,10},{4,12},{6,14},{8,0},{10,2},{12,4},{14,6},{16,24},{18,... | collective-permute-start | bytes 55304 | tf_op jit(solution)/shard_map/ppermute | solution.py:36
  134.0 11.6 %collective-permute-start.18 = (bf16[2,24,768]{2,1,0:T(8,128)(2,1)S(1)}, bf16[2,24,768]{2,1,0:T(8,128)(2,1)S(1)}, u32[]{:S(2)}, u32[]{:S(2)}) collective-permute-start(bf16[2,24,768]{2,1,0:T(8,128)(2,1)S(1)} %dynamic-slice_convert_fusion.15), channel_id=1, source_target_pairs={{0,8},{2,10},{4,12},{6,14},{8,0},{10,2},{12,4},{14,6},{16,24},{18,... | collective-permute-start | bytes 221192 | tf_op jit(solution)/shard_map/ppermute | solution.py:36
  142.8 13.0 %copy-start.40 = (bf16[1536,768]{1,0:T(8,128)(2,1)S(1)}, bf16[1536,768]{1,0:T(8,128)(2,1)}, u32[]{:S(2)}) copy-start(bf16[1536,768]{1,0:T(8,128)(2,1)} %param.21) | copy-start | bytes 7077892
  142.8 5.6 %collective-permute-start.27 = (f32[4608]{0:T(1024)S(1)}, f32[4608]{0:T(1024)S(1)}, u32[]{:S(2)}, u32[]{:S(2)}) collective-permute-start(f32[4608]{0:T(1024)S(1)} %add.308), channel_id=1, source_target_pairs={{0,16},{2,18},{4,20},{6,22},{8,24},{10,26},{12,28},{14,30},{16,0},... | collective-permute-start | bytes 55304 | tf_op jit(solution)/shard_map/ppermute | solution.py:36
  145.6 5.2 %collective-permute-start.19 = (bf16[1,24,768]{2,1,0:T(8,128)(2,1)S(1)}, bf16[1,24,768]{2,1,0:T(8,128)(2,1)S(1)}, u32[]{:S(2)}, u32[]{:S(2)}) collective-permute-start(bf16[1,24,768]{2,1,0:T(8,128)(2,1)S(1)} %dynamic-slice_convert_fusion.18), channel_id=1, source_target_pairs={{0,16},{2,18},{4,20},{6,22},{8,24},{10,26},{12,28},{14,30},{16,0},... | collective-permute-start | bytes 110600 | tf_op jit(solution)/shard_map/ppermute | solution.py:36
  148.4 30.3 %collective-permute-start.7 = (bf16[1024,384]{1,0:T(8,128)(2,1)}, bf16[1024,384]{1,0:T(8,128)(2,1)}, u32[]{:S(2)}, u32[]{:S(2)}) collective-permute-start(bf16[1024,384]{1,0:T(8,128)(2,1)} %convolution_convert_fusion.1), channel_id=1, source_target_pairs={{0,1},{1,0},{2,3},{3,2},{4,5},{5,4},{6,7},{7,6},{8,9},{9,8},{10,11... | collective-permute-start | bytes 2359304 | tf_op jit(solution)/shard_map/ppermute | solution.py:36
  150.8 5.0 %collective-permute-start.20 = (bf16[1,24,768]{2,1,0:T(8,128)(2,1)S(1)}, bf16[1,24,768]{2,1,0:T(8,128)(2,1)S(1)}, u32[]{:S(2)}, u32[]{:S(2)}) collective-permute-start(bf16[1,24,768]{2,1,0:T(8,128)(2,1)S(1)} %add_convert_fusion.5), channel_id=1, source_target_pairs={{0,16},{2,18},{4,20},{6,22},{8,24},{10,26},{12,28},{14,30},{16,0},... | collective-permute-start | bytes 110600 | tf_op jit(solution)/shard_map/ppermute | solution.py:36
  155.7 25.9 %collective-permute-start.8 = (bf16[8,48,1152]{2,1,0:T(8,128)(2,1)}, bf16[8,48,1152]{2,1,0:T(8,128)(2,1)}, u32[]{:S(2)}, u32[]{:S(2)}) collective-permute-start(bf16[8,48,1152]{2,1,0:T(8,128)(2,1)} %dynamic-slice_convert_fusion.2), channel_id=1, source_target_pairs={{0,2},{2,0},{4,6},{6,4},{8,10},{10,8},{12,14},{14,12},{16,18},{18,... | collective-permute-start | bytes 2654216 | tf_op jit(solution)/shard_map/ppermute | solution.py:36
  155.7 11.1 %copy-start.31 = (f32[384]{0:T(512)S(1)}, f32[384]{0:T(512)}, u32[]{:S(2)}) copy-start(f32[384]{0:T(512)} %dynamic_slice.127) | copy-start | bytes 4612
  155.8 11.1 %copy-start.32 = (f32[384]{0:T(512)S(1)}, f32[384]{0:T(512)}, u32[]{:S(2)}) copy-start(f32[384]{0:T(512)} %dynamic_slice.126) | copy-start | bytes 4612
  160.1 6.2 %collective-permute-start.3 = (f32[1024,2]{0,1:T(2,128)S(1)}, f32[1024,2]{0,1:T(2,128)S(1)}, u32[]{:S(2)}, u32[]{:S(2)}) collective-permute-start(f32[1024,2]{0,1:T(2,128)S(1)} %pad_maximum_fusion.20), channel_id=1, source_target_pairs={{0,1},{1,0},{2,3},{3,2},{4,5},{5,4},{6,7},{7,6},{8,9},{9,8},{10,11... | collective-permute-start | bytes 24584 | tf_op jit(solution)/shard_map/ppermute | solution.py:36
  166.3 4.4 %collective-permute-start.21 = (bf16[2,24,768]{2,1,0:T(8,128)(2,1)S(1)}, bf16[2,24,768]{2,1,0:T(8,128)(2,1)S(1)}, u32[]{:S(2)}, u32[]{:S(2)}) collective-permute-start(bf16[2,24,768]{2,1,0:T(8,128)(2,1)S(1)} %pad_maximum_fusion.19), channel_id=1, source_target_pairs={{0,8},{2,10},{4,12},{6,14},{8,0},{10,2},{12,4},{14,6},{16,24},{18,... | collective-permute-start | bytes 221192 | tf_op jit(solution)/shard_map/ppermute | solution.py:36
  170.7 10.7 %collective-permute-start.22 = (bf16[4,24,768]{2,1,0:T(8,128)(2,1)S(1)}, bf16[4,24,768]{2,1,0:T(8,128)(2,1)S(1)}, u32[]{:S(2)}, u32[]{:S(2)}) collective-permute-start(bf16[4,24,768]{2,1,0:T(8,128)(2,1)S(1)} %pad_maximum_fusion.18), channel_id=1, source_target_pairs={{0,4},{2,6},{4,0},{6,2},{8,12},{10,14},{12,8},{14,10},{16,20},{18,... | collective-permute-start | bytes 442376 | tf_op jit(solution)/shard_map/ppermute | solution.py:36
  174.2 4.5 %copy-start.5 = (f32[1024,384]{1,0:T(8,128)S(1)}, f32[1024,384]{1,0:T(8,128)}, u32[]{:S(2)}) copy-start(f32[1024,384]{1,0:T(8,128)} %fusion.49) | copy-start | bytes 4718596
  174.2 4.5 %copy-start.13 = (f32[1024,384]{1,0:T(8,128)S(1)}, f32[1024,384]{1,0:T(8,128)}, u32[]{:S(2)}) copy-start(f32[1024,384]{1,0:T(8,128)} %fusion.54) | copy-start | bytes 4718596
  174.2 35.9 %collective-permute-start.29 = (bf16[4,48,1536]{2,1,0:T(8,128)(2,1)S(1)}, bf16[4,48,1536]{2,1,0:T(8,128)(2,1)S(1)}, u32[]{:S(2)}, u32[]{:S(2)}) collective-permute-start(bf16[4,48,1536]{2,1,0:T(8,128)(2,1)S(1)} %dynamic-slice_convert_fusion.4), channel_id=1, source_target_pairs={{0,4},{2,6},{4,0},{6,2},{8,12},{10,14},{12,8},{14,10},{16,20},{18,... | collective-permute-start | bytes 1769480 | tf_op jit(solution)/shard_map/ppermute | solution.py:36
  177.7 3.9 %copy-start.4 = (f32[768,1152]{1,0:T(8,128)S(1)}, f32[768,1152]{1,0:T(8,128)}, u32[]{:S(2)}) copy-start(f32[768,1152]{1,0:T(8,128)} %copy.60) | copy-start | bytes 10616836
  177.7 34.1 %collective-permute-start.37 = (bf16[4,96,768]{2,1,0:T(8,128)(2,1)S(1)}, bf16[4,96,768]{2,1,0:T(8,128)(2,1)S(1)}, u32[]{:S(2)}, u32[]{:S(2)}) collective-permute-start(bf16[4,96,768]{2,1,0:T(8,128)(2,1)S(1)} %dynamic-slice_convert_fusion.3), channel_id=1, source_target_pairs={{0,4},{2,6},{4,0},{6,2},{8,12},{10,14},{12,8},{14,10},{16,20},{18,... | collective-permute-start | bytes 1769480 | tf_op jit(solution)/shard_map/ppermute | solution.py:36
  181.6 2.6 collective-permute-start.23
  183.1 26.2 %collective-permute-start.9 = (bf16[4,48,1152]{2,1,0:T(8,128)(2,1)S(1)}, bf16[4,48,1152]{2,1,0:T(8,128)(2,1)S(1)}, u32[]{:S(2)}, u32[]{:S(2)}) collective-permute-start(bf16[4,48,1152]{2,1,0:T(8,128)(2,1)S(1)} %dynamic-slice_convert_fusion.5), channel_id=1, source_target_pairs={{0,4},{2,6},{4,0},{6,2},{8,12},{10,14},{12,8},{14,10},{16,20},{18,... | collective-permute-start | bytes 1327112 | tf_op jit(solution)/shard_map/ppermute | solution.py:36
  209.4 9.5 %collective-permute-start.10 = (bf16[2,48,1152]{2,1,0:T(8,128)(2,1)S(1)}, bf16[2,48,1152]{2,1,0:T(8,128)(2,1)S(1)}, u32[]{:S(2)}, u32[]{:S(2)}) collective-permute-start(bf16[2,48,1152]{2,1,0:T(8,128)(2,1)S(1)} %dynamic-slice_convert_fusion.9), channel_id=1, source_target_pairs={{0,8},{2,10},{4,12},{6,14},{8,0},{10,2},{12,4},{14,6},{16,24},{18,... | collective-permute-start | bytes 663560 | tf_op jit(solution)/shard_map/ppermute | solution.py:36
  210.3 17.9 %collective-permute-start.30 = (bf16[2,48,1536]{2,1,0:T(8,128)(2,1)S(1)}, bf16[2,48,1536]{2,1,0:T(8,128)(2,1)S(1)}, u32[]{:S(2)}, u32[]{:S(2)}) collective-permute-start(bf16[2,48,1536]{2,1,0:T(8,128)(2,1)S(1)} %dynamic-slice_convert_fusion.7), channel_id=1, source_target_pairs={{0,8},{2,10},{4,12},{6,14},{8,0},{10,2},{12,4},{14,6},{16,24},{18,... | collective-permute-start | bytes 884744 | tf_op jit(solution)/shard_map/ppermute | solution.py:36
  219.1 7.0 %collective-permute-start.11 = (bf16[1,48,1152]{2,1,0:T(8,128)(2,1)S(1)}, bf16[1,48,1152]{2,1,0:T(8,128)(2,1)S(1)}, u32[]{:S(2)}, u32[]{:S(2)}) collective-permute-start(bf16[1,48,1152]{2,1,0:T(8,128)(2,1)S(1)} %dynamic-slice_convert_fusion.14), channel_id=1, source_target_pairs={{0,16},{2,18},{4,20},{6,22},{8,24},{10,26},{12,28},{14,30},{16,0},... | collective-permute-start | bytes 331784 | tf_op jit(solution)/shard_map/ppermute | solution.py:36
  220.6 14.0 %collective-permute-start.38 = (bf16[2,96,768]{2,1,0:T(8,128)(2,1)S(1)}, bf16[2,96,768]{2,1,0:T(8,128)(2,1)S(1)}, u32[]{:S(2)}, u32[]{:S(2)}) collective-permute-start(bf16[2,96,768]{2,1,0:T(8,128)(2,1)S(1)} %dynamic-slice_convert_fusion.6), channel_id=1, source_target_pairs={{0,8},{2,10},{4,12},{6,14},{8,0},{10,2},{12,4},{14,6},{16,24},{18,... | collective-permute-start | bytes 884744 | tf_op jit(solution)/shard_map/ppermute | solution.py:36
  226.0 9.5 %collective-permute-start.12 = (bf16[1,48,1152]{2,1,0:T(8,128)(2,1)S(1)}, bf16[1,48,1152]{2,1,0:T(8,128)(2,1)S(1)}, u32[]{:S(2)}, u32[]{:S(2)}) collective-permute-start(bf16[1,48,1152]{2,1,0:T(8,128)(2,1)S(1)} %add_convert_fusion.4), channel_id=1, source_target_pairs={{0,16},{2,18},{4,20},{6,22},{8,24},{10,26},{12,28},{14,30},{16,0},... | collective-permute-start | bytes 331784 | tf_op jit(solution)/shard_map/ppermute | solution.py:36
  228.3 17.5 %collective-permute-start.31 = (bf16[1,48,1536]{2,1,0:T(8,128)(2,1)S(1)}, bf16[1,48,1536]{2,1,0:T(8,128)(2,1)S(1)}, u32[]{:S(2)}, u32[]{:S(2)}) collective-permute-start(bf16[1,48,1536]{2,1,0:T(8,128)(2,1)S(1)} %dynamic-slice_convert_fusion.12), channel_id=1, source_target_pairs={{0,16},{2,18},{4,20},{6,22},{8,24},{10,26},{12,28},{14,30},{16,0},... | collective-permute-start | bytes 442376 | tf_op jit(solution)/shard_map/ppermute | solution.py:36
  234.6 14.4 %collective-permute-start.39 = (bf16[1,96,768]{2,1,0:T(8,128)(2,1)S(1)}, bf16[1,96,768]{2,1,0:T(8,128)(2,1)S(1)}, u32[]{:S(2)}, u32[]{:S(2)}) collective-permute-start(bf16[1,96,768]{2,1,0:T(8,128)(2,1)S(1)} %dynamic-slice_convert_fusion.11), channel_id=1, source_target_pairs={{0,16},{2,18},{4,20},{6,22},{8,24},{10,26},{12,28},{14,30},{16,0},... | collective-permute-start | bytes 442376 | tf_op jit(solution)/shard_map/ppermute | solution.py:36
  235.6 22.5 %collective-permute-start.13 = (bf16[2,48,1152]{2,1,0:T(8,128)(2,1)S(1)}, bf16[2,48,1152]{2,1,0:T(8,128)(2,1)S(1)}, u32[]{:S(2)}, u32[]{:S(2)}) collective-permute-start(bf16[2,48,1152]{2,1,0:T(8,128)(2,1)S(1)} %pad_maximum_fusion.17), channel_id=1, source_target_pairs={{0,8},{2,10},{4,12},{6,14},{8,0},{10,2},{12,4},{14,6},{16,24},{18,... | collective-permute-start | bytes 663560 | tf_op jit(solution)/shard_map/ppermute | solution.py:36
  245.8 6.9 %collective-permute-start.32 = (bf16[1,48,1536]{2,1,0:T(8,128)(2,1)S(1)}, bf16[1,48,1536]{2,1,0:T(8,128)(2,1)S(1)}, u32[]{:S(2)}, u32[]{:S(2)}) collective-permute-start(bf16[1,48,1536]{2,1,0:T(8,128)(2,1)S(1)} %add_convert_fusion.3), channel_id=1, source_target_pairs={{0,16},{2,18},{4,20},{6,22},{8,24},{10,26},{12,28},{14,30},{16,0},... | collective-permute-start | bytes 442376 | tf_op jit(solution)/shard_map/ppermute | solution.py:36
  249.0 7.7 %collective-permute-start.40 = (bf16[1,96,768]{2,1,0:T(8,128)(2,1)S(1)}, bf16[1,96,768]{2,1,0:T(8,128)(2,1)S(1)}, u32[]{:S(2)}, u32[]{:S(2)}) collective-permute-start(bf16[1,96,768]{2,1,0:T(8,128)(2,1)S(1)} %add_convert_fusion.2), channel_id=1, source_target_pairs={{0,16},{2,18},{4,20},{6,22},{8,24},{10,26},{12,28},{14,30},{16,0},... | collective-permute-start | bytes 442376 | tf_op jit(solution)/shard_map/ppermute | solution.py:36
  252.8 10.1 %collective-permute-start.33 = (bf16[2,48,1536]{2,1,0:T(8,128)(2,1)S(1)}, bf16[2,48,1536]{2,1,0:T(8,128)(2,1)S(1)}, u32[]{:S(2)}, u32[]{:S(2)}) collective-permute-start(bf16[2,48,1536]{2,1,0:T(8,128)(2,1)S(1)} %pad_maximum_fusion.15), channel_id=1, source_target_pairs={{0,8},{2,10},{4,12},{6,14},{8,0},{10,2},{12,4},{14,6},{16,24},{18,... | collective-permute-start | bytes 884744 | tf_op jit(solution)/shard_map/ppermute | solution.py:36
  256.7 10.6 %collective-permute-start.41 = (bf16[2,96,768]{2,1,0:T(8,128)(2,1)S(1)}, bf16[2,96,768]{2,1,0:T(8,128)(2,1)S(1)}, u32[]{:S(2)}, u32[]{:S(2)}) collective-permute-start(bf16[2,96,768]{2,1,0:T(8,128)(2,1)S(1)} %pad_maximum_fusion.16), channel_id=1, source_target_pairs={{0,8},{2,10},{4,12},{6,14},{8,0},{10,2},{12,4},{14,6},{16,24},{18,... | collective-permute-start | bytes 884744 | tf_op jit(solution)/shard_map/ppermute | solution.py:36
  258.3 12.9 %collective-permute-start.14 = (bf16[4,48,1152]{2,1,0:T(8,128)(2,1)S(1)}, bf16[4,48,1152]{2,1,0:T(8,128)(2,1)S(1)}, u32[]{:S(2)}, u32[]{:S(2)}) collective-permute-start(bf16[4,48,1152]{2,1,0:T(8,128)(2,1)S(1)} %pad_maximum_fusion.13), channel_id=1, source_target_pairs={{0,4},{2,6},{4,0},{6,2},{8,12},{10,14},{12,8},{14,10},{16,20},{18,... | collective-permute-start | bytes 1327112 | tf_op jit(solution)/shard_map/ppermute | solution.py:36
  263.0 20.8 %collective-permute-start.34 = (bf16[4,48,1536]{2,1,0:T(8,128)(2,1)S(1)}, bf16[4,48,1536]{2,1,0:T(8,128)(2,1)S(1)}, u32[]{:S(2)}, u32[]{:S(2)}) collective-permute-start(bf16[4,48,1536]{2,1,0:T(8,128)(2,1)S(1)} %pad_maximum_fusion.11), channel_id=1, source_target_pairs={{0,4},{2,6},{4,0},{6,2},{8,12},{10,14},{12,8},{14,10},{16,20},{18,... | collective-permute-start | bytes 1769480 | tf_op jit(solution)/shard_map/ppermute | solution.py:36
  267.5 24.4 %collective-permute-start.42 = (bf16[4,96,768]{2,1,0:T(8,128)(2,1)S(1)}, bf16[4,96,768]{2,1,0:T(8,128)(2,1)S(1)}, u32[]{:S(2)}, u32[]{:S(2)}) collective-permute-start(bf16[4,96,768]{2,1,0:T(8,128)(2,1)S(1)} %pad_maximum_fusion.12), channel_id=1, source_target_pairs={{0,4},{2,6},{4,0},{6,2},{8,12},{10,14},{12,8},{14,10},{16,20},{18,... | collective-permute-start | bytes 1769480 | tf_op jit(solution)/shard_map/ppermute | solution.py:36
  271.4 21.7 %collective-permute-start.15 = (bf16[8,48,1152]{2,1,0:T(8,128)(2,1)S(1)}, bf16[8,48,1152]{2,1,0:T(8,128)(2,1)S(1)}, u32[]{:S(2)}, u32[]{:S(2)}) collective-permute-start(bf16[8,48,1152]{2,1,0:T(8,128)(2,1)S(1)} %pad_maximum_fusion.9), channel_id=1, source_target_pairs={{0,2},{2,0},{4,6},{6,4},{8,10},{10,8},{12,14},{14,12},{16,18},{18,... | collective-permute-start | bytes 2654216 | tf_op jit(solution)/shard_map/ppermute | solution.py:36
  285.0 20.8 %collective-permute-start.35 = (bf16[8,48,1536]{2,1,0:T(8,128)(2,1)}, bf16[8,48,1536]{2,1,0:T(8,128)(2,1)}, u32[]{:S(2)}, u32[]{:S(2)}) collective-permute-start(bf16[8,48,1536]{2,1,0:T(8,128)(2,1)} %pad_maximum_fusion.5), channel_id=1, source_target_pairs={{0,2},{2,0},{4,6},{6,4},{8,10},{10,8},{12,14},{14,12},{16,18},{18,... | collective-permute-start | bytes 3538952 | tf_op jit(solution)/shard_map/ppermute | solution.py:36
  293.1 17.3 %collective-permute-start.43 = (bf16[8,96,768]{2,1,0:T(8,128)(2,1)}, bf16[8,96,768]{2,1,0:T(8,128)(2,1)}, u32[]{:S(2)}, u32[]{:S(2)}) collective-permute-start(bf16[8,96,768]{2,1,0:T(8,128)(2,1)} %pad_maximum_fusion.6), channel_id=1, source_target_pairs={{0,2},{2,0},{4,6},{6,4},{8,10},{10,8},{12,14},{14,12},{16,18},{18,... | collective-permute-start | bytes 3538952 | tf_op jit(solution)/shard_map/ppermute | solution.py:36
  (28 other events, 57.4 us)

commit v2 on v1

v2 whole, which is shorter than its diff:
```python
import functools

import jax
import jax.numpy as jnp
from jax import lax
from jax.experimental import pallas as pl
from jax.experimental.pallas import tpu as pltpu
from jax.sharding import PartitionSpec as P

HEAD_DIM = 64
norm_eps = 1e-06
root_half = 0.7071067811865476
inv_root_two_pi = 0.3989422804014327
log2_e = 1.4426950408889634
LOW = jnp.bfloat16
WIDE = jnp.float32
LANES = 128
MESH = pl.DeviceIdType.MESH
VMEM_BYTES = 67043328


def dot(a, b):
    return lax.dot_general(a, b, (((1,), (0,)), ((), ())), preferred_element_type=WIDE)


def dot_nt(a, b):
    return lax.dot_general(a, b, (((1,), (1,)), ((), ())), preferred_element_type=WIDE)


def dot_tn(a, b):
    return lax.dot_general(a, b, (((0,), (0,)), ((), ())), preferred_element_type=WIDE)


def normalize(values):
    centered = values - jnp.mean(values, axis=-1, keepdims=True)
    inverse = lax.rsqrt(jnp.mean(centered * centered, axis=-1, keepdims=True) + norm_eps)
    return centered * inverse, inverse


def norm_backward(upstream, normal, inverse, gain_vec):
    scaled = upstream * gain_vec
    return inverse * (
        scaled
        - jnp.mean(scaled, axis=-1, keepdims=True)
        - normal * jnp.mean(scaled * normal, axis=-1, keepdims=True)
    )


def col_sum(x):
    return jnp.sum(x, axis=0, keepdims=True)


def cat(parts):
    return jnp.concatenate(parts, axis=1)


class Ring:
    def __init__(self, order, extra, first, out, recv, send, keep, fin, xsend, xrecv, sems, peer, bit_of):
        self.order, self.extra = order, extra
        self.first, self.out = first, out
        self.recv, self.send, self.keep, self.fin = recv, send, keep, fin
        self.xsend, self.xrecv = xsend, xrecv
        self.ssem, self.rsem, self.lsem = sems
        self.peer = peer
        self.mine = [bit_of(b) for b in order]
        units = first.shape[0]
        self.sizes = [units >> (k + 1) for k in range(len(order))]
        self.base = []
        base = 0
        for k in range(len(order)):
            base = base + self.mine[k] * self.sizes[k]
            self.base.append(base)

    def _copy(self, src, dst, slot, bit):
        return pltpu.make_async_remote_copy(
            src_ref=src, dst_ref=dst, send_sem=self.ssem.at[slot], recv_sem=self.rsem.at[slot],
            device_id=self.peer(bit), device_id_type=MESH)

    def _rs(self, k):
        size = self.sizes[k]
        if k == 0:
            src = self.first.at[pl.ds((1 - self.mine[0]) * size, size)]
        else:
            src = self.send[k - 1]
        return self._copy(src, self.recv[k], k, self.order[k])

    def _x(self, j):
        return self._copy(self.xsend, self.xrecv.at[pl.ds(j, 1)], len(self.order) + j, self.extra[j])

    def _ag(self, k):
        last = len(self.order) - 1
        slot = len(self.order) + len(self.extra) + k
        if k == last:
            return self._copy(self.fin, self.out.at[pl.ds(self.base[k], 1)], slot, self.order[k])
        size = self.sizes[k]
        part = self.out.at[pl.ds(self.base[k], size)]
        return self._copy(part, part, slot, self.order[k])

    def _own(self):
        return pltpu.make_async_copy(self.fin, self.out.at[pl.ds(self.base[-1], 1)], self.lsem)

    def start(self):
        self._rs(0).start()

    def _value(self, k, u):
        got = self.recv[k][u].astype(WIDE)
        if k == 0:
            return self.first[self.mine[0] * self.sizes[0] + u].astype(WIDE) + got
        return self.keep[k - 1][u] + got

    def reduce(self, k):
        self._rs(k).wait_recv()
        if k + 1 < len(self.order):
            half = self.sizes[k + 1]
            mine = self.mine[k + 1]

            def out_part(j, c):
                self.send[k][j] = self._value(k, (1 - mine) * half + j).astype(LOW)
                return c

            lax.fori_loop(0, half, out_part, 0)
            self._rs(k + 1).start()

            def own_part(j, c):
                self.keep[k][j] = self._value(k, mine * half + j)
                return c

            lax.fori_loop(0, half, own_part, 0)
        else:
            total = self._value(k, 0)
            for j in range(len(self.extra)):
                self.xsend[0] = total.astype(LOW)
                self._x(j).start()
                self._x(j).wait()
                total = self.xsend[0].astype(WIDE) + self.xrecv[j].astype(WIDE)
            self.fin[0] = total.astype(LOW)
            self._ag(k).start()
            self._own().start()

    def gather(self, k):
        self._ag(k + 1).wait_recv()
        if k + 2 == len(self.order):
            self._own().wait()
        if k >= 0:
            self._ag(k).start()

    def finish(self):
        for k in range(len(self.order)):
            self._rs(k).wait_send()
            self._ag(k).wait_send()


def kernel(n, refs):
    (tokens, wqkv_hbm, wout_hbm, wup_hbm, wdown_hbm, gain_one, shift_one, b_up, gain_two, shift_two,
     perm, count, index, cot,
     result, grad_tokens, o_down, o_up, o_out, o_qkv, small_out,
     wqkv, wout, wup, wdown, wsem,
     tok, qkv, sel_t, sel, blk, tokc, qc, probs, ctxc, normal_one, inverse_one, normed_one, low_one, slope,
     hidden, part, part_got, gb, gtwo, gin, back, back_got, gattn, gctx, dqc, dall, far, far_got, near,
     ctx, pre_two, down_far, down_got, stats, stats_got,
     f_down, f_up, f_out, f_qkv, small, small_got,
     xs_send, xs_recv, lsem, ring_refs) = refs
    rows, own = tokens.shape
    width = wout.shape[0]
    local = wqkv.shape[1] // 3
    pairs = local // LANES
    slots = index.shape[1]
    ff = wup.shape[1]
    block_len = rows // 2
    tile = 256
    tiles = rows // tile
    scale = HEAD_DIM ** (-0.5)
    b = lax.axis_index("batch")
    h = lax.axis_index("head")
    other = 1 - h
    bits = [1 << k for k in range(n.bit_length() - 1)]

    def bit_of(bit):
        return lax.rem(lax.div(b, bit), 2)

    def peer(bit):
        return (b + bit - 2 * bit * bit_of(bit), h)

    x_peer = (b, other)

    def x_copy(src, dst, slot):
        return pltpu.make_async_remote_copy(
            src_ref=src, dst_ref=dst, send_sem=xs_send.at[slot], recv_sem=xs_recv.at[slot],
            device_id=x_peer, device_id_type=MESH)

    loads = [pltpu.make_async_copy(s, d, wsem.at[i]) for i, (s, d) in enumerate(
        ((wqkv_hbm, wqkv), (wout_hbm, wout), (wup_hbm, wup), (wdown_hbm, wdown)))]
    for cp in loads:
        cp.start()
    barrier = pltpu.get_barrier_semaphore()
    pl.semaphore_signal(barrier, inc=1, device_id=x_peer, device_id_type=MESH)
    for bit in bits:
        pl.semaphore_signal(barrier, inc=1, device_id=peer(bit), device_id_type=MESH)
    pl.semaphore_wait(barrier, 1 + len(bits))

    own_cols = pl.ds(pl.multiple_of(h * own, LANES), own)
    far_cols = pl.ds(pl.multiple_of(other * own, LANES), own)

    def row_tile(r):
        return pl.ds(pl.multiple_of(r * tile, tile), tile)

    def tok_copy(r):
        return x_copy(tokens.at[row_tile(r)], tok.at[row_tile(r), own_cols], r)

    for r in range(tiles):
        tok_copy(r).start()
    own_tok = pltpu.make_async_copy(tokens, tok.at[:, own_cols], lsem.at[0])
    own_tok.start()

    lane_slot = lax.broadcasted_iota(jnp.int32, (1, slots), 1)
    idx = jnp.where(lane_slot < count[...], index[...], -1)
    picked = jnp.where(lax.broadcasted_iota(jnp.int32, (rows, slots), 0) == idx, 1.0, 0.0)
    sel_t[...] = picked.astype(LOW)
    picked = jnp.transpose(picked)
    sel[...] = picked.astype(LOW)
    blk[...] = jnp.broadcast_to(jnp.sum(picked[:, block_len:], axis=1, keepdims=True), blk.shape)
    own_tok.wait()
    loads[0].wait()

    def qkv_tile(r, c):
        tok_copy(r).wait_recv()
        out = dot(tok[row_tile(r), :], wqkv[...]).astype(LOW)
        for j in range(3 * pairs):
            qkv[j, row_tile(r), :] = out[:, j * LANES:(j + 1) * LANES]
        return c

    lax.fori_loop(0, tiles, qkv_tile, 0)

    low_lane = lax.broadcasted_iota(jnp.int32, (1, LANES), 1) < HEAD_DIM
    tokc[...] = dot(sel[...], tok[...]).astype(LOW)

    def keep_head(x, e):
        return jnp.where(low_lane, x, 0.0).astype(LOW) if e == 0 else jnp.where(low_lane, 0.0, x).astype(LOW)

    def second(head):
        pair = perm[pl.ds(head, 1), :].astype(WIDE)
        return (pair[:, :1] + blk[:, :1] * (pair[:, 1:] - pair[:, :1])) > 0.5

    def masked_attention(p, c):
        q2 = dot(sel[...], qkv[p]).astype(LOW)
        qc[p] = q2
        halves = []
        for e in range(2):
            head = 2 * p + e
            late = second(head)
            qm = keep_head(q2.astype(WIDE), e)
            s = jnp.where(late, dot_nt(qm, qkv[pairs + p, block_len:, :]),
                          dot_nt(qm, qkv[pairs + p, :block_len, :])) * (scale * log2_e)
            ex = jnp.exp2(s - jnp.max(s, axis=-1, keepdims=True))
            pr = ex * (1.0 / jnp.sum(ex, axis=-1, keepdims=True))
            probs[head] = pr
            pr = pr.astype(LOW)
            halves.append(jnp.where(late, dot(pr, qkv[2 * pairs + p, block_len:, :]),
                                    dot(pr, qkv[2 * pairs + p, :block_len, :])))
        ctxc[h * pairs + p] = jnp.where(low_lane, halves[0], halves[1]).astype(LOW)
        return c

    lax.fori_loop(0, pairs, masked_attention, 0)
    mine_c = ctxc.at[pl.ds(h * pairs, pairs)]
    ctxc_copy = x_copy(mine_c, mine_c, 4)
    ctxc_copy.start()

    def attend(i, c):
        p = lax.div(i, 2)
        q_block = lax.rem(i, 2)
        q_rows = pl.ds(pl.multiple_of(q_block * block_len, block_len), block_len)
        q2 = qkv[p, q_rows, :].astype(WIDE)
        even, odd = (perm[pl.ds(2 * p + e, 1), :].astype(WIDE) for e in range(2))
        late = jnp.where(low_lane, jnp.where(q_block == 0, even[:, :1], even[:, 1:]),
                         jnp.where(q_block == 0, odd[:, :1], odd[:, 1:])) > 0.5

        def chosen(j):
            return jnp.where(late, qkv[j, block_len:, :].astype(WIDE), qkv[j, :block_len, :].astype(WIDE)).astype(LOW)

        k2, v2 = chosen(pairs + p), chosen(2 * pairs + p)
        halves = []
        for e in range(2):
            s = dot_nt(keep_head(q2, e), k2) * (scale * log2_e)
            ex = jnp.exp2(s - jnp.max(s, axis=-1, keepdims=True))
            inv = 1.0 / jnp.sum(ex, axis=-1, keepdims=True)
            halves.append(dot(ex.astype(LOW), v2) * inv)
        ctx[h * pairs + p, q_rows, :] = jnp.where(low_lane, halves[0], halves[1]).astype(LOW)
        return c

    attend_units = 2 * pairs
    cut = attend_units // 3
    lax.fori_loop(0, cut, attend, 0)

    ctxc_copy.wait_recv()
    for cp in loads[1:]:
        cp.wait()
    pre = tokc[...].astype(WIDE) + dot(cat([ctxc[j] for j in range(2 * pairs)]), wout[...])
    nrm_c, inv_c = normalize(pre)
    normal_one[...] = nrm_c
    inverse_one[...] = jnp.broadcast_to(inv_c, inverse_one.shape)
    nrm_c = nrm_c * gain_one[...] + shift_one[...]
    normed_one[...] = nrm_c
    low_one[...] = nrm_c.astype(LOW)
    ff_tile = 384

    def up_tile(i, c):
        cols = pl.ds(pl.multiple_of(i * ff_tile, ff_tile), ff_tile)
        u = dot(low_one[...], wup[:, cols]) + b_up[:, cols]
        cdf = 0.5 * (1.0 + lax.erf(u * root_half))
        hidden[:, cols] = (u * cdf).astype(LOW)
        slope[:, cols] = cdf + u * inv_root_two_pi * jnp.exp(-0.5 * u * u)
        return c

    lax.fori_loop(0, ff // ff_tile, up_tile, 0)
    part[...] = dot(hidden[...], wdown[...]).astype(LOW)
    part_copy = x_copy(part, part_got, 5)
    part_copy.start()
    lax.fori_loop(cut, attend_units, attend, 0)
    part_copy.wait_recv()

    normal_two, inv_two = normalize(normed_one[...] + (part[...].astype(WIDE) + part_got[...].astype(WIDE)))
    alive = lax.broadcasted_iota(jnp.int32, (slots, 1), 0) < count[...]
    up = jnp.where(alive, cot[...].astype(WIDE), 0.0)
    g2 = norm_backward(up, normal_two, inv_two, gain_two[...])
    gtwo[...] = g2
    gb[...] = g2.astype(LOW)
    small[2:3, :] = cat([col_sum(up * normal_two), col_sum(up)])

    def in_tile(i, c):
        cols = pl.ds(pl.multiple_of(i * ff_tile, ff_tile), ff_tile)
        g = (dot_nt(gb[...], wdown[cols, :]) * slope[:, cols]).astype(LOW)
        gin[:, cols] = g
        small[0:1, cols] = col_sum(g.astype(WIDE))
        return c

    lax.fori_loop(0, ff // ff_tile, in_tile, 0)
    back[...] = dot_nt(gin[...], wup[...]).astype(LOW)
    back_copy = x_copy(back, back_got, 6)
    back_copy.start()

    rings = ring_refs
    ring_down, ring_up, ring_out, ring_qkv = (
        Ring(peer=peer, bit_of=bit_of, **r) for r in rings)

    def put(first, unit, value):
        r = first.shape[1]
        for j in range(value.shape[0] // r):
            first[unit + j] = value[j * r:(j + 1) * r, :]

    units = f_down.shape[0]

    def down_tile(i, c):
        cols = pl.ds(pl.multiple_of(i * ff_tile, ff_tile), ff_tile)
        put(f_down, i * (ff_tile * units // ff), dot_tn(hidden[:, cols], gb[...]).astype(LOW))
        return c

    lax.fori_loop(0, ff // ff_tile, down_tile, 0)
    ring_down.start()

    def up_grad_tile(i, c):
        cols = pl.ds(pl.multiple_of(i * ff_tile, ff_tile), ff_tile)
        put(f_up, i * (ff_tile * units // width), dot_tn(low_one[:, cols], gin[...]).astype(LOW))
        return c

    lax.fori_loop(0, width // ff_tile, up_grad_tile, 0)
    ring_up.start()
    ring_down.reduce(0)
    ring_up.reduce(0)
    back_copy.wait_recv()

    gn = gtwo[...] + (back[...].astype(WIDE) + back_got[...].astype(WIDE))
    small[1:2, :] = cat([col_sum(gn * normal_one[...]), col_sum(gn)])
    g1 = norm_backward(gn, normal_one[...], inverse_one[:, :1], gain_one[...])
    gtwo[...] = g1
    gattn[...] = g1.astype(LOW)
    own_rows = pl.ds(pl.multiple_of(h * local, LANES), local)
    gc = dot_nt(gattn[...], wout[own_rows, :]).astype(LOW)
    for p in range(pairs):
        gctx[p] = gc[:, p * LANES:(p + 1) * LANES]

    def masked_backward(p, c):
        q2 = qc[p].astype(WIDE)
        g2 = gctx[p].astype(WIDE)
        k2 = cat([qkv[pairs + p, :block_len, :], qkv[pairs + p, block_len:, :]])
        dk = jnp.zeros((block_len, 2 * LANES), WIDE)
        dv = jnp.zeros((block_len, 2 * LANES), WIDE)
        dq = []
        for e in range(2):
            head = 2 * p + e
            late = second(head)
            gm = keep_head(g2, e)
            dp = jnp.where(late, dot_nt(gm, qkv[2 * pairs + p, block_len:, :]),
                           dot_nt(gm, qkv[2 * pairs + p, :block_len, :]))
            pr = probs[head]
            t = dp * pr
            ds = (t - pr * jnp.sum(t, axis=-1, keepdims=True)).astype(LOW)
            qm = keep_head(q2, e).astype(WIDE)
            gm = gm.astype(WIDE)
            dk = dk + dot_tn(ds, cat([jnp.where(late, 0.0, qm), jnp.where(late, qm, 0.0)]).astype(LOW))
            dv = dv + dot_tn(pr.astype(LOW),
                             cat([jnp.where(late, 0.0, gm), jnp.where(late, gm, 0.0)]).astype(LOW))
            both = dot(ds, k2)
            dq.append(jnp.where(late, both[:, LANES:], both[:, :LANES]))
        d = (jnp.where(low_lane, dq[0], dq[1]) * scale).astype(LOW)
        dqc[p] = d
        dall[p] = dot(sel_t[...], d).astype(LOW)
        dk = (dk * scale).astype(LOW)
        dv = dv.astype(LOW)
        dall[pairs + p, :block_len, :] = dk[:, :LANES]
        dall[pairs + p, block_len:, :] = dk[:, LANES:]
        dall[2 * pairs + p, :block_len, :] = dv[:, :LANES]
        dall[2 * pairs + p, block_len:, :] = dv[:, LANES:]
        return c

    lax.fori_loop(0, pairs, masked_backward, 0)

    small[3:8, :] = jnp.zeros((5, small.shape[1]), WIDE)

    def small_copy(k):
        return pltpu.make_async_remote_copy(
            src_ref=small.at[pl.ds(8 * k, 8)], dst_ref=small_got.at[pl.ds(8 * k, 8)],
            send_sem=xs_send.at[18 + k], recv_sem=xs_recv.at[18 + k],
            device_id=peer(bits[k]), device_id_type=MESH)

    def small_step(k):
        small_copy(k).wait_recv()
        total = small[8 * k:8 * k + 8, :] + small_got[8 * k:8 * k + 8, :]
        if k + 1 < len(bits):
            small[8 * k + 8:8 * k + 16, :] = total
            small_copy(k + 1).start()
        else:
            small_out[...] = total

    small_copy(0).start()

    put(f_out, 0, dot_tn(cat([ctxc[h * pairs + p] for p in range(pairs)]), gattn[...]).astype(LOW))
    ring_out.start()

    def qkv_grad_tile(i, c):
        cols = pl.ds(pl.multiple_of(i * ff_tile, ff_tile), ff_tile)
        gq = dot_tn(tokc[:, cols], cat([dqc[p] for p in range(pairs)]))
        gkv = dot_tn(tok[:, cols], cat([dall[pairs + j] for j in range(2 * pairs)]))
        put(f_qkv, i * (ff_tile * units // width), cat([gq, gkv]).astype(LOW))
        return c

    lax.fori_loop(0, width // ff_tile, qkv_grad_tile, 0)
    ring_qkv.start()
    small_step(0)

    def far_copy(r):
        return x_copy(far.at[row_tile(r)], far_got.at[row_tile(r)], 7 + r)

    def far_tile(r, c):
        d = cat([dall[j, row_tile(r), :] for j in range(3 * pairs)])
        far[row_tile(r), :] = dot_nt(d, wqkv[far_cols, :]).astype(LOW)
        far_copy(r).start()
        return c

    def ctx_copy():
        part_ref = ctx.at[pl.ds(h * pairs, pairs)]
        return x_copy(part_ref, part_ref, 11)

    ctx_copy().start()
    lax.fori_loop(0, tiles, far_tile, 0)
    ring_out.reduce(0)
    ring_qkv.reduce(0)
    ring_down.reduce(1)
    ring_up.reduce(1)
    for k in range(1, len(bits)):
        small_step(k)
    mine = gtwo[:, own_cols]
    high = mine.astype(LOW)
    rest = (mine - high.astype(WIDE)).astype(LOW)
    halves = cat([high, rest])

    def near_tile(r, c):
        d = cat([dall[j, row_tile(r), :] for j in range(3 * pairs)])
        spread = dot(sel_t[row_tile(r), :], halves)
        near[row_tile(r), :] = dot_nt(d, wqkv[own_cols, :]) + (spread[:, :own] + spread[:, own:])
        return c

    lax.fori_loop(0, tiles, near_tile, 0)
    ring_down.reduce(2)
    ring_up.reduce(2)
    ctx_copy().wait_recv()

    def down_copy(r):
        return x_copy(down_far.at[row_tile(r)], down_got.at[row_tile(r)], 12 + r)

    def layer_tile(r, c):
        rs = row_tile(r)
        pre_r = tok[rs, :].astype(WIDE) + dot(cat([ctx[j, rs, :] for j in range(2 * pairs)]), wout[...])
        normed = normalize(pre_r)[0] * gain_one[...] + shift_one[...]
        normed_one[...] = normed
        u = dot(normed.astype(LOW), wup[...]) + b_up[...]
        hid = (u * (0.5 * (1.0 + lax.erf(u * root_half)))).astype(LOW)
        down_far[rs, :] = dot(hid, wdown[:, far_cols]).astype(LOW)
        down_copy(r).start()
        pre_two[rs, :] = normed_one[:, own_cols] + dot(hid, wdown[:, own_cols])
        return c

    lax.fori_loop(0, tiles // 2, layer_tile, 0)
    ring_out.reduce(1)
    ring_qkv.reduce(1)
    ring_down.reduce(3)
    ring_up.reduce(3)
    lax.fori_loop(tiles // 2, tiles, layer_tile, 0)
    ring_out.reduce(2)
    ring_qkv.reduce(2)
    ring_down.gather(2)
    ring_up.gather(2)

    def grad_tile(r, c):
        far_copy(r).wait_recv()
        far_copy(r).wait_send()
        far[row_tile(r), :] = (near[row_tile(r), :] + far_got[row_tile(r), :].astype(WIDE)).astype(LOW)
        return c

    lax.fori_loop(0, tiles, grad_tile, 0)
    grad_out = pltpu.make_async_copy(far, grad_tokens, lsem.at[1])
    grad_out.start()
    ring_out.reduce(3)
    ring_qkv.reduce(3)
    ring_down.gather(1)
    ring_up.gather(1)

    first_lane = lax.broadcasted_iota(jnp.int32, (1, LANES), 1) < 1

    def stat_tile(r, c):
        rs = row_tile(r)
        down_copy(r).wait_recv()
        x = pre_two[rs, :] + down_got[rs, :].astype(WIDE)
        pre_two[rs, :] = x
        mean = jnp.mean(x, axis=-1, keepdims=True)
        dev = x - mean
        var = jnp.mean(dev * dev, axis=-1, keepdims=True)
        both = jnp.where(first_lane, mean, var)
        stats[r] = jnp.transpose(both)[:8, :]
        return c

    lax.fori_loop(0, tiles, stat_tile, 0)
    stats_copy = x_copy(stats, stats_got, 16)
    stats_copy.start()
    ring_out.gather(2)
    ring_qkv.gather(2)
    ring_down.gather(0)
    ring_up.gather(0)
    stats_copy.wait_recv()

    def result_tile(r, c):
        rs = row_tile(r)
        x = pre_two[rs, :]
        fill = jnp.zeros((LANES - 8, tile), WIDE)
        one = jnp.transpose(jnp.concatenate([stats[r], fill], axis=0))
        two = jnp.transpose(jnp.concatenate([stats_got[r], fill], axis=0))
        mean = 0.5 * (one[:, :1] + two[:, :1])
        gap = 0.5 * (one[:, :1] - two[:, :1])
        var = 0.5 * (one[:, 1:2] + two[:, 1:2]) + gap * gap
        down_copy(r).wait_send()
        down_far[rs, :] = ((x - mean) * lax.rsqrt(var + norm_eps) * gain_two[:, own_cols]
                         + shift_two[:, own_cols]).astype(LOW)
        return c

    lax.fori_loop(0, tiles, result_tile, 0)
    result_out = pltpu.make_async_copy(down_far, result, lsem.at[2])
    result_out.start()
    ring_out.gather(1)
    ring_qkv.gather(1)
    ring_out.gather(0)
    ring_qkv.gather(0)
    for ring in (ring_down, ring_up, ring_out, ring_qkv):
        ring.gather(-1)

    for r in range(tiles):
        tok_copy(r).wait_send()
    grad_out.wait()
    result_out.wait()
    for cp in (ctxc_copy, part_copy, back_copy, ctx_copy(), stats_copy):
        cp.wait_send()
    for k in range(len(bits)):
        small_copy(k).wait_send()
    for ring in (ring_down, ring_up, ring_out, ring_qkv):
        ring.finish()


def build(n, tokens, wqkv, wout, gain_one, shift_one, wup, b_up, wdown, gain_two, shift_two, perm, index,
          count, cot):
    rows, own = tokens.shape
    width = wout.shape[0]
    local = wqkv.shape[1] // 3
    pairs = local // LANES
    heads = local // HEAD_DIM
    slots = index.shape[1]
    ff = wup.shape[1]
    block_len = rows // 2
    tile = 256
    steps = n.bit_length() - 1
    bits = [1 << k for k in range(steps)]
    depth = min(4, steps)
    units = 1 << depth
    halving, extra = bits[:depth], bits[depth:]

    vm = pltpu.VMEM
    groups = {"down": (ff // units, width), "up": (width // units, ff), "out": (local // units, width),
              "qkv": (width // units, 3 * local)}
    orders = {g: halving for g in groups}
    dma = pltpu.SemaphoreType.DMA

    def ring_scratch(g):
        r, c = groups[g]
        sizes = [units >> (k + 1) for k in range(depth)]
        return {
            "recv": [vm((s, r, c), LOW) for s in sizes],
            "send": [vm((s, r, c), LOW) for s in sizes[1:]],
            "keep": [vm((s, r, c), WIDE) for s in sizes[1:]],
            "fin": vm((1, r, c), LOW),
            "xsend": vm((1, r, c) if extra else (1, 8, LANES), LOW),
            "xrecv": vm((len(extra), r, c) if extra else (1, 8, LANES), LOW),
            "sems": (dma((2 * depth + len(extra),)), dma((2 * depth + len(extra),)), dma(())),
        }

    f = [vm((units,) + groups[g], LOW) for g in groups]
    scratch = [
        vm(wqkv.shape, LOW), vm(wout.shape, LOW), vm(wup.shape, LOW), vm(wdown.shape, LOW), dma((4,)),
        vm((rows, width), LOW), vm((3 * pairs, rows, LANES), LOW), vm((rows, slots), LOW), vm((slots, rows), LOW),
        vm((slots, LANES), WIDE), vm((slots, width), LOW), vm((pairs, slots, LANES), LOW),
        vm((heads, slots, block_len), WIDE), vm((2 * pairs, slots, LANES), LOW), vm((slots, width), WIDE),
        vm((slots, LANES), WIDE), vm((slots, width), WIDE), vm((slots, width), LOW), vm((slots, ff), WIDE),
        vm((slots, ff), LOW), vm((slots, width), LOW), vm((slots, width), LOW), vm((slots, width), LOW),
        vm((slots, width), WIDE), vm((slots, ff), LOW), vm((slots, width), LOW), vm((slots, width), LOW),
        vm((slots, width), LOW), vm((pairs, slots, LANES), LOW),
        vm((pairs, slots, LANES), LOW), vm((3 * pairs, rows, LANES), LOW), vm((rows, own), LOW),
        vm((rows, own), LOW), vm((rows, own), WIDE),
        vm((2 * pairs, rows, LANES), LOW), vm((rows, own), WIDE), vm((rows, own), LOW),
        vm((rows, own), LOW), vm((rows // tile, 8, tile), WIDE), vm((rows // tile, 8, tile), WIDE),
        *f, vm((8 * steps, ff), WIDE), vm((8 * steps, ff), WIDE),
        dma((18 + steps,)), dma((18 + steps,)), dma((3,)),
    ]
    plain = len(scratch)
    ring_specs = [ring_scratch(g) for g in groups]
    flat, tree = jax.tree.flatten(ring_specs, is_leaf=lambda x: not isinstance(x, (dict, list, tuple)))
    n_in, n_out = 14, 7

    def run(*refs):
        head_refs = refs[:n_in + n_out + plain]
        rings = jax.tree.unflatten(tree, refs[n_in + n_out + plain:])
        firsts = head_refs[-(len(groups) + 5):-5]
        outs = refs[n_in + 2:n_in + 2 + len(groups)]
        full = []
        for g, ring, first, out in zip(groups, rings, firsts, outs):
            full.append(dict(order=orders[g], extra=extra, first=first, out=out, **ring))
        kernel(n, (*head_refs, full))

    hbm = pl.BlockSpec(memory_space=pl.ANY)
    v = pl.BlockSpec(memory_space=pltpu.VMEM)
    shape = jax.ShapeDtypeStruct
    return pl.pallas_call(
        run,
        out_shape=(shape((rows, own), LOW), shape((rows, own), LOW),
                   *(shape((units,) + groups[g], LOW) for g in groups), shape((8, ff), WIDE)),
        in_specs=[hbm, hbm, hbm, hbm, hbm, v, v, v, v, v, v, v, v, v],
        out_specs=(hbm, hbm, hbm, hbm, hbm, hbm, v),
        scratch_shapes=scratch + flat,
        compiler_params=pltpu.CompilerParams(
            collective_id=0, has_side_effects=True, vmem_limit_bytes=VMEM_BYTES),
        name="layer",
    )(tokens, wqkv, wout, wup, wdown, gain_one, shift_one, b_up, gain_two, shift_two, perm, count, index, cot)


def body(n, tokens, w_qkv, w_out, gain_one, attention_norm_bias, w_up, b_up, w_down, gain_two, shift_two,
         block_perm, mask_index, mask_count, cotangent):
    width = w_out.shape[0]
    local = w_qkv.shape[2]

    def row(x):
        return x.reshape(1, -1)

    result, grad_tokens, g_down, g_up, g_out, g_qkv, small = build(
        n, tokens, w_qkv.reshape(width, 3 * local), w_out, row(gain_one), row(attention_norm_bias), w_up,
        row(b_up), w_down, row(gain_two), row(shift_two), block_perm, mask_index, mask_count.reshape(1, 1), cotangent[0])
    return (
        result, grad_tokens, g_qkv.reshape(width, 3, local).astype(WIDE), g_out.reshape(local, width).astype(WIDE),
        small[1, :width], small[1, width:], g_up.reshape(w_up.shape).astype(WIDE), small[0],
        g_down.reshape(w_down.shape).astype(WIDE), small[2, :width], small[2, width:])


def solution(mesh):
    return jax.shard_map(
        functools.partial(body, mesh.shape["batch"]),
        mesh=mesh,
        in_specs=(P("batch", "head"), P(None, None, "head"), P(), P(), P(), P(None, "head"), P("head"),
                  P("head", None), P(), P(), P("head", None), P("batch", None), P("batch"),
                  P("batch", None, None)),
        out_specs=(P("batch", "head"), P("batch", "head"), P(None, None, "head"), P("head", None), P(), P(),
                   P(None, "head"), P("head"), P("head", None), P(), P()),
        check_vma=False,
    )
```

time: 321 us -> 213 us (0.66); the launches traced: 315 us -> 213 us
  Pallas kernels: 0 us -> 181 us
  waiting for transfers between devices: 110 us -> 0 us
  matrix products: 74 us -> 0 us
  starting transfers between devices: 48.9 us -> 0 us
  other arithmetic: 33.8 us -> 6.81 us
  local copies, waits for them, and re-layouts: 45.7 us -> 23.3 us
    pallas_call x0 -> x1, Pallas kernels: none -> 181 us  [build(): pl.pallas_call(run, out_shape=(shape((rows, own), LOW), shape((rows, own)...]
    ppermute x44 -> x0, waiting for transfers between devices: 110 us -> none  [swap(): return lax.ppermute(x, axis, [(i, i ^ bit) for i in range(n)])]
    dot_general x29 -> x0, matrix products: 57.8 us -> none  [the longest x23 38.3 us: dot(): return lax.dot_general(a, b, (dims, ((), ())), preferred_element_type=WIDE)]
    ppermute x44 -> x0, starting transfers between devices: 48.9 us -> none  [swap(): return lax.ppermute(x, axis, [(i, i ^ bit) for i in range(n)])]
    sub x2 -> x0, matrix products: 16.2 us -> none  [the longest x1 10.9 us: body(): ex = jnp.exp(sc - top)]
    select_n x21 -> x0, other arithmetic: 7.37 us -> none  [the longest x16 3.66 us: sum_batch(): jnp.where(mine, x, other)]
    add x17 -> x0, other arithmetic: 7.04 us -> none  [the longest x12 6.53 us: sum_batch(): x = keep + swap(send.astype(LOW), 'batch', bit).astype(WIDE)]
    convert_element_type x20 -> x1, local copies, waits for them, and re-layouts: 12.7 us -> 5.66 us  [body(): g_qkv.reshape(width, 3, local).astype(WIDE)]
  transfers between devices with their start and end apart: 44 -> 0, of which waited for: 21 -> 0; matrix products, arithmetic and copies ran while one was open for 37% -> 0% of each run, Pallas kernels for 0% -> 0%
where the time goes in v2:
time: 213 us
  Pallas kernels  181 us (85%)
  local copies, waits for them, and re-layouts  23.3 us (11%)
  other arithmetic  6.81 us (3%)
    pallas_call x1, Pallas kernels, build(): pl.pallas_call(run, out_shape=(shape((rows, own), LOW), shape((rows, own)...  181 us
    unnamed x27, local copies, waits for them, and re-layouts  9.63 us
    convert_element_type x1, local copies, waits for them, and re-layouts, body(): g_qkv.reshape(width, 3, local).astype(WIDE)  5.66 us

profile of v2, /device:TPU:0, one launch (start us, length us, event | category | flops | bytes accessed | tf_op | source)
XLA Modules:
  0.0 212.9 jit_solution(8489195331115676851)
XLA Ops:
  0.6 2.6 %copy.28 = bf16[768,3,384]{0,2,1:T(8,128)(2,1)S(1)} copy(bf16[768,3,384]{2,0,1:T(8,128)(2,1)} %param.15) | data formatting | bytes 3538944 | tf_op args[1]
  3.3 0.0 copy-start.5
  3.3 0.0 copy-start.10
  3.3 0.0 copy-start.6
  3.3 0.0 copy-start.7
  3.3 0.0 copy-start.8
  3.3 0.0 copy-start.9
  3.3 2.2 %copy.29.refs_1_ = bf16[768,1152]{1,0:T(8,128)(2,1)} copy(bf16[768,1152]{0,1:T(8,128)(2,1)S(1)} %bitcast.13) | data formatting | bytes 3538944 | tf_op jit(solution)/shard_map/reshape | solution.py:679
  5.6 0.0 copy-done.5
  5.6 0.6 reshape.58.refs_7_
  6.2 0.0 copy-done.10
  6.2 0.7 copy.30.refs_10_
  6.8 0.0 copy-done.6
  6.8 0.6 reshape.56.refs_5_
  7.4 0.0 copy-done.7
  7.4 0.6 reshape.57.refs_6_
  8.0 0.0 copy-done.8
  8.0 0.6 reshape.59.refs_8_
  8.6 0.0 copy-done.9
  8.6 0.6 reshape.60.refs_9_
  9.8 181.4 %layer.1 = (bf16[1024,384]{1,0:T(8,128)(2,1)}, bf16[1024,384]{1,0:T(8,128)(2,1)}, bf16[16,96,768]{2,1,0:T(8,128)(2,1)}, bf16[16,48,1536]{2,1,0:T(8,128)(2,1)}, b...) custom-call(bf16[1024,384]{1,0:T(8,128)(2,1)} %refs_0_.1, ...), custom_call_target="tpu_custom_call" | custom-call | tf_op jit(solution)/shard_map/layer/pallas_call | solution.py:657
  191.2 1.5 slice_reduce_fusion.1
  192.7 1.4 slice_reduce_fusion
  194.1 5.7 %reshape.62 = f32[768,3,384]{2,1,0:T(4,128)} reshape(bf16[16,48,1152]{2,1,0:T(8,128)(2,1)} %get-tuple-element.20) | data formatting | bytes 5308416 | tf_op jit(solution)/shard_map/convert_element_type | solution.py:682
  199.8 0.0 copy-start.1
  199.8 4.5 %copy.31 = f32[768,3,384]{2,0,1:T(8,128)} copy(f32[768,3,384]{2,1,0:T(4,128)} %reshape.62) | data formatting | bytes 7077888
  204.3 0.0 copy-done.1
  204.3 0.0 copy-start
  204.3 2.7 %bitcast_convert_fusion = f32[1536,768]{1,0:T(8,128)} fusion(bf16[16,96,768]{2,1,0:T(8,128)(2,1)S(1)} %copy-done.1), kind=kLoop, calls=%fused_computation | loop fusion | flops 1179648 | bytes 7077888 | tf_op jit(solution)/shard_map/convert_element_type | solution.py:684
  207.0 0.0 copy-done
  207.0 0.0 copy-start.4
  207.0 0.0 copy-start.3
  207.0 3.0 %bitcast_convert_fusion.1 = f32[768,1536]{1,0:T(8,128)} fusion(bf16[16,48,1536]{2,1,0:T(8,128)(2,1)S(1)} %copy-done), kind=kLoop, calls=%fused_computation.1 | loop fusion | flops 1179648 | bytes 7077888 | tf_op jit(solution)/shard_map/convert_element_type | solution.py:683
  210.0 0.0 copy-start.2
  210.0 0.0 copy-done.4
  210.0 1.1 bitcast_convert_fusion.2
  211.1 0.0 copy-done.3
  211.1 0.9 copy.35
  212.0 0.0 copy-done.2
  212.0 0.9 copy.36
Async XLA Ops:
  3.3 2.3 %copy-start.5 = (f32[1536]{0:T(1024)S(1)}, f32[1536]{0:T(1024)}, u32[]{:S(2)}) copy-start(f32[1536]{0:T(1024)} %param.20) | copy-start | bytes 18436
  3.3 2.9 %copy-start.10 = (s32[6,2]{0,1:T(2,128)S(1)}, s32[6,2]{0,1:T(2,128)}, u32[]{:S(2)}) copy-start(s32[6,2]{0,1:T(2,128)} %param.24) | copy-start | bytes 148
  3.3 3.5 %copy-start.6 = (f32[768]{0:T(1024)S(1)}, f32[768]{0:T(1024)}, u32[]{:S(2)}) copy-start(f32[768]{0:T(1024)} %param.17) | copy-start | bytes 9220
  3.3 4.1 %copy-start.7 = (f32[768]{0:T(1024)S(1)}, f32[768]{0:T(1024)}, u32[]{:S(2)}) copy-start(f32[768]{0:T(1024)} %param.18) | copy-start | bytes 9220
  3.3 4.7 %copy-start.8 = (f32[768]{0:T(1024)S(1)}, f32[768]{0:T(1024)}, u32[]{:S(2)}) copy-start(f32[768]{0:T(1024)} %param.22) | copy-start | bytes 9220
  3.3 5.3 %copy-start.9 = (f32[768]{0:T(1024)S(1)}, f32[768]{0:T(1024)}, u32[]{:S(2)}) copy-start(f32[768]{0:T(1024)} %param.23) | copy-start | bytes 9220
  199.8 4.5 %copy-start.1 = (bf16[16,96,768]{2,1,0:T(8,128)(2,1)S(1)}, bf16[16,96,768]{2,1,0:T(8,128)(2,1)}, u32[]{:S(2)}) copy-start(bf16[16,96,768]{2,1,0:T(8,128)(2,1)} %get-tuple-element.24) | copy-start | bytes 7077892
  204.3 2.7 %copy-start = (bf16[16,48,1536]{2,1,0:T(8,128)(2,1)S(1)}, bf16[16,48,1536]{2,1,0:T(8,128)(2,1)}, u32[]{:S(2)}) copy-start(bf16[16,48,1536]{2,1,0:T(8,128)(2,1)} %get-tuple-element.23) | copy-start | bytes 7077892
  207.0 3.0 %copy-start.4 = (bf16[16,24,768]{2,1,0:T(8,128)(2,1)S(1)}, bf16[16,24,768]{2,1,0:T(8,128)(2,1)}, u32[]{:S(2)}) copy-start(bf16[16,24,768]{2,1,0:T(8,128)(2,1)} %get-tuple-element.21) | copy-start | bytes 1769476
  207.0 4.1 %copy-start.3 = (bf16[1024,384]{1,0:T(8,128)(2,1)S(1)}, bf16[1024,384]{1,0:T(8,128)(2,1)}, u32[]{:S(2)}) copy-start(bf16[1024,384]{1,0:T(8,128)(2,1)} %get-tuple-element.62) | copy-start | bytes 2359300
  210.0 2.0 copy-start.2

commit v3 on v2

--- a/solution.py
+++ b/solution.py
@@ -151,10 +151,10 @@
 
 
 def kernel(n, refs):
-    (tokens, wqkv_hbm, wout_hbm, wup_hbm, wdown_hbm, gain_one, shift_one, b_up, gain_two, shift_two,
+    (tokens, wqkv_hbm, wout_hbm, wup_hbm, wdown_hbm, *vectors,
      perm, count, index, cot,
      result, grad_tokens, o_down, o_up, o_out, o_qkv, small_out,
-     wqkv, wout, wup, wdown, wsem,
+     wqkv, wout, wup, wdown, wsem, vecs,
      tok, qkv, sel_t, sel, blk, tokc, qc, probs, ctxc, normal_one, inverse_one, normed_one, low_one, slope,
      hidden, part, part_got, gb, gtwo, gin, back, back_got, gattn, gctx, dqc, dall, far, far_got, near,
      ctx, pre_two, down_far, down_got, stats, stats_got,
@@ -189,7 +189,8 @@
             device_id=x_peer, device_id_type=MESH)
 
     loads = [pltpu.make_async_copy(s, d, wsem.at[i]) for i, (s, d) in enumerate(
-        ((wqkv_hbm, wqkv), (wout_hbm, wout), (wup_hbm, wup), (wdown_hbm, wdown)))]
+        [(wqkv_hbm.at[j], wqkv.at[:, pl.ds(j * local, local)]) for j in range(3)]
+        + [(wout_hbm, wout), (wup_hbm, wup), (wdown_hbm, wdown)])]
     for cp in loads:
         cp.start()
     barrier = pltpu.get_barrier_semaphore()
@@ -211,6 +212,11 @@
         tok_copy(r).start()
     own_tok = pltpu.make_async_copy(tokens, tok.at[:, own_cols], lsem.at[0])
     own_tok.start()
+
+    for i, vector in enumerate(vectors):
+        vecs[i:i + 1, :vector.shape[0]] = vector[...].reshape(1, -1)
+    gain_one, shift_one, gain_two, shift_two = (vecs.at[i:i + 1, :width] for i in range(4))
+    b_up = vecs.at[4:5, :]
 
     lane_slot = lax.broadcasted_iota(jnp.int32, (1, slots), 1)
     idx = jnp.where(lane_slot < count[...], index[...], -1)
@@ -220,7 +226,8 @@
     sel[...] = picked.astype(LOW)
     blk[...] = jnp.broadcast_to(jnp.sum(picked[:, block_len:], axis=1, keepdims=True), blk.shape)
     own_tok.wait()
-    loads[0].wait()
+    for cp in loads[:3]:
+        cp.wait()
 
     def qkv_tile(r, c):
         tok_copy(r).wait_recv()
@@ -237,9 +244,15 @@
     def keep_head(x, e):
         return jnp.where(low_lane, x, 0.0).astype(LOW) if e == 0 else jnp.where(low_lane, 0.0, x).astype(LOW)
 
+    order = perm[...].astype(WIDE)
+    head_lane = lax.broadcasted_iota(jnp.int32, order.shape, 1)
+
+    def blocks_of(head):
+        return jnp.sum(jnp.where(head_lane == head, order, 0.0), axis=1, keepdims=True)
+
     def second(head):
-        pair = perm[pl.ds(head, 1), :].astype(WIDE)
-        return (pair[:, :1] + blk[:, :1] * (pair[:, 1:] - pair[:, :1])) > 0.5
+        pair = blocks_of(head)
+        return (pair[:1] + blk[:, :1] * (pair[1:] - pair[:1])) > 0.5
 
     def masked_attention(p, c):
         q2 = dot(sel[...], qkv[p]).astype(LOW)
@@ -270,9 +283,9 @@
         q_block = lax.rem(i, 2)
         q_rows = pl.ds(pl.multiple_of(q_block * block_len, block_len), block_len)
         q2 = qkv[p, q_rows, :].astype(WIDE)
-        even, odd = (perm[pl.ds(2 * p + e, 1), :].astype(WIDE) for e in range(2))
-        late = jnp.where(low_lane, jnp.where(q_block == 0, even[:, :1], even[:, 1:]),
-                         jnp.where(q_block == 0, odd[:, :1], odd[:, 1:])) > 0.5
+        even, odd = blocks_of(2 * p), blocks_of(2 * p + 1)
+        late = jnp.where(low_lane, jnp.where(q_block == 0, even[:1], even[1:]),
+                         jnp.where(q_block == 0, odd[:1], odd[1:])) > 0.5
 
         def chosen(j):
             return jnp.where(late, qkv[j, block_len:, :].astype(WIDE), qkv[j, :block_len, :].astype(WIDE)).astype(LOW)
@@ -292,7 +305,7 @@
     lax.fori_loop(0, cut, attend, 0)
 
     ctxc_copy.wait_recv()
-    for cp in loads[1:]:
+    for cp in loads[3:]:
         cp.wait()
     pre = tokc[...].astype(WIDE) + dot(cat([ctxc[j] for j in range(2 * pairs)]), wout[...])
     nrm_c, inv_c = normalize(pre)
@@ -305,7 +318,7 @@
 
     def up_tile(i, c):
         cols = pl.ds(pl.multiple_of(i * ff_tile, ff_tile), ff_tile)
-        u = dot(low_one[...], wup[:, cols]) + b_up[:, cols]
+        u = dot(low_one[...], wup[:, cols]) + vecs[4:5, cols]
         cdf = 0.5 * (1.0 + lax.erf(u * root_half))
         hidden[:, cols] = (u * cdf).astype(LOW)
         slope[:, cols] = cdf + u * inv_root_two_pi * jnp.exp(-0.5 * u * u)
@@ -557,8 +570,8 @@
         gap = 0.5 * (one[:, :1] - two[:, :1])
         var = 0.5 * (one[:, 1:2] + two[:, 1:2]) + gap * gap
         down_copy(r).wait_send()
-        down_far[rs, :] = ((x - mean) * lax.rsqrt(var + norm_eps) * gain_two[:, own_cols]
-                         + shift_two[:, own_cols]).astype(LOW)
+        down_far[rs, :] = ((x - mean) * lax.rsqrt(var + norm_eps) * vecs[2:3, own_cols]
+                         + vecs[3:4, own_cols]).astype(LOW)
         return c
 
     lax.fori_loop(0, tiles, result_tile, 0)
@@ -587,7 +600,7 @@
           count, cot):
     rows, own = tokens.shape
     width = wout.shape[0]
-    local = wqkv.shape[1] // 3
+    local = wqkv.shape[2]
     pairs = local // LANES
     heads = local // HEAD_DIM
     slots = index.shape[1]
@@ -621,7 +634,8 @@
 
     f = [vm((units,) + groups[g], LOW) for g in groups]
     scratch = [
-        vm(wqkv.shape, LOW), vm(wout.shape, LOW), vm(wup.shape, LOW), vm(wdown.shape, LOW), dma((4,)),
+        vm((width, 3 * local), LOW), vm(wout.shape, LOW), vm(wup.shape, LOW), vm(wdown.shape, LOW), dma((6,)),
+        vm((8, ff), WIDE),
         vm((rows, width), LOW), vm((3 * pairs, rows, LANES), LOW), vm((rows, slots), LOW), vm((slots, rows), LOW),
         vm((slots, LANES), WIDE), vm((slots, width), LOW), vm((pairs, slots, LANES), LOW),
         vm((heads, slots, block_len), WIDE), vm((2 * pairs, slots, LANES), LOW), vm((slots, width), WIDE),
@@ -664,24 +678,101 @@
         compiler_params=pltpu.CompilerParams(
             collective_id=0, has_side_effects=True, vmem_limit_bytes=VMEM_BYTES),
         name="layer",
-    )(tokens, wqkv, wout, wup, wdown, gain_one, shift_one, b_up, gain_two, shift_two, perm, count, index, cot)
+    )(tokens, wqkv, wout, wup, wdown, gain_one, shift_one, gain_two, shift_two, b_up, perm, count, index, cot)
+
+
+def finish(refs):
+    (f_down, f_up, f_out, f_qkv, small, res_in, tok_in,
+     down, up, out, qkv, gain_one, shift_one, bias, gain_two, shift_two, res, tok,
+     b_down, b_up, b_out, b_qkv, w_down, w_up, w_out, w_qkv, b_res, b_tok, isem, osem) = refs
+    width = gain_one.shape[0]
+    local = qkv.shape[2]
+    reads, writes = [], []
+
+    def read(src, dst):
+        cp = pltpu.make_async_copy(src, dst, isem.at[len(reads)])
+        cp.start()
+        reads.append(cp)
+        return cp
+
+    def write(src, dst):
+        cp = pltpu.make_async_copy(src, dst, osem.at[len(writes)])
+        cp.start()
+        writes.append(cp)
+
+    parts = 4
+    jobs = []
+    for src, low, wide, dst in ((f_down, b_down, w_down, down), (f_up, b_up, w_up, up),
+                                (f_out, b_out, w_out, out), (f_qkv, b_qkv, w_qkv, qkv)):
+        step = src.shape[0] // parts if src.shape[0] % parts == 0 else src.shape[0]
+        for u in range(0, src.shape[0], step):
+            jobs.append((read(src.at[pl.ds(u, step)], low.at[pl.ds(u, step)]), u, step, low, wide, dst))
+    pass_on = [(read(a, b), b, c) for a, b, c in ((res_in, b_res, res), (tok_in, b_tok, tok))]
+    gain_one[...] = small[1:2, :width].reshape(width)
+    shift_one[...] = small[1:2, width:].reshape(width)
+    gain_two[...] = small[2:3, :width].reshape(width)
+    shift_two[...] = small[2:3, width:].reshape(width)
+    bias[...] = small[0:1, :].reshape(bias.shape[0])
+    for cp, u, step, low, wide, dst in jobs:
+        cp.wait()
+        r = low.shape[1]
+
+        def unit(j, c, u=u, low=low, wide=wide, r=r, dst=dst):
+            v = low[u + j].astype(WIDE)
+            rows = pl.ds(pl.multiple_of((u + j) * r, r), r)
+            if dst is qkv:
+                for k in range(3):
+                    wide[k, rows, :] = v[:, k * local:(k + 1) * local]
+            else:
+                wide[rows, :] = v
+            return c
+
+        lax.fori_loop(0, step, unit, 0)
+        rows = pl.ds(u * r, step * r)
+        if dst is qkv:
+            write(wide.at[:, rows, :], dst.at[:, rows, :])
+        else:
+            write(wide.at[rows, :], dst.at[rows, :])
+    for cp, src, dst in pass_on:
+        cp.wait()
+        write(src, dst)
+    for cp in writes:
+        cp.wait()
+
+
+def widen(g_down, g_up, g_out, g_qkv, small, result, grad_tokens):
+    units, r_qkv, three = g_qkv.shape
+    local, width, ff = three // 3, g_down.shape[2], g_up.shape[2]
+    shape = jax.ShapeDtypeStruct
+    hbm = pl.BlockSpec(memory_space=pl.ANY)
+    v = pl.BlockSpec(memory_space=pltpu.VMEM)
+    wide = [(ff, width), (width, ff), (local, width), (3, width, local)]
+    low = [g.shape for g in (g_down, g_up, g_out, g_qkv)]
+    acts = [result.shape, grad_tokens.shape]
+    return pl.pallas_call(
+        lambda *refs: finish(refs),
+        out_shape=(*(shape(x, WIDE) for x in wide), shape((width,), WIDE), shape((width,), WIDE),
+                   shape((ff,), WIDE), shape((width,), WIDE), shape((width,), WIDE),
+                   *(shape(x, LOW) for x in acts)),
+        in_specs=[hbm, hbm, hbm, hbm, v, hbm, hbm],
+        out_specs=(hbm, hbm, hbm, hbm, v, v, v, v, v, hbm, hbm),
+        scratch_shapes=[*(pltpu.VMEM(x, LOW) for x in low), *(pltpu.VMEM(x, WIDE) for x in wide),
+                        *(pltpu.VMEM(x, LOW) for x in acts), pltpu.SemaphoreType.DMA((18,)),
+                        pltpu.SemaphoreType.DMA((18,))],
+        compiler_params=pltpu.CompilerParams(vmem_limit_bytes=VMEM_BYTES * 3 // 4),
+        name="widen",
+    )(g_down, g_up, g_out, g_qkv, small, result, grad_tokens)
 
 
 def body(n, tokens, w_qkv, w_out, gain_one, attention_norm_bias, w_up, b_up, w_down, gain_two, shift_two,
          block_perm, mask_index, mask_count, cotangent):
-    width = w_out.shape[0]
-    local = w_qkv.shape[2]
-
-    def row(x):
-        return x.reshape(1, -1)
-
     result, grad_tokens, g_down, g_up, g_out, g_qkv, small = build(
-        n, tokens, w_qkv.reshape(width, 3 * local), w_out, row(gain_one), row(attention_norm_bias), w_up,
-        row(b_up), w_down, row(gain_two), row(shift_two), block_perm, mask_index, mask_count.reshape(1, 1), cotangent[0])
-    return (
-        result, grad_tokens, g_qkv.reshape(width, 3, local).astype(WIDE), g_out.reshape(local, width).astype(WIDE),
-        small[1, :width], small[1, width:], g_up.reshape(w_up.shape).astype(WIDE), small[0],
-        g_down.reshape(w_down.shape).astype(WIDE), small[2, :width], small[2, width:])
+        n, tokens, w_qkv.transpose(1, 0, 2), w_out, gain_one, attention_norm_bias, w_up, b_up, w_down, gain_two,
+        shift_two, block_perm.T, mask_index, mask_count.reshape(1, 1), cotangent[0])
+    (g_down, g_up, g_out, g_qkv, g_gain_one, g_shift_one, g_bias, g_gain_two, g_shift_two, result,
+     grad_tokens) = widen(g_down, g_up, g_out, g_qkv, small, result, grad_tokens)
+    return (result, grad_tokens, g_qkv.transpose(1, 0, 2), g_out, g_gain_one, g_shift_one, g_up, g_bias, g_down,
+            g_gain_two, g_shift_two)
 
 
 def solution(mesh):

time: 213 us -> 198 us (0.930)
  local copies, waits for them, and re-layouts: 23.3 us -> 5.6 us
  Pallas kernels: 181 us -> 190 us
  other arithmetic: 6.81 us -> 0 us
    pallas_call x0 -> x1, Pallas kernels: none -> 8.39 us  [widen(): pl.pallas_call(lambda *refs: finish(refs), out_shape=(*(shape(x, WIDE) fo...]
    convert_element_type x3 -> x0, other arithmetic: 6.81 us -> none  [the longest x1 2.98 us: body(): g_up.reshape(w_up.shape).astype(WIDE)]
    convert_element_type x1 -> x0, local copies, waits for them, and re-layouts: 5.66 us -> none  [body(): g_qkv.reshape(width, 3, local).astype(WIDE)]
    reshape x6 -> x0, local copies, waits for them, and re-layouts: 5.13 us -> none  [the longest x5 2.92 us: row(): return x.reshape(1, -1)]
    unnamed x27 -> x10, local copies, waits for them, and re-layouts: 9.63 us -> 5.6 us
    slice x2 -> x0, local copies, waits for them, and re-layouts: 2.87 us -> none  [the longest x1 1.46 us: body(): small[2, width:]]
where the time goes in v3:
time: 198 us; the launch traced here: 197 us
  Pallas kernels  190 us (96%)
  local copies, waits for them, and re-layouts  5.6 us (3%)
    pallas_call x1, Pallas kernels, build(): pl.pallas_call(run, out_shape=(shape((rows, own), LOW), shape((rows, own)...  182 us
    pallas_call x1, Pallas kernels, widen(): pl.pallas_call(lambda *refs: finish(refs), out_shape=(*(shape(x, WIDE) fo...  8.39 us
    unnamed x10, local copies, waits for them, and re-layouts  5.6 us

profile of v3, /device:TPU:0, one launch (start us, length us, event | category | flops | bytes accessed | tf_op | source)
XLA Modules:
  0.0 197.2 jit_solution(7065156744662568792)
XLA Ops:
  1.3 181.8 %layer.1 = (bf16[1024,384]{1,0:T(8,128)(2,1)}, bf16[1024,384]{1,0:T(8,128)(2,1)}, bf16[16,96,768]{2,1,0:T(8,128)(2,1)}, bf16[16,48,1536]{2,1,0:T(8,128)(2,1)}, b...) custom-call(bf16[1024,384]{1,0:T(8,128)(2,1)} %refs_0_.1, ...), custom_call_target="tpu_custom_call" | custom-call | tf_op jit(solution)/shard_map/layer/pallas_call | solution.py:671
  183.1 0.0 copy-start
  183.1 1.5 copy-done
  184.5 0.0 copy-start.1
  184.6 1.1 copy-done.1
  185.7 0.0 copy-start.2
  185.7 1.1 copy-done.2
  186.8 0.0 copy-start.3
  186.8 1.1 copy-done.3
  187.9 0.0 copy-start.4
  187.9 0.8 copy-done.4
  188.7 8.4 %widen.1 = (f32[1536,768]{1,0:T(8,128)}, f32[768,1536]{1,0:T(8,128)}, f32[384,768]{1,0:T(8,128)}, f32[3,768,384]{2,1,0:T(8,128)}, f32[768]{0:T(1024)}, /*index=5...) custom-call(bf16[16,96,768]{2,1,0:T(8,128)(2,1)} %get-tuple-element., ...), custom_call_target="tpu_custom_call" | custom-call | tf_op jit(solution)/shard_map/widen/pallas_call | solution.py:752
Async XLA Ops:
  183.1 1.5 copy-start
  184.5 1.1 copy-start.1
  185.7 1.1 copy-start.2
  186.8 1.1 copy-start.3
  187.9 0.8 copy-start.4

commit v4 on v3

--- a/solution.py
+++ b/solution.py
@@ -17,6 +17,23 @@
 LANES = 128
 MESH = pl.DeviceIdType.MESH
 VMEM_BYTES = 67043328
+CUTS = (2, 4)
+CHUNKS = {"D": 2, "U": 2, "O": 1, "Q": 2}
+ORDERS = {"D": [[0, 1, 2, 3], [0, 1, 2, 3]], "U": [[0, 2, 1, 3], [0, 1, 2, 3]],
+          "O": [[0, 1, 2, 3]], "Q": [[0, 1, 2, 3], [0, 2, 1, 3]]}
+PLAN = (
+    ("D0", 0), ("D1", 0), ("U0", 0), ("attend",), ("U1", 0), ("layer", 0), ("layer", 1), ("D0", 1), ("U0", 1),
+    ("norm",), ("mb", 0), ("D1", 1), ("mb", 1), ("D0", 2), ("small", 0), ("mb", 2), ("out",), ("U1", 1),
+    ("D1", 2), ("qkv", 0), ("O0", 0), ("small", 1), ("qkv", 1), ("U0", 2), ("D0", 3), ("Q0", 0), ("U1", 2),
+    ("far", 0), ("Q1", 0), ("D1", 3), ("small", 2), ("far", 1), ("O0", 1), ("far", 2), ("far", 3), ("layer", 2),
+    ("U0", 3), ("Q0", 1), ("Q1", 1), ("D0", 4), ("small", 3), ("layer", 3), ("O0", 2), ("U1", 3), ("Q0", 2),
+    ("Q1", 2), ("near", 0), ("near", 1), ("D1", 4), ("near", 2), ("D0", 5), ("near", 3), ("grad", 0),
+    ("grad", 1), ("grad", 2), ("U0", 4), ("stat", 0), ("stat", 1), ("O0", 3), ("grad", 3), ("gout",), ("D1", 5),
+    ("U1", 4), ("stat", 2), ("D0", 6), ("Q0", 3), ("D0", 7), ("Q1", 3), ("U1", 5), ("U0", 5), ("stat", 3),
+    ("O0", 4), ("stats",), ("Q0", 4), ("result",), ("Q1", 4), ("D1", 6), ("U0", 6), ("D1", 7), ("O0", 5),
+    ("U0", 7), ("Q0", 5), ("U1", 6), ("Q1", 5), ("U1", 7), ("O0", 6), ("O0", 7), ("Q1", 6), ("Q0", 6),
+    ("Q1", 7), ("Q0", 7),
+)
 
 
 def dot(a, b):
@@ -144,6 +161,13 @@
         if k >= 0:
             self._ag(k).start()
 
+    def advance(self, stage):
+        depth = len(self.order)
+        if stage < depth:
+            self.reduce(stage)
+        else:
+            self.gather(2 * depth - 2 - stage)
+
     def finish(self):
         for k in range(len(self.order)):
             self._rs(k).wait_send()
@@ -159,7 +183,7 @@
      hidden, part, part_got, gb, gtwo, gin, back, back_got, gattn, gctx, dqc, dall, far, far_got, near,
      ctx, pre_two, down_far, down_got, stats, stats_got,
      f_down, f_up, f_out, f_qkv, small, small_got,
-     xs_send, xs_recv, lsem, ring_refs) = refs
+     xs_send, xs_recv, lsem, rings) = refs
     rows, own = tokens.shape
     width = wout.shape[0]
     local = wqkv.shape[1] // 3
@@ -271,16 +295,18 @@
             halves.append(jnp.where(late, dot(pr, qkv[2 * pairs + p, block_len:, :]),
                                     dot(pr, qkv[2 * pairs + p, :block_len, :])))
         ctxc[h * pairs + p] = jnp.where(low_lane, halves[0], halves[1]).astype(LOW)
-        return c
+        ctxc_copy(p).start()
+        return c
+
+    def ctxc_copy(p):
+        mine_c = ctxc.at[pl.ds(h * pairs + p, 1)]
+        return x_copy(mine_c, mine_c, tiles + p)
 
     lax.fori_loop(0, pairs, masked_attention, 0)
-    mine_c = ctxc.at[pl.ds(h * pairs, pairs)]
-    ctxc_copy = x_copy(mine_c, mine_c, 4)
-    ctxc_copy.start()
 
     def attend(i, c):
-        p = lax.div(i, 2)
-        q_block = lax.rem(i, 2)
+        p = lax.rem(i, pairs)
+        q_block = lax.div(i, pairs)
         q_rows = pl.ds(pl.multiple_of(q_block * block_len, block_len), block_len)
         q2 = qkv[p, q_rows, :].astype(WIDE)
         even, odd = blocks_of(2 * p), blocks_of(2 * p + 1)
@@ -298,13 +324,22 @@
             inv = 1.0 / jnp.sum(ex, axis=-1, keepdims=True)
             halves.append(dot(ex.astype(LOW), v2) * inv)
         ctx[h * pairs + p, q_rows, :] = jnp.where(low_lane, halves[0], halves[1]).astype(LOW)
-        return c
+        ctx_copy(i).start()
+        return c
+
+    x_base = tiles + pairs
+
+    def ctx_copy(i):
+        q_rows = pl.ds(pl.multiple_of(lax.div(i, pairs) * block_len, block_len), block_len)
+        part_ref = ctx.at[pl.ds(h * pairs + lax.rem(i, pairs), 1), q_rows]
+        return x_copy(part_ref, part_ref, x_base + i)
 
     attend_units = 2 * pairs
-    cut = attend_units // 3
-    lax.fori_loop(0, cut, attend, 0)
-
-    ctxc_copy.wait_recv()
+    x_base2 = x_base + attend_units
+    lax.fori_loop(0, CUTS[0], attend, 0)
+
+    for p in range(pairs):
+        ctxc_copy(p).wait_recv()
     for cp in loads[3:]:
         cp.wait()
     pre = tokc[...].astype(WIDE) + dot(cat([ctxc[j] for j in range(2 * pairs)]), wout[...])
@@ -326,9 +361,9 @@
 
     lax.fori_loop(0, ff // ff_tile, up_tile, 0)
     part[...] = dot(hidden[...], wdown[...]).astype(LOW)
-    part_copy = x_copy(part, part_got, 5)
+    part_copy = x_copy(part, part_got, x_base2)
     part_copy.start()
-    lax.fori_loop(cut, attend_units, attend, 0)
+    lax.fori_loop(CUTS[0], CUTS[1], attend, 0)
     part_copy.wait_recv()
 
     normal_two, inv_two = normalize(normed_one[...] + (part[...].astype(WIDE) + part_got[...].astype(WIDE)))
@@ -339,6 +374,23 @@
     gb[...] = g2.astype(LOW)
     small[2:3, :] = cat([col_sum(up * normal_two), col_sum(up)])
 
+    def put(first, unit, value):
+        r = first.shape[1]
+        for j in range(value.shape[0] // r):
+            first[unit + j] = value[j * r:(j + 1) * r, :]
+
+    ring = {name: Ring(peer=peer, bit_of=bit_of, **r) for name, r in rings.items()}
+
+    def down_tile(i, c):
+        cols = pl.ds(pl.multiple_of(i * ff_tile, ff_tile), ff_tile)
+        put(f_down, i * (ff_tile * f_down.shape[0] // ff), dot_tn(hidden[:, cols], gb[...]).astype(LOW))
+        return c
+
+    def up_grad_tile(i, c):
+        cols = pl.ds(pl.multiple_of(i * ff_tile, ff_tile), ff_tile)
+        put(f_up, i * (ff_tile * f_up.shape[0] // width), dot_tn(low_one[:, cols], gin[...]).astype(LOW))
+        return c
+
     def in_tile(i, c):
         cols = pl.ds(pl.multiple_of(i * ff_tile, ff_tile), ff_tile)
         g = (dot_nt(gb[...], wdown[cols, :]) * slope[:, cols]).astype(LOW)
@@ -346,50 +398,34 @@
         small[0:1, cols] = col_sum(g.astype(WIDE))
         return c
 
+    back_copy = x_copy(back, back_got, x_base2 + 1)
+    for k in range(2):
+        lax.fori_loop(k * ff // (2 * ff_tile), (k + 1) * ff // (2 * ff_tile), down_tile, 0)
+        ring["D%d" % k].start()
     lax.fori_loop(0, ff // ff_tile, in_tile, 0)
     back[...] = dot_nt(gin[...], wup[...]).astype(LOW)
-    back_copy = x_copy(back, back_got, 6)
     back_copy.start()
-
-    rings = ring_refs
-    ring_down, ring_up, ring_out, ring_qkv = (
-        Ring(peer=peer, bit_of=bit_of, **r) for r in rings)
-
-    def put(first, unit, value):
-        r = first.shape[1]
-        for j in range(value.shape[0] // r):
-            first[unit + j] = value[j * r:(j + 1) * r, :]
-
-    units = f_down.shape[0]
-
-    def down_tile(i, c):
-        cols = pl.ds(pl.multiple_of(i * ff_tile, ff_tile), ff_tile)
-        put(f_down, i * (ff_tile * units // ff), dot_tn(hidden[:, cols], gb[...]).astype(LOW))
-        return c
-
-    lax.fori_loop(0, ff // ff_tile, down_tile, 0)
-    ring_down.start()
-
-    def up_grad_tile(i, c):
-        cols = pl.ds(pl.multiple_of(i * ff_tile, ff_tile), ff_tile)
-        put(f_up, i * (ff_tile * units // width), dot_tn(low_one[:, cols], gin[...]).astype(LOW))
-        return c
-
-    lax.fori_loop(0, width // ff_tile, up_grad_tile, 0)
-    ring_up.start()
-    ring_down.reduce(0)
-    ring_up.reduce(0)
-    back_copy.wait_recv()
-
-    gn = gtwo[...] + (back[...].astype(WIDE) + back_got[...].astype(WIDE))
-    small[1:2, :] = cat([col_sum(gn * normal_one[...]), col_sum(gn)])
-    g1 = norm_backward(gn, normal_one[...], inverse_one[:, :1], gain_one[...])
-    gtwo[...] = g1
-    gattn[...] = g1.astype(LOW)
+    for k in range(2):
+        lax.fori_loop(k * width // (2 * ff_tile), (k + 1) * width // (2 * ff_tile), up_grad_tile, 0)
+        ring["U%d" % k].start()
+
+    def attend_more():
+        lax.fori_loop(CUTS[1], attend_units, attend, 0)
+
     own_rows = pl.ds(pl.multiple_of(h * local, LANES), local)
-    gc = dot_nt(gattn[...], wout[own_rows, :]).astype(LOW)
-    for p in range(pairs):
-        gctx[p] = gc[:, p * LANES:(p + 1) * LANES]
+
+    def first_norm():
+        back_copy.wait_recv()
+        gn = gtwo[...] + (back[...].astype(WIDE) + back_got[...].astype(WIDE))
+        small[1:2, :] = cat([col_sum(gn * normal_one[...]), col_sum(gn)])
+        g1 = norm_backward(gn, normal_one[...], inverse_one[:, :1], gain_one[...])
+        gtwo[...] = g1
+        gattn[...] = g1.astype(LOW)
+        gc = dot_nt(gattn[...], wout[own_rows, :]).astype(LOW)
+        for p in range(pairs):
+            gctx[p] = gc[:, p * LANES:(p + 1) * LANES]
+        small[3:8, :] = jnp.zeros((5, small.shape[1]), WIDE)
+        small_copy(0).start()
 
     def masked_backward(p, c):
         q2 = qc[p].astype(WIDE)
@@ -425,14 +461,10 @@
         dall[2 * pairs + p, block_len:, :] = dv[:, LANES:]
         return c
 
-    lax.fori_loop(0, pairs, masked_backward, 0)
-
-    small[3:8, :] = jnp.zeros((5, small.shape[1]), WIDE)
-
     def small_copy(k):
         return pltpu.make_async_remote_copy(
             src_ref=small.at[pl.ds(8 * k, 8)], dst_ref=small_got.at[pl.ds(8 * k, 8)],
-            send_sem=xs_send.at[18 + k], recv_sem=xs_recv.at[18 + k],
+            send_sem=xs_send.at[x_slots + k], recv_sem=xs_recv.at[x_slots + k],
             device_id=peer(bits[k]), device_id_type=MESH)
 
     def small_step(k):
@@ -444,63 +476,52 @@
         else:
             small_out[...] = total
 
-    small_copy(0).start()
-
-    put(f_out, 0, dot_tn(cat([ctxc[h * pairs + p] for p in range(pairs)]), gattn[...]).astype(LOW))
-    ring_out.start()
+    def out_grad():
+        put(f_out, 0, dot_tn(cat([ctxc[h * pairs + p] for p in range(pairs)]), gattn[...]).astype(LOW))
+        ring["O0"].start()
 
     def qkv_grad_tile(i, c):
         cols = pl.ds(pl.multiple_of(i * ff_tile, ff_tile), ff_tile)
         gq = dot_tn(tokc[:, cols], cat([dqc[p] for p in range(pairs)]))
         gkv = dot_tn(tok[:, cols], cat([dall[pairs + j] for j in range(2 * pairs)]))
-        put(f_qkv, i * (ff_tile * units // width), cat([gq, gkv]).astype(LOW))
-        return c
-
-    lax.fori_loop(0, width // ff_tile, qkv_grad_tile, 0)
-    ring_qkv.start()
-    small_step(0)
+        put(f_qkv, i * (ff_tile * f_qkv.shape[0] // width), cat([gq, gkv]).astype(LOW))
+        return c
+
+    def qkv_grad(k):
+        lax.fori_loop(k * width // (2 * ff_tile), (k + 1) * width // (2 * ff_tile), qkv_grad_tile, 0)
+        ring["Q%d" % k].start()
 
     def far_copy(r):
-        return x_copy(far.at[row_tile(r)], far_got.at[row_tile(r)], 7 + r)
-
-    def far_tile(r, c):
+        return x_copy(far.at[row_tile(r)], far_got.at[row_tile(r)], x_base2 + 2 + r)
+
+    def far_tile(r):
         d = cat([dall[j, row_tile(r), :] for j in range(3 * pairs)])
         far[row_tile(r), :] = dot_nt(d, wqkv[far_cols, :]).astype(LOW)
         far_copy(r).start()
-        return c
-
-    def ctx_copy():
-        part_ref = ctx.at[pl.ds(h * pairs, pairs)]
-        return x_copy(part_ref, part_ref, 11)
-
-    ctx_copy().start()
-    lax.fori_loop(0, tiles, far_tile, 0)
-    ring_out.reduce(0)
-    ring_qkv.reduce(0)
-    ring_down.reduce(1)
-    ring_up.reduce(1)
-    for k in range(1, len(bits)):
-        small_step(k)
-    mine = gtwo[:, own_cols]
-    high = mine.astype(LOW)
-    rest = (mine - high.astype(WIDE)).astype(LOW)
-    halves = cat([high, rest])
-
-    def near_tile(r, c):
+
+    def near_tile(r):
+        mine = gtwo[:, own_cols]
+        high = mine.astype(LOW)
+        rest = (mine - high.astype(WIDE)).astype(LOW)
         d = cat([dall[j, row_tile(r), :] for j in range(3 * pairs)])
-        spread = dot(sel_t[row_tile(r), :], halves)
+        spread = dot(sel_t[row_tile(r), :], cat([high, rest]))
         near[row_tile(r), :] = dot_nt(d, wqkv[own_cols, :]) + (spread[:, :own] + spread[:, own:])
-        return c
-
-    lax.fori_loop(0, tiles, near_tile, 0)
-    ring_down.reduce(2)
-    ring_up.reduce(2)
-    ctx_copy().wait_recv()
+
+    def grad_tile(r):
+        far_copy(r).wait_recv()
+        far_copy(r).wait_send()
+        far[row_tile(r), :] = (near[row_tile(r), :] + far_got[row_tile(r), :].astype(WIDE)).astype(LOW)
+
+    grad_out = pltpu.make_async_copy(far, grad_tokens, lsem.at[1])
 
     def down_copy(r):
-        return x_copy(down_far.at[row_tile(r)], down_got.at[row_tile(r)], 12 + r)
-
-    def layer_tile(r, c):
+        return x_copy(down_far.at[row_tile(r)], down_got.at[row_tile(r)], x_base2 + 2 + tiles + r)
+
+    def layer_tile(r):
+        if r * tile % block_len == 0:
+            block = r * tile // block_len
+            for i in range(block * pairs, (block + 1) * pairs):
+                ctx_copy(i).wait_recv()
         rs = row_tile(r)
         pre_r = tok[rs, :].astype(WIDE) + dot(cat([ctx[j, rs, :] for j in range(2 * pairs)]), wout[...])
         normed = normalize(pre_r)[0] * gain_one[...] + shift_one[...]
@@ -510,36 +531,11 @@
         down_far[rs, :] = dot(hid, wdown[:, far_cols]).astype(LOW)
         down_copy(r).start()
         pre_two[rs, :] = normed_one[:, own_cols] + dot(hid, wdown[:, own_cols])
-        return c
-
-    lax.fori_loop(0, tiles // 2, layer_tile, 0)
-    ring_out.reduce(1)
-    ring_qkv.reduce(1)
-    ring_down.reduce(3)
-    ring_up.reduce(3)
-    lax.fori_loop(tiles // 2, tiles, layer_tile, 0)
-    ring_out.reduce(2)
-    ring_qkv.reduce(2)
-    ring_down.gather(2)
-    ring_up.gather(2)
-
-    def grad_tile(r, c):
-        far_copy(r).wait_recv()
-        far_copy(r).wait_send()
-        far[row_tile(r), :] = (near[row_tile(r), :] + far_got[row_tile(r), :].astype(WIDE)).astype(LOW)
-        return c
-
-    lax.fori_loop(0, tiles, grad_tile, 0)
-    grad_out = pltpu.make_async_copy(far, grad_tokens, lsem.at[1])
-    grad_out.start()
-    ring_out.reduce(3)
-    ring_qkv.reduce(3)
-    ring_down.gather(1)
-    ring_up.gather(1)
 
     first_lane = lax.broadcasted_iota(jnp.int32, (1, LANES), 1) < 1
-
-    def stat_tile(r, c):
+    stats_copy = x_copy(stats, stats_got, x_base2 + 2 + 2 * tiles)
+
+    def stat_tile(r):
         rs = row_tile(r)
         down_copy(r).wait_recv()
         x = pre_two[rs, :] + down_got[rs, :].astype(WIDE)
@@ -549,16 +545,6 @@
         var = jnp.mean(dev * dev, axis=-1, keepdims=True)
         both = jnp.where(first_lane, mean, var)
         stats[r] = jnp.transpose(both)[:8, :]
-        return c
-
-    lax.fori_loop(0, tiles, stat_tile, 0)
-    stats_copy = x_copy(stats, stats_got, 16)
-    stats_copy.start()
-    ring_out.gather(2)
-    ring_qkv.gather(2)
-    ring_down.gather(0)
-    ring_up.gather(0)
-    stats_copy.wait_recv()
 
     def result_tile(r, c):
         rs = row_tile(r)
@@ -574,26 +560,40 @@
                          + vecs[3:4, own_cols]).astype(LOW)
         return c
 
-    lax.fori_loop(0, tiles, result_tile, 0)
     result_out = pltpu.make_async_copy(down_far, result, lsem.at[2])
-    result_out.start()
-    ring_out.gather(1)
-    ring_qkv.gather(1)
-    ring_out.gather(0)
-    ring_qkv.gather(0)
-    for ring in (ring_down, ring_up, ring_out, ring_qkv):
-        ring.gather(-1)
+
+    def write_result():
+        stats_copy.wait_recv()
+        lax.fori_loop(0, tiles, result_tile, 0)
+        result_out.start()
+
+    x_slots = x_base2 + 3 + 2 * tiles
+    steps = {"norm": first_norm, "attend": attend_more, "mb": lambda p: masked_backward(p, 0), "out": out_grad,
+             "qkv": qkv_grad, "far": far_tile, "near": near_tile, "grad": grad_tile, "layer": layer_tile,
+             "stat": stat_tile, "stats": stats_copy.start, "gout": grad_out.start, "result": write_result,
+             "small": small_step}
+    for name, *at in PLAN:
+        if name in ring:
+            ring[name].advance(at[0])
+        else:
+            steps[name](*at)
+    for k in range(min(len(bits), 4), len(bits)):
+        small_step(k)
 
     for r in range(tiles):
         tok_copy(r).wait_send()
     grad_out.wait()
     result_out.wait()
-    for cp in (ctxc_copy, part_copy, back_copy, ctx_copy(), stats_copy):
+    for i in range(attend_units):
+        ctx_copy(i).wait_send()
+    for p in range(pairs):
+        ctxc_copy(p).wait_send()
+    for cp in (part_copy, back_copy, stats_copy):
         cp.wait_send()
     for k in range(len(bits)):
         small_copy(k).wait_send()
-    for ring in (ring_down, ring_up, ring_out, ring_qkv):
-        ring.finish()
+    for one in ring.values():
+        one.finish()
 
 
 def build(n, tokens, wqkv, wout, gain_one, shift_one, wup, b_up, wdown, gain_two, shift_two, perm, index,
@@ -614,13 +614,13 @@
     halving, extra = bits[:depth], bits[depth:]
 
     vm = pltpu.VMEM
-    groups = {"down": (ff // units, width), "up": (width // units, ff), "out": (local // units, width),
-              "qkv": (width // units, 3 * local)}
-    orders = {g: halving for g in groups}
+    groups = {"D": (ff, width), "U": (width, ff), "O": (local, width), "Q": (width, 3 * local)}
+    shapes = {g: (CHUNKS[g] * units, r // (CHUNKS[g] * units), c) for g, (r, c) in groups.items()}
+    names = [(g, k) for g in groups for k in range(CHUNKS[g])]
     dma = pltpu.SemaphoreType.DMA
 
     def ring_scratch(g):
-        r, c = groups[g]
+        _, r, c = shapes[g]
         sizes = [units >> (k + 1) for k in range(depth)]
         return {
             "recv": [vm((s, r, c), LOW) for s in sizes],
@@ -632,7 +632,8 @@
             "sems": (dma((2 * depth + len(extra),)), dma((2 * depth + len(extra),)), dma(())),
         }
 
-    f = [vm((units,) + groups[g], LOW) for g in groups]
+    f = [vm(shapes[g], LOW) for g in groups]
+    x_slots = 3 * (rows // tile) + 3 * pairs + 3
     scratch = [
         vm((width, 3 * local), LOW), vm(wout.shape, LOW), vm(wup.shape, LOW), vm(wdown.shape, LOW), dma((6,)),
         vm((8, ff), WIDE),
@@ -648,10 +649,10 @@
         vm((2 * pairs, rows, LANES), LOW), vm((rows, own), WIDE), vm((rows, own), LOW),
         vm((rows, own), LOW), vm((rows // tile, 8, tile), WIDE), vm((rows // tile, 8, tile), WIDE),
         *f, vm((8 * steps, ff), WIDE), vm((8 * steps, ff), WIDE),
-        dma((18 + steps,)), dma((18 + steps,)), dma((3,)),
+        dma((x_slots + steps,)), dma((x_slots + steps,)), dma((3,)),
     ]
     plain = len(scratch)
-    ring_specs = [ring_scratch(g) for g in groups]
+    ring_specs = [ring_scratch(g) for g, _ in names]
     flat, tree = jax.tree.flatten(ring_specs, is_leaf=lambda x: not isinstance(x, (dict, list, tuple)))
     n_in, n_out = 14, 7
 
@@ -660,9 +661,12 @@
         rings = jax.tree.unflatten(tree, refs[n_in + n_out + plain:])
         firsts = head_refs[-(len(groups) + 5):-5]
         outs = refs[n_in + 2:n_in + 2 + len(groups)]
-        full = []
-        for g, ring, first, out in zip(groups, rings, firsts, outs):
-            full.append(dict(order=orders[g], extra=extra, first=first, out=out, **ring))
+        full = {}
+        for (g, k), ring in zip(names, rings):
+            i = list(groups).index(g)
+            part = pl.ds(k * units, units)
+            full["%s%d" % (g, k)] = dict(order=[halving[j] for j in ORDERS[g][k] if j < depth], extra=extra,
+                                         first=firsts[i].at[part], out=outs[i].at[part], **ring)
         kernel(n, (*head_refs, full))
 
     hbm = pl.BlockSpec(memory_space=pl.ANY)
@@ -671,7 +675,7 @@
     return pl.pallas_call(
         run,
         out_shape=(shape((rows, own), LOW), shape((rows, own), LOW),
-                   *(shape((units,) + groups[g], LOW) for g in groups), shape((8, ff), WIDE)),
+                   *(shape(shapes[g], LOW) for g in groups), shape((8, ff), WIDE)),
         in_specs=[hbm, hbm, hbm, hbm, hbm, v, v, v, v, v, v, v, v, v],
         out_specs=(hbm, hbm, hbm, hbm, hbm, hbm, v),
         scratch_shapes=scratch + flat,
@@ -759,7 +763,7 @@
         scratch_shapes=[*(pltpu.VMEM(x, LOW) for x in low), *(pltpu.VMEM(x, WIDE) for x in wide),
                         *(pltpu.VMEM(x, LOW) for x in acts), pltpu.SemaphoreType.DMA((18,)),
                         pltpu.SemaphoreType.DMA((18,))],
-        compiler_params=pltpu.CompilerParams(vmem_limit_bytes=VMEM_BYTES * 3 // 4),
+        compiler_params=pltpu.CompilerParams(vmem_limit_bytes=VMEM_BYTES),
         name="widen",
     )(g_down, g_up, g_out, g_qkv, small, result, grad_tokens)
 

time: 198 us -> 157 us (0.79)
  Pallas kernels: 190 us -> 155 us
  local copies, waits for them, and re-layouts: 5.6 us -> 0 us
    pallas_call x1, Pallas kernels: 182 us -> 145 us  [build(): pl.pallas_call(run, out_shape=(shape((rows, own), LOW), shape((rows, own)...]
    unnamed x10 -> x0, local copies, waits for them, and re-layouts: 5.6 us -> none
where the time goes in v4:
time: 157 us; the launch traced here: 156 us
  Pallas kernels  155 us (99%)
    pallas_call x1, Pallas kernels, build(): pl.pallas_call(run, out_shape=(shape((rows, own), LOW), shape((rows, own)...  145 us
    pallas_call x1, Pallas kernels, widen(): pl.pallas_call(lambda *refs: finish(refs), out_shape=(*(shape(x, WIDE) fo...  9.45 us

profile of v4, /device:TPU:0, one launch (start us, length us, event | category | flops | bytes accessed | tf_op | source)
XLA Modules:
  0.0 156.2 jit_solution(11922145570900091449)
XLA Ops:
  1.3 145.3 %layer.1 = (bf16[1024,384]{1,0:T(8,128)(2,1)}, bf16[1024,384]{1,0:T(8,128)(2,1)}, bf16[32,48,768]{2,1,0:T(8,128)(2,1)}, bf16[32,24,1536]{2,1,0:T(8,128)(2,1)}, b...) custom-call(bf16[1024,384]{1,0:T(8,128)(2,1)} %refs_0_.1, ...), custom_call_target="tpu_custom_call" | custom-call | tf_op jit(solution)/shard_map/layer/pallas_call | solution.py:675
  146.6 9.5 %widen.1 = (f32[1536,768]{1,0:T(8,128)}, f32[768,1536]{1,0:T(8,128)}, f32[384,768]{1,0:T(8,128)}, f32[3,768,384]{2,1,0:T(8,128)}, f32[768]{0:T(1024)}, /*index=5...) custom-call(bf16[32,48,768]{2,1,0:T(8,128)(2,1)} %get-tuple-element., ...), custom_call_target="tpu_custom_call" | custom-call | tf_op jit(solution)/shard_map/widen/pallas_call | solution.py:756

commit v5 on v4

--- a/solution.py
+++ b/solution.py
@@ -72,10 +72,10 @@
 
 
 class Ring:
-    def __init__(self, order, extra, first, out, recv, send, keep, fin, xsend, xrecv, sems, peer, bit_of):
+    def __init__(self, order, extra, first, out, recv, send, keep, xsend, xrecv, sems, peer, bit_of):
         self.order, self.extra = order, extra
         self.first, self.out = first, out
-        self.recv, self.send, self.keep, self.fin = recv, send, keep, fin
+        self.recv, self.send, self.keep = recv, send, keep
         self.xsend, self.xrecv = xsend, xrecv
         self.ssem, self.rsem, self.lsem = sems
         self.peer = peer
@@ -105,16 +105,12 @@
         return self._copy(self.xsend, self.xrecv.at[pl.ds(j, 1)], len(self.order) + j, self.extra[j])
 
     def _ag(self, k):
-        last = len(self.order) - 1
         slot = len(self.order) + len(self.extra) + k
-        if k == last:
-            return self._copy(self.fin, self.out.at[pl.ds(self.base[k], 1)], slot, self.order[k])
-        size = self.sizes[k]
-        part = self.out.at[pl.ds(self.base[k], size)]
+        part = self.first.at[pl.ds(self.base[k], self.sizes[k])]
         return self._copy(part, part, slot, self.order[k])
 
-    def _own(self):
-        return pltpu.make_async_copy(self.fin, self.out.at[pl.ds(self.base[-1], 1)], self.lsem)
+    def _write(self):
+        return pltpu.make_async_copy(self.first, self.out, self.lsem)
 
     def start(self):
         self._rs(0).start()
@@ -127,6 +123,8 @@
 
     def reduce(self, k):
         self._rs(k).wait_recv()
+        if k == 0:
+            self._rs(0).wait_send()
         if k + 1 < len(self.order):
             half = self.sizes[k + 1]
             mine = self.mine[k + 1]
@@ -150,16 +148,15 @@
                 self._x(j).start()
                 self._x(j).wait()
                 total = self.xsend[0].astype(WIDE) + self.xrecv[j].astype(WIDE)
-            self.fin[0] = total.astype(LOW)
+            self.first[self.base[k]] = total.astype(LOW)
             self._ag(k).start()
-            self._own().start()
 
     def gather(self, k):
         self._ag(k + 1).wait_recv()
-        if k + 2 == len(self.order):
-            self._own().wait()
         if k >= 0:
             self._ag(k).start()
+        else:
+            self._write().start()
 
     def advance(self, stage):
         depth = len(self.order)
@@ -170,8 +167,10 @@
 
     def finish(self):
         for k in range(len(self.order)):
-            self._rs(k).wait_send()
+            if k > 0:
+                self._rs(k).wait_send()
             self._ag(k).wait_send()
+        self._write().wait()
 
 
 def kernel(n, refs):
@@ -182,7 +181,7 @@
      tok, qkv, sel_t, sel, blk, tokc, qc, probs, ctxc, normal_one, inverse_one, normed_one, low_one, slope,
      hidden, part, part_got, gb, gtwo, gin, back, back_got, gattn, gctx, dqc, dall, far, far_got, near,
      ctx, pre_two, down_far, down_got, stats, stats_got,
-     f_down, f_up, f_out, f_qkv, small, small_got,
+     f_down, f_up, f_out, f_qkv, small, small_got, small_sum,
      xs_send, xs_recv, lsem, rings) = refs
     rows, own = tokens.shape
     width = wout.shape[0]
@@ -263,8 +262,6 @@
     lax.fori_loop(0, tiles, qkv_tile, 0)
 
     low_lane = lax.broadcasted_iota(jnp.int32, (1, LANES), 1) < HEAD_DIM
-    tokc[...] = dot(sel[...], tok[...]).astype(LOW)
-
     def keep_head(x, e):
         return jnp.where(low_lane, x, 0.0).astype(LOW) if e == 0 else jnp.where(low_lane, 0.0, x).astype(LOW)
 
@@ -334,6 +331,7 @@
         part_ref = ctx.at[pl.ds(h * pairs + lax.rem(i, pairs), 1), q_rows]
         return x_copy(part_ref, part_ref, x_base + i)
 
+    tokc[...] = dot(sel[...], tok[...]).astype(LOW)
     attend_units = 2 * pairs
     x_base2 = x_base + attend_units
     lax.fori_loop(0, CUTS[0], attend, 0)
@@ -467,6 +465,8 @@
             send_sem=xs_send.at[x_slots + k], recv_sem=xs_recv.at[x_slots + k],
             device_id=peer(bits[k]), device_id_type=MESH)
 
+    small_write = pltpu.make_async_copy(small_sum, small_out, lsem.at[3])
+
     def small_step(k):
         small_copy(k).wait_recv()
         total = small[8 * k:8 * k + 8, :] + small_got[8 * k:8 * k + 8, :]
@@ -474,7 +474,8 @@
             small[8 * k + 8:8 * k + 16, :] = total
             small_copy(k + 1).start()
         else:
-            small_out[...] = total
+            small_sum[...] = total
+            small_write.start()
 
     def out_grad():
         put(f_out, 0, dot_tn(cat([ctxc[h * pairs + p] for p in range(pairs)]), gattn[...]).astype(LOW))
@@ -584,6 +585,7 @@
         tok_copy(r).wait_send()
     grad_out.wait()
     result_out.wait()
+    small_write.wait()
     for i in range(attend_units):
         ctx_copy(i).wait_send()
     for p in range(pairs):
@@ -626,7 +628,6 @@
             "recv": [vm((s, r, c), LOW) for s in sizes],
             "send": [vm((s, r, c), LOW) for s in sizes[1:]],
             "keep": [vm((s, r, c), WIDE) for s in sizes[1:]],
-            "fin": vm((1, r, c), LOW),
             "xsend": vm((1, r, c) if extra else (1, 8, LANES), LOW),
             "xrecv": vm((len(extra), r, c) if extra else (1, 8, LANES), LOW),
             "sems": (dma((2 * depth + len(extra),)), dma((2 * depth + len(extra),)), dma(())),
@@ -648,8 +649,8 @@
         vm((rows, own), LOW), vm((rows, own), WIDE),
         vm((2 * pairs, rows, LANES), LOW), vm((rows, own), WIDE), vm((rows, own), LOW),
         vm((rows, own), LOW), vm((rows // tile, 8, tile), WIDE), vm((rows // tile, 8, tile), WIDE),
-        *f, vm((8 * steps, ff), WIDE), vm((8 * steps, ff), WIDE),
-        dma((x_slots + steps,)), dma((x_slots + steps,)), dma((3,)),
+        *f, vm((8 * steps, ff), WIDE), vm((8 * steps, ff), WIDE), vm((8, ff), WIDE),
+        dma((x_slots + steps,)), dma((x_slots + steps,)), dma((4,)),
     ]
     plain = len(scratch)
     ring_specs = [ring_scratch(g) for g, _ in names]
@@ -659,7 +660,7 @@
     def run(*refs):
         head_refs = refs[:n_in + n_out + plain]
         rings = jax.tree.unflatten(tree, refs[n_in + n_out + plain:])
-        firsts = head_refs[-(len(groups) + 5):-5]
+        firsts = head_refs[-(len(groups) + 6):-6]
         outs = refs[n_in + 2:n_in + 2 + len(groups)]
         full = {}
         for (g, k), ring in zip(names, rings):
@@ -677,7 +678,7 @@
         out_shape=(shape((rows, own), LOW), shape((rows, own), LOW),
                    *(shape(shapes[g], LOW) for g in groups), shape((8, ff), WIDE)),
         in_specs=[hbm, hbm, hbm, hbm, hbm, v, v, v, v, v, v, v, v, v],
-        out_specs=(hbm, hbm, hbm, hbm, hbm, hbm, v),
+        out_specs=(hbm,) * 7,
         scratch_shapes=scratch + flat,
         compiler_params=pltpu.CompilerParams(
             collective_id=0, has_side_effects=True, vmem_limit_bytes=VMEM_BYTES),
@@ -688,7 +689,8 @@
 def finish(refs):
     (f_down, f_up, f_out, f_qkv, small, res_in, tok_in,
      down, up, out, qkv, gain_one, shift_one, bias, gain_two, shift_two, res, tok,
-     b_down, b_up, b_out, b_qkv, w_down, w_up, w_out, w_qkv, b_res, b_tok, isem, osem) = refs
+     b_down, b_up, b_out, b_qkv, w_down, w_up, w_out, w_qkv, b_res, b_tok, b_small, v_one, v_two, v_bias, v_three,
+     v_four, isem, osem) = refs
     width = gain_one.shape[0]
     local = qkv.shape[2]
     reads, writes = [], []
@@ -712,11 +714,7 @@
         for u in range(0, src.shape[0], step):
             jobs.append((read(src.at[pl.ds(u, step)], low.at[pl.ds(u, step)]), u, step, low, wide, dst))
     pass_on = [(read(a, b), b, c) for a, b, c in ((res_in, b_res, res), (tok_in, b_tok, tok))]
-    gain_one[...] = small[1:2, :width].reshape(width)
-    shift_one[...] = small[1:2, width:].reshape(width)
-    gain_two[...] = small[2:3, :width].reshape(width)
-    shift_two[...] = small[2:3, width:].reshape(width)
-    bias[...] = small[0:1, :].reshape(bias.shape[0])
+    small_read = read(small, b_small)
     for cp, u, step, low, wide, dst in jobs:
         cp.wait()
         r = low.shape[1]
@@ -740,6 +738,12 @@
     for cp, src, dst in pass_on:
         cp.wait()
         write(src, dst)
+    small_read.wait()
+    for row, at, vec, dst in ((1, 0, v_one, gain_one), (1, width, v_two, shift_one), (0, 0, v_bias, bias),
+                              (2, 0, v_three, gain_two), (2, width, v_four, shift_two)):
+        size = vec.shape[0]
+        vec[...] = b_small[row:row + 1, at:at + size].reshape(size)
+        write(vec, dst)
     for cp in writes:
         cp.wait()
 
@@ -749,7 +753,6 @@
     local, width, ff = three // 3, g_down.shape[2], g_up.shape[2]
     shape = jax.ShapeDtypeStruct
     hbm = pl.BlockSpec(memory_space=pl.ANY)
-    v = pl.BlockSpec(memory_space=pltpu.VMEM)
     wide = [(ff, width), (width, ff), (local, width), (3, width, local)]
     low = [g.shape for g in (g_down, g_up, g_out, g_qkv)]
     acts = [result.shape, grad_tokens.shape]
@@ -758,11 +761,12 @@
         out_shape=(*(shape(x, WIDE) for x in wide), shape((width,), WIDE), shape((width,), WIDE),
                    shape((ff,), WIDE), shape((width,), WIDE), shape((width,), WIDE),
                    *(shape(x, LOW) for x in acts)),
-        in_specs=[hbm, hbm, hbm, hbm, v, hbm, hbm],
-        out_specs=(hbm, hbm, hbm, hbm, v, v, v, v, v, hbm, hbm),
+        in_specs=[hbm] * 7,
+        out_specs=(hbm,) * 11,
         scratch_shapes=[*(pltpu.VMEM(x, LOW) for x in low), *(pltpu.VMEM(x, WIDE) for x in wide),
-                        *(pltpu.VMEM(x, LOW) for x in acts), pltpu.SemaphoreType.DMA((18,)),
-                        pltpu.SemaphoreType.DMA((18,))],
+                        *(pltpu.VMEM(x, LOW) for x in acts), pltpu.VMEM(small.shape, WIDE),
+                        *(pltpu.VMEM(x, WIDE) for x in ((width,), (width,), (ff,), (width,), (width,))),
+                        pltpu.SemaphoreType.DMA((24,)), pltpu.SemaphoreType.DMA((24,))],
         compiler_params=pltpu.CompilerParams(vmem_limit_bytes=VMEM_BYTES),
         name="widen",
     )(g_down, g_up, g_out, g_qkv, small, result, grad_tokens)

time: 157 us -> 154 us (0.981)
  Pallas kernels: 155 us -> 151 us
    pallas_call x1, Pallas kernels: 145 us -> 143 us  [build(): pl.pallas_call(run, out_shape=(shape((rows, own), LOW), shape((rows, own)...]
where the time goes in v5:
time: 154 us; the launch traced here: 153 us
  Pallas kernels  151 us (98%)
    pallas_call x1, Pallas kernels, build(): pl.pallas_call(run, out_shape=(shape((rows, own), LOW), shape((rows, own)...  143 us
    pallas_call x1, Pallas kernels, widen(): pl.pallas_call(lambda *refs: finish(refs), out_shape=(*(shape(x, WIDE) fo...  8.18 us

profile of v5, /device:TPU:0, one launch (start us, length us, event | category | flops | bytes accessed | tf_op | source)
XLA Modules:
  0.0 152.5 jit_solution(16040213876930317178)
XLA Ops:
  1.3 142.9 %layer.1 = (bf16[1024,384]{1,0:T(8,128)(2,1)}, bf16[1024,384]{1,0:T(8,128)(2,1)}, bf16[32,48,768]{2,1,0:T(8,128)(2,1)}, bf16[32,24,1536]{2,1,0:T(8,128)(2,1)}, b...) custom-call(bf16[1024,384]{1,0:T(8,128)(2,1)} %refs_0_.1, ...), custom_call_target="tpu_custom_call" | custom-call | tf_op jit(solution)/shard_map/layer/pallas_call | solution.py:676
  144.2 8.2 %widen.1 = (f32[1536,768]{1,0:T(8,128)}, f32[768,1536]{1,0:T(8,128)}, f32[384,768]{1,0:T(8,128)}, f32[3,768,384]{2,1,0:T(8,128)}, f32[768]{0:T(1024)}, /*index=5...) custom-call(bf16[32,48,768]{2,1,0:T(8,128)(2,1)} %get-tuple-element., ...), custom_call_target="tpu_custom_call" | custom-call | tf_op jit(solution)/shard_map/widen/pallas_call | solution.py:759

commit v6 on v5

--- a/solution.py
+++ b/solution.py
@@ -18,21 +18,27 @@
 MESH = pl.DeviceIdType.MESH
 VMEM_BYTES = 67043328
 CUTS = (2, 4)
-CHUNKS = {"D": 2, "U": 2, "O": 1, "Q": 2}
-ORDERS = {"D": [[0, 1, 2, 3], [0, 1, 2, 3]], "U": [[0, 2, 1, 3], [0, 1, 2, 3]],
-          "O": [[0, 1, 2, 3]], "Q": [[0, 1, 2, 3], [0, 2, 1, 3]]}
+CHUNKS = {"D": 4, "U": 3, "O": 1, "Q": 2}
+ORDERS = {"D": [[0, 1, 2, 3], [0, 1, 2, 3], [0, 1, 2, 3], [0, 1, 2, 3]],
+          "U": [[0, 1, 2, 3], [0, 1, 2, 3], [0, 2, 1, 3]],
+          "O": [[0, 1, 2, 3]],
+          "Q": [[0, 2, 1, 3], [0, 1, 2, 3]]}
 PLAN = (
-    ("D0", 0), ("D1", 0), ("U0", 0), ("attend",), ("U1", 0), ("layer", 0), ("layer", 1), ("D0", 1), ("U0", 1),
-    ("norm",), ("mb", 0), ("D1", 1), ("mb", 1), ("D0", 2), ("small", 0), ("mb", 2), ("out",), ("U1", 1),
-    ("D1", 2), ("qkv", 0), ("O0", 0), ("small", 1), ("qkv", 1), ("U0", 2), ("D0", 3), ("Q0", 0), ("U1", 2),
-    ("far", 0), ("Q1", 0), ("D1", 3), ("small", 2), ("far", 1), ("O0", 1), ("far", 2), ("far", 3), ("layer", 2),
-    ("U0", 3), ("Q0", 1), ("Q1", 1), ("D0", 4), ("small", 3), ("layer", 3), ("O0", 2), ("U1", 3), ("Q0", 2),
-    ("Q1", 2), ("near", 0), ("near", 1), ("D1", 4), ("near", 2), ("D0", 5), ("near", 3), ("grad", 0),
-    ("grad", 1), ("grad", 2), ("U0", 4), ("stat", 0), ("stat", 1), ("O0", 3), ("grad", 3), ("gout",), ("D1", 5),
-    ("U1", 4), ("stat", 2), ("D0", 6), ("Q0", 3), ("D0", 7), ("Q1", 3), ("U1", 5), ("U0", 5), ("stat", 3),
-    ("O0", 4), ("stats",), ("Q0", 4), ("result",), ("Q1", 4), ("D1", 6), ("U0", 6), ("D1", 7), ("O0", 5),
-    ("U0", 7), ("Q0", 5), ("U1", 6), ("Q1", 5), ("U1", 7), ("O0", 6), ("O0", 7), ("Q1", 6), ("Q0", 6),
-    ("Q1", 7), ("Q0", 7),
+    ("down", 0), ("down", 1), ("in",), ("D0", 0), ("D1", 0), ("down", 2), ("down", 3), ("up", 0), ("up", 1),
+    ("D2", 0), ("up", 2), ("D3", 0), ("U0", 0), ("U1", 0), ("D0", 1), ("U2", 0), ("attend",), ("ctx", 0),
+    ("layer", 0, 1), ("D1", 1), ("D0", 2), ("D2", 1), ("norm",), ("U2", 1), ("mb", 0), ("D3", 1), ("D1", 2),
+    ("D0", 3), ("mb", 1), ("D2", 2), ("small", 0), ("U0", 1), ("D3", 2), ("mb", 2), ("D1", 3), ("out",),
+    ("D0", 4), ("small", 1), ("qkv", 0), ("U1", 1), ("D2", 3), ("U0", 2), ("O0", 0), ("U2", 2), ("D3", 3),
+    ("Q0", 0), ("small", 2), ("D1", 4), ("qkv", 1), ("D0", 5), ("far", 0, 2), ("U1", 2), ("far", 2, 3),
+    ("Q1", 0), ("O0", 1), ("D2", 4), ("small", 3), ("far", 3, 4), ("U0", 3), ("layer", 1, 2), ("U2", 3),
+    ("D0", 6), ("D3", 4), ("ctx", 1), ("layer", 2, 3), ("Q0", 1), ("D0", 7), ("Q1", 1), ("D1", 5),
+    ("layer", 3, 4), ("U1", 3), ("O0", 2), ("D2", 5), ("Q0", 2), ("near", 0, 1), ("U0", 4), ("near", 1, 2),
+    ("U2", 4), ("near", 2, 3), ("D1", 6), ("D3", 5), ("near", 3, 4), ("grad", 0, 2), ("D1", 7), ("grad", 2, 4),
+    ("Q1", 2), ("gout",), ("stat", 0, 1), ("D2", 6), ("stat", 1, 2), ("U1", 4), ("O0", 3), ("D2", 7), ("U2", 5),
+    ("Q0", 3), ("U0", 5), ("stat", 2, 3), ("D3", 6), ("Q1", 3), ("D3", 7), ("U1", 5), ("stat", 3, 4), ("O0", 4),
+    ("stats",), ("U0", 6), ("U0", 7), ("result",), ("U2", 6), ("U1", 6), ("Q0", 4), ("U2", 7), ("Q1", 4),
+    ("U1", 7), ("O0", 5), ("Q0", 5), ("Q1", 5), ("O0", 6), ("O0", 7), ("Q0", 6), ("Q1", 6), ("Q0", 7),
+    ("Q1", 7),
 )
 
 
@@ -379,15 +385,24 @@
 
     ring = {name: Ring(peer=peer, bit_of=bit_of, **r) for name, r in rings.items()}
 
-    def down_tile(i, c):
-        cols = pl.ds(pl.multiple_of(i * ff_tile, ff_tile), ff_tile)
-        put(f_down, i * (ff_tile * f_down.shape[0] // ff), dot_tn(hidden[:, cols], gb[...]).astype(LOW))
-        return c
-
-    def up_grad_tile(i, c):
-        cols = pl.ds(pl.multiple_of(i * ff_tile, ff_tile), ff_tile)
-        put(f_up, i * (ff_tile * f_up.shape[0] // width), dot_tn(low_one[:, cols], gin[...]).astype(LOW))
-        return c
+    def by_tiles(group, k, first, grad):
+        units = first.shape[0] // CHUNKS[group]
+        size = units * first.shape[1]
+        step = 256 if size % 256 == 0 else 384
+
+        def one_tile(i, c):
+            at = k * size + i * step
+            put(first, k * units + i * (step * units // size), grad(pl.ds(pl.multiple_of(at, LANES), step)))
+            return c
+
+        lax.fori_loop(0, size // step, one_tile, 0)
+        ring["%s%d" % (group, k)].start()
+
+    def down_grad(k):
+        by_tiles("D", k, f_down, lambda cols: dot_tn(hidden[:, cols], gb[...]).astype(LOW))
+
+    def up_grad(k):
+        by_tiles("U", k, f_up, lambda cols: dot_tn(low_one[:, cols], gin[...]).astype(LOW))
 
     def in_tile(i, c):
         cols = pl.ds(pl.multiple_of(i * ff_tile, ff_tile), ff_tile)
@@ -397,15 +412,11 @@
         return c
 
     back_copy = x_copy(back, back_got, x_base2 + 1)
-    for k in range(2):
-        lax.fori_loop(k * ff // (2 * ff_tile), (k + 1) * ff // (2 * ff_tile), down_tile, 0)
-        ring["D%d" % k].start()
-    lax.fori_loop(0, ff // ff_tile, in_tile, 0)
-    back[...] = dot_nt(gin[...], wup[...]).astype(LOW)
-    back_copy.start()
-    for k in range(2):
-        lax.fori_loop(k * width // (2 * ff_tile), (k + 1) * width // (2 * ff_tile), up_grad_tile, 0)
-        ring["U%d" % k].start()
+
+    def input_grad():
+        lax.fori_loop(0, ff // ff_tile, in_tile, 0)
+        back[...] = dot_nt(gin[...], wup[...]).astype(LOW)
+        back_copy.start()
 
     def attend_more():
         lax.fori_loop(CUTS[1], attend_units, attend, 0)
@@ -481,16 +492,13 @@
         put(f_out, 0, dot_tn(cat([ctxc[h * pairs + p] for p in range(pairs)]), gattn[...]).astype(LOW))
         ring["O0"].start()
 
-    def qkv_grad_tile(i, c):
-        cols = pl.ds(pl.multiple_of(i * ff_tile, ff_tile), ff_tile)
-        gq = dot_tn(tokc[:, cols], cat([dqc[p] for p in range(pairs)]))
-        gkv = dot_tn(tok[:, cols], cat([dall[pairs + j] for j in range(2 * pairs)]))
-        put(f_qkv, i * (ff_tile * f_qkv.shape[0] // width), cat([gq, gkv]).astype(LOW))
-        return c
-
     def qkv_grad(k):
-        lax.fori_loop(k * width // (2 * ff_tile), (k + 1) * width // (2 * ff_tile), qkv_grad_tile, 0)
-        ring["Q%d" % k].start()
+        def grad(cols):
+            gq = dot_tn(tokc[:, cols], cat([dqc[p] for p in range(pairs)]))
+            gkv = dot_tn(tok[:, cols], cat([dall[pairs + j] for j in range(2 * pairs)]))
+            return cat([gq, gkv]).astype(LOW)
+
+        by_tiles("Q", k, f_qkv, grad)
 
     def far_copy(r):
         return x_copy(far.at[row_tile(r)], far_got.at[row_tile(r)], x_base2 + 2 + r)
@@ -518,11 +526,11 @@
     def down_copy(r):
         return x_copy(down_far.at[row_tile(r)], down_got.at[row_tile(r)], x_base2 + 2 + tiles + r)
 
+    def ctx_wait(block):
+        for i in range(block * pairs, (block + 1) * pairs):
+            ctx_copy(i).wait_recv()
+
     def layer_tile(r):
-        if r * tile % block_len == 0:
-            block = r * tile // block_len
-            for i in range(block * pairs, (block + 1) * pairs):
-                ctx_copy(i).wait_recv()
         rs = row_tile(r)
         pre_r = tok[rs, :].astype(WIDE) + dot(cat([ctx[j, rs, :] for j in range(2 * pairs)]), wout[...])
         normed = normalize(pre_r)[0] * gain_one[...] + shift_one[...]
@@ -569,13 +577,15 @@
         result_out.start()
 
     x_slots = x_base2 + 3 + 2 * tiles
-    steps = {"norm": first_norm, "attend": attend_more, "mb": lambda p: masked_backward(p, 0), "out": out_grad,
-             "qkv": qkv_grad, "far": far_tile, "near": near_tile, "grad": grad_tile, "layer": layer_tile,
-             "stat": stat_tile, "stats": stats_copy.start, "gout": grad_out.start, "result": write_result,
-             "small": small_step}
+    steps = {"down": down_grad, "in": input_grad, "up": up_grad, "norm": first_norm, "attend": attend_more,
+             "mb": lambda p: masked_backward(p, 0), "out": out_grad, "qkv": qkv_grad, "gout": grad_out.start,
+             "stats": stats_copy.start, "result": write_result, "small": small_step, "ctx": ctx_wait}
+    looped = {"far": far_tile, "near": near_tile, "grad": grad_tile, "layer": layer_tile, "stat": stat_tile}
     for name, *at in PLAN:
         if name in ring:
             ring[name].advance(at[0])
+        elif name in looped:
+            lax.fori_loop(at[0], at[1], lambda r, c, name=name: looped[name](r) or c, 0)
         else:
             steps[name](*at)
     for k in range(min(len(bits), 4), len(bits)):

time: 154 us -> 148 us (0.961)
  Pallas kernels: 151 us -> 147 us
    pallas_call x1, Pallas kernels: 143 us -> 138 us  [build(): pl.pallas_call(run, out_shape=(shape((rows, own), LOW), shape((rows, own)...]
where the time goes in v6:
time: 148 us
  Pallas kernels  147 us (99%)
  between operations  1.48 us (1%)
    pallas_call x1, Pallas kernels, build(): pl.pallas_call(run, out_shape=(shape((rows, own), LOW), shape((rows, own)...  138 us
    pallas_call x1, Pallas kernels, widen(): pl.pallas_call(lambda *refs: finish(refs), out_shape=(*(shape(x, WIDE) fo...  8.17 us

profile of v6, /device:TPU:0, one launch (start us, length us, event | category | flops | bytes accessed | tf_op | source)
XLA Modules:
  0.0 148.1 jit_solution(14624003837641155619)
XLA Ops:
  1.3 138.4 %layer.1 = (bf16[1024,384]{1,0:T(8,128)(2,1)}, bf16[1024,384]{1,0:T(8,128)(2,1)}, bf16[64,24,768]{2,1,0:T(8,128)(2,1)}, bf16[48,16,1536]{2,1,0:T(8,128)(2,1)}, b...) custom-call(bf16[1024,384]{1,0:T(8,128)(2,1)} %refs_0_.1, ...), custom_call_target="tpu_custom_call" | custom-call | tf_op jit(solution)/shard_map/layer/pallas_call | solution.py:686
  139.7 8.2 %widen.1 = (f32[1536,768]{1,0:T(8,128)}, f32[768,1536]{1,0:T(8,128)}, f32[384,768]{1,0:T(8,128)}, f32[3,768,384]{2,1,0:T(8,128)}, f32[768]{0:T(1024)}, /*index=5...) custom-call(bf16[64,24,768]{2,1,0:T(8,128)(2,1)} %get-tuple-element., ...), custom_call_target="tpu_custom_call" | custom-call | tf_op jit(solution)/shard_map/widen/pallas_call | solution.py:769

commit v7 on v6

--- a/solution.py
+++ b/solution.py
@@ -18,27 +18,26 @@
 MESH = pl.DeviceIdType.MESH
 VMEM_BYTES = 67043328
 CUTS = (2, 4)
-CHUNKS = {"D": 4, "U": 3, "O": 1, "Q": 2}
-ORDERS = {"D": [[0, 1, 2, 3], [0, 1, 2, 3], [0, 1, 2, 3], [0, 1, 2, 3]],
-          "U": [[0, 1, 2, 3], [0, 1, 2, 3], [0, 2, 1, 3]],
+CHUNKS = {"D": 3, "U": 3, "O": 1, "Q": 2}
+ORDERS = {"D": [[0, 1, 2, 3], [0, 2, 3, 1], [0, 2, 1, 3]],
+          "U": [[0, 1, 2, 3], [0, 1, 2, 3], [0, 1, 2, 3]],
           "O": [[0, 1, 2, 3]],
-          "Q": [[0, 2, 1, 3], [0, 1, 2, 3]]}
+          "Q": [[0, 1, 2, 3], [0, 1, 3, 2]]}
 PLAN = (
-    ("down", 0), ("down", 1), ("in",), ("D0", 0), ("D1", 0), ("down", 2), ("down", 3), ("up", 0), ("up", 1),
-    ("D2", 0), ("up", 2), ("D3", 0), ("U0", 0), ("U1", 0), ("D0", 1), ("U2", 0), ("attend",), ("ctx", 0),
-    ("layer", 0, 1), ("D1", 1), ("D0", 2), ("D2", 1), ("norm",), ("U2", 1), ("mb", 0), ("D3", 1), ("D1", 2),
-    ("D0", 3), ("mb", 1), ("D2", 2), ("small", 0), ("U0", 1), ("D3", 2), ("mb", 2), ("D1", 3), ("out",),
-    ("D0", 4), ("small", 1), ("qkv", 0), ("U1", 1), ("D2", 3), ("U0", 2), ("O0", 0), ("U2", 2), ("D3", 3),
-    ("Q0", 0), ("small", 2), ("D1", 4), ("qkv", 1), ("D0", 5), ("far", 0, 2), ("U1", 2), ("far", 2, 3),
-    ("Q1", 0), ("O0", 1), ("D2", 4), ("small", 3), ("far", 3, 4), ("U0", 3), ("layer", 1, 2), ("U2", 3),
-    ("D0", 6), ("D3", 4), ("ctx", 1), ("layer", 2, 3), ("Q0", 1), ("D0", 7), ("Q1", 1), ("D1", 5),
-    ("layer", 3, 4), ("U1", 3), ("O0", 2), ("D2", 5), ("Q0", 2), ("near", 0, 1), ("U0", 4), ("near", 1, 2),
-    ("U2", 4), ("near", 2, 3), ("D1", 6), ("D3", 5), ("near", 3, 4), ("grad", 0, 2), ("D1", 7), ("grad", 2, 4),
-    ("Q1", 2), ("gout",), ("stat", 0, 1), ("D2", 6), ("stat", 1, 2), ("U1", 4), ("O0", 3), ("D2", 7), ("U2", 5),
-    ("Q0", 3), ("U0", 5), ("stat", 2, 3), ("D3", 6), ("Q1", 3), ("D3", 7), ("U1", 5), ("stat", 3, 4), ("O0", 4),
-    ("stats",), ("U0", 6), ("U0", 7), ("result",), ("U2", 6), ("U1", 6), ("Q0", 4), ("U2", 7), ("Q1", 4),
-    ("U1", 7), ("O0", 5), ("Q0", 5), ("Q1", 5), ("O0", 6), ("O0", 7), ("Q0", 6), ("Q1", 6), ("Q0", 7),
-    ("Q1", 7),
+    ("down", 0), ("down", 1), ("in",), ("D0", 0), ("D1", 0), ("down", 2), ("up", 0), ("up", 1), ("up", 2),
+    ("D2", 0), ("attend",), ("U0", 0), ("U1", 0), ("U2", 0), ("D0", 1), ("D1", 1), ("ctx", 0), ("layer", 0, 1),
+    ("D2", 1), ("norm",), ("U0", 1), ("D0", 2), ("mb", 0), ("mb", 1), ("D1", 2), ("U1", 1), ("U0", 2),
+    ("small", 0), ("mb", 2), ("D0", 3), ("U2", 1), ("out",), ("U1", 2), ("qkv", 0), ("O0", 0), ("U0", 3),
+    ("small", 1), ("far", 0, 1), ("qkv", 1), ("Q0", 0), ("D0", 4), ("U2", 2), ("far", 1, 2), ("D2", 2),
+    ("U1", 3), ("Q1", 0), ("O0", 1), ("small", 2), ("far", 2, 3), ("U0", 4), ("ctx", 1), ("layer", 2, 3),
+    ("D0", 5), ("U2", 3), ("Q0", 1), ("D2", 3), ("small", 3), ("far", 3, 4), ("layer", 3, 4), ("O0", 2),
+    ("Q1", 1), ("near", 0, 1), ("U2", 4), ("near", 1, 2), ("U0", 5), ("Q0", 2), ("near", 2, 3), ("U1", 4),
+    ("D0", 6), ("near", 3, 4), ("D2", 4), ("grad", 0, 1), ("layer", 1, 2), ("D1", 3), ("O0", 3), ("D0", 7),
+    ("U0", 6), ("U2", 5), ("Q1", 2), ("grad", 1, 4), ("gout",), ("stat", 0, 1), ("U0", 7), ("stat", 2, 3),
+    ("Q0", 3), ("D1", 4), ("U1", 5), ("stat", 3, 4), ("O0", 4), ("Q1", 3), ("U2", 6), ("Q0", 4),
+    ("stat", 1, 2), ("stats",), ("U2", 7), ("O0", 5), ("U1", 6), ("Q1", 4), ("result",), ("D1", 5), ("U1", 7), ("D2", 5),
+    ("Q0", 5), ("O0", 6), ("O0", 7), ("Q1", 5), ("Q0", 6), ("D1", 6), ("Q0", 7), ("D1", 7), ("D2", 6),
+    ("Q1", 6), ("D2", 7), ("Q1", 7),
 )
 
 

time: 148 us -> 141 us (0.953)
  Pallas kernels: 147 us -> 139 us
    pallas_call x1, Pallas kernels: 138 us -> 131 us  [build(): pl.pallas_call(run, out_shape=(shape((rows, own), LOW), shape((rows, own)...]
where the time goes in v7:
time: 141 us
  Pallas kernels  139 us (99%)
  between operations  1.48 us (1%)
    pallas_call x1, Pallas kernels, build(): pl.pallas_call(run, out_shape=(shape((rows, own), LOW), shape((rows, own)...  131 us
    pallas_call x1, Pallas kernels, widen(): pl.pallas_call(lambda *refs: finish(refs), out_shape=(*(shape(x, WIDE) fo...  8.18 us

profile of v7, /device:TPU:0, one launch (start us, length us, event | category | flops | bytes accessed | tf_op | source)
XLA Modules:
  0.0 140.8 jit_solution(14988681225666210719)
XLA Ops:
  1.3 131.1 %layer.1 = (bf16[1024,384]{1,0:T(8,128)(2,1)}, bf16[1024,384]{1,0:T(8,128)(2,1)}, bf16[48,32,768]{2,1,0:T(8,128)(2,1)}, bf16[48,16,1536]{2,1,0:T(8,128)(2,1)}, b...) custom-call(bf16[1024,384]{1,0:T(8,128)(2,1)} %refs_0_.1, ...), custom_call_target="tpu_custom_call" | custom-call | tf_op jit(solution)/shard_map/layer/pallas_call | solution.py:685
  132.4 8.2 %widen.1 = (f32[1536,768]{1,0:T(8,128)}, f32[768,1536]{1,0:T(8,128)}, f32[384,768]{1,0:T(8,128)}, f32[3,768,384]{2,1,0:T(8,128)}, f32[768]{0:T(1024)}, /*index=5...) custom-call(bf16[48,32,768]{2,1,0:T(8,128)(2,1)} %get-tuple-element., ...), custom_call_target="tpu_custom_call" | custom-call | tf_op jit(solution)/shard_map/widen/pallas_call | solution.py:768

commit v8 on v7

--- a/solution.py
+++ b/solution.py
@@ -19,25 +19,24 @@
 VMEM_BYTES = 67043328
 CUTS = (2, 4)
 CHUNKS = {"D": 3, "U": 3, "O": 1, "Q": 2}
-ORDERS = {"D": [[0, 1, 2, 3], [0, 2, 3, 1], [0, 2, 1, 3]],
-          "U": [[0, 1, 2, 3], [0, 1, 2, 3], [0, 1, 2, 3]],
+ORDERS = {"D": [[0, 2, 3, 1], [0, 1, 2, 3], [0, 1, 2, 3]],
+          "U": [[0, 2, 1, 3], [0, 1, 2, 3], [0, 1, 2, 3]],
           "O": [[0, 1, 2, 3]],
-          "Q": [[0, 1, 2, 3], [0, 1, 3, 2]]}
+          "Q": [[0, 1, 2, 3], [0, 1, 2, 3]]}
 PLAN = (
-    ("down", 0), ("down", 1), ("in",), ("D0", 0), ("D1", 0), ("down", 2), ("up", 0), ("up", 1), ("up", 2),
-    ("D2", 0), ("attend",), ("U0", 0), ("U1", 0), ("U2", 0), ("D0", 1), ("D1", 1), ("ctx", 0), ("layer", 0, 1),
-    ("D2", 1), ("norm",), ("U0", 1), ("D0", 2), ("mb", 0), ("mb", 1), ("D1", 2), ("U1", 1), ("U0", 2),
-    ("small", 0), ("mb", 2), ("D0", 3), ("U2", 1), ("out",), ("U1", 2), ("qkv", 0), ("O0", 0), ("U0", 3),
-    ("small", 1), ("far", 0, 1), ("qkv", 1), ("Q0", 0), ("D0", 4), ("U2", 2), ("far", 1, 2), ("D2", 2),
-    ("U1", 3), ("Q1", 0), ("O0", 1), ("small", 2), ("far", 2, 3), ("U0", 4), ("ctx", 1), ("layer", 2, 3),
-    ("D0", 5), ("U2", 3), ("Q0", 1), ("D2", 3), ("small", 3), ("far", 3, 4), ("layer", 3, 4), ("O0", 2),
-    ("Q1", 1), ("near", 0, 1), ("U2", 4), ("near", 1, 2), ("U0", 5), ("Q0", 2), ("near", 2, 3), ("U1", 4),
-    ("D0", 6), ("near", 3, 4), ("D2", 4), ("grad", 0, 1), ("layer", 1, 2), ("D1", 3), ("O0", 3), ("D0", 7),
-    ("U0", 6), ("U2", 5), ("Q1", 2), ("grad", 1, 4), ("gout",), ("stat", 0, 1), ("U0", 7), ("stat", 2, 3),
-    ("Q0", 3), ("D1", 4), ("U1", 5), ("stat", 3, 4), ("O0", 4), ("Q1", 3), ("U2", 6), ("Q0", 4),
-    ("stat", 1, 2), ("stats",), ("U2", 7), ("O0", 5), ("U1", 6), ("Q1", 4), ("result",), ("D1", 5), ("U1", 7), ("D2", 5),
-    ("Q0", 5), ("O0", 6), ("O0", 7), ("Q1", 5), ("Q0", 6), ("D1", 6), ("Q0", 7), ("D1", 7), ("D2", 6),
-    ("Q1", 6), ("D2", 7), ("Q1", 7),
+    ("down", 0), ("in",), ("D0", 0), ("down", 1), ("down", 2), ("up", 0), ("up", 1), ("D1", 0), ("up", 2),
+    ("D2", 0), ("U0", 0), ("U1", 0), ("attend",), ("U2", 0), ("D0", 1), ("ctx", 0), ("layer", 1, 2), ("D1", 1),
+    ("U0", 1), ("norm",), ("D2", 1), ("mb", 0), ("D0", 2), ("D1", 2), ("mb", 1), ("U1", 1), ("D2", 2),
+    ("small", 0), ("mb", 2), ("D1", 3), ("out",), ("U2", 1), ("U1", 2), ("qkv", 0), ("O0", 0), ("U0", 2),
+    ("D2", 3), ("small", 1), ("qkv", 1), ("Q0", 0), ("D1", 4), ("U2", 2), ("far", 0, 2), ("Q1", 0), ("U1", 3),
+    ("O0", 1), ("small", 2), ("far", 2, 3), ("U0", 3), ("ctx", 1), ("layer", 2, 3), ("D1", 5), ("D2", 4),
+    ("Q0", 1), ("D0", 3), ("U2", 3), ("small", 3), ("far", 3, 4), ("O0", 2), ("layer", 0, 1), ("U1", 4),
+    ("Q1", 1), ("D2", 5), ("layer", 3, 4), ("Q0", 2), ("D1", 6), ("U2", 4), ("O0", 3), ("near", 0, 1),
+    ("U1", 5), ("near", 1, 2), ("D1", 7), ("near", 2, 4), ("Q1", 2), ("D2", 6), ("grad", 0, 3), ("stat", 1, 2),
+    ("Q0", 3), ("stat", 2, 3), ("D2", 7), ("grad", 3, 4), ("gout",), ("U2", 5), ("O0", 4), ("U1", 6), ("Q1", 3),
+    ("U0", 4), ("U1", 7), ("stat", 0, 1), ("Q0", 4), ("D0", 4), ("O0", 5), ("U2", 6), ("Q1", 4), ("U2", 7),
+    ("stat", 3, 4), ("U0", 5), ("Q0", 5), ("stats",), ("result",), ("O0", 6), ("D0", 5), ("Q1", 5), ("O0", 7),
+    ("Q0", 6), ("U0", 6), ("Q0", 7), ("U0", 7), ("Q1", 6), ("D0", 6), ("Q1", 7), ("D0", 7),
 )
 
 

time: 141 us -> 143 us (1.014)
  Pallas kernels: 139 us -> 141 us
where the time goes in v8:
time: 143 us; the launch traced here: 142 us
  Pallas kernels  141 us (99%)
  between operations  1.48 us (1%)
    pallas_call x1, Pallas kernels, build(): pl.pallas_call(run, out_shape=(shape((rows, own), LOW), shape((rows, own)...  132 us
    pallas_call x1, Pallas kernels, widen(): pl.pallas_call(lambda *refs: finish(refs), out_shape=(*(shape(x, WIDE) fo...  8.18 us

profile of v8, /device:TPU:0, one launch (start us, length us, event | category | flops | bytes accessed | tf_op | source)
XLA Modules:
  0.0 142.0 jit_solution(2227590688120606705)
XLA Ops:
  1.3 132.4 %layer.1 = (bf16[1024,384]{1,0:T(8,128)(2,1)}, bf16[1024,384]{1,0:T(8,128)(2,1)}, bf16[48,32,768]{2,1,0:T(8,128)(2,1)}, bf16[48,16,1536]{2,1,0:T(8,128)(2,1)}, b...) custom-call(bf16[1024,384]{1,0:T(8,128)(2,1)} %refs_0_.1, ...), custom_call_target="tpu_custom_call" | custom-call | tf_op jit(solution)/shard_map/layer/pallas_call | solution.py:684
  133.7 8.2 %widen.1 = (f32[1536,768]{1,0:T(8,128)}, f32[768,1536]{1,0:T(8,128)}, f32[384,768]{1,0:T(8,128)}, f32[3,768,384]{2,1,0:T(8,128)}, f32[768]{0:T(1024)}, /*index=5...) custom-call(bf16[48,32,768]{2,1,0:T(8,128)(2,1)} %get-tuple-element., ...), custom_call_target="tpu_custom_call" | custom-call | tf_op jit(solution)/shard_map/widen/pallas_call | solution.py:767

commit v9 on v7

--- a/solution.py
+++ b/solution.py
@@ -19,24 +19,24 @@
 VMEM_BYTES = 67043328
 CUTS = (2, 4)
 CHUNKS = {"D": 3, "U": 3, "O": 1, "Q": 2}
-ORDERS = {"D": [[0, 1, 2, 3], [0, 2, 3, 1], [0, 2, 1, 3]],
-          "U": [[0, 1, 2, 3], [0, 1, 2, 3], [0, 1, 2, 3]],
+ORDERS = {"D": [[0, 1, 2, 3], [0, 1, 2, 3], [0, 2, 1, 3]],
+          "U": [[0, 1, 2, 3], [0, 2, 1, 3], [0, 1, 2, 3]],
           "O": [[0, 1, 2, 3]],
           "Q": [[0, 1, 2, 3], [0, 1, 3, 2]]}
 PLAN = (
-    ("down", 0), ("down", 1), ("in",), ("D0", 0), ("D1", 0), ("down", 2), ("up", 0), ("up", 1), ("up", 2),
-    ("D2", 0), ("attend",), ("U0", 0), ("U1", 0), ("U2", 0), ("D0", 1), ("D1", 1), ("ctx", 0), ("layer", 0, 1),
-    ("D2", 1), ("norm",), ("U0", 1), ("D0", 2), ("mb", 0), ("mb", 1), ("D1", 2), ("U1", 1), ("U0", 2),
-    ("small", 0), ("mb", 2), ("D0", 3), ("U2", 1), ("out",), ("U1", 2), ("qkv", 0), ("O0", 0), ("U0", 3),
-    ("small", 1), ("far", 0, 1), ("qkv", 1), ("Q0", 0), ("D0", 4), ("U2", 2), ("far", 1, 2), ("D2", 2),
-    ("U1", 3), ("Q1", 0), ("O0", 1), ("small", 2), ("far", 2, 3), ("U0", 4), ("ctx", 1), ("layer", 2, 3),
-    ("D0", 5), ("U2", 3), ("Q0", 1), ("D2", 3), ("small", 3), ("far", 3, 4), ("layer", 3, 4), ("O0", 2),
-    ("Q1", 1), ("near", 0, 1), ("U2", 4), ("near", 1, 2), ("U0", 5), ("Q0", 2), ("near", 2, 3), ("U1", 4),
-    ("D0", 6), ("near", 3, 4), ("D2", 4), ("grad", 0, 1), ("layer", 1, 2), ("D1", 3), ("O0", 3), ("D0", 7),
-    ("U0", 6), ("U2", 5), ("Q1", 2), ("grad", 1, 4), ("gout",), ("stat", 0, 1), ("U0", 7), ("stat", 2, 3),
-    ("Q0", 3), ("D1", 4), ("U1", 5), ("stat", 3, 4), ("O0", 4), ("Q1", 3), ("U2", 6), ("Q0", 4),
-    ("stat", 1, 2), ("stats",), ("U2", 7), ("O0", 5), ("U1", 6), ("Q1", 4), ("result",), ("D1", 5), ("U1", 7), ("D2", 5),
-    ("Q0", 5), ("O0", 6), ("O0", 7), ("Q1", 5), ("Q0", 6), ("D1", 6), ("Q0", 7), ("D1", 7), ("D2", 6),
+    ("down", 0), ("down", 1), ("down", 2), ("in",), ("D0", 0), ("D1", 0), ("D2", 0), ("up", 0), ("up", 1),
+    ("up", 2), ("attend",), ("U0", 0), ("U1", 0), ("U2", 0), ("D0", 1), ("ctx", 0), ("layer", 0, 1), ("D2", 1),
+    ("D1", 1), ("norm",), ("U1", 1), ("mb", 0), ("D0", 2), ("U0", 1), ("mb", 1), ("D1", 2), ("small", 0),
+    ("mb", 2), ("U2", 1), ("D0", 3), ("U0", 2), ("out",), ("qkv", 0), ("D1", 3), ("O0", 0), ("U1", 2),
+    ("small", 1), ("U2", 2), ("far", 0, 1), ("Q0", 0), ("qkv", 1), ("D0", 4), ("far", 1, 2), ("U0", 3),
+    ("small", 2), ("far", 2, 3), ("O0", 1), ("Q1", 0), ("D1", 4), ("ctx", 1), ("layer", 2, 3), ("U1", 3),
+    ("D0", 5), ("Q0", 1), ("U2", 3), ("small", 3), ("O0", 2), ("far", 3, 4), ("near", 0, 1), ("U0", 4),
+    ("near", 1, 2), ("D1", 5), ("near", 2, 4), ("Q1", 1), ("U1", 4), ("grad", 0, 1), ("layer", 3, 4), ("Q0", 2),
+    ("U2", 4), ("D0", 6), ("O0", 3), ("grad", 1, 3), ("U0", 5), ("layer", 1, 2), ("D2", 2), ("D0", 7),
+    ("D1", 6), ("Q1", 2), ("grad", 3, 4), ("gout",), ("stat", 0, 1), ("Q0", 3), ("U2", 5), ("stat", 2, 3),
+    ("D1", 7), ("O0", 4), ("stat", 3, 4), ("D2", 3), ("Q1", 3), ("Q0", 4), ("O0", 5), ("stat", 1, 2), ("U0", 6),
+    ("stats",), ("U2", 6), ("D2", 4), ("Q1", 4), ("U1", 5), ("U0", 7), ("U2", 7), ("result",), ("Q0", 5),
+    ("O0", 6), ("O0", 7), ("D2", 5), ("Q1", 5), ("U1", 6), ("Q0", 6), ("U1", 7), ("Q0", 7), ("D2", 6),
     ("Q1", 6), ("D2", 7), ("Q1", 7),
 )
 

time: 141 us -> 140 us (level)
  Pallas kernels: 139 us -> 137 us
    pallas_call x1, Pallas kernels: 131 us -> 129 us  [build(): pl.pallas_call(run, out_shape=(shape((rows, own), LOW), shape((rows, own)...]
where the time goes in v9:
time: 140 us; the launch traced here: 139 us
  Pallas kernels  137 us (98%)
  between operations  1.48 us (1%)
    pallas_call x1, Pallas kernels, build(): pl.pallas_call(run, out_shape=(shape((rows, own), LOW), shape((rows, own)...  129 us
    pallas_call x1, Pallas kernels, widen(): pl.pallas_call(lambda *refs: finish(refs), out_shape=(*(shape(x, WIDE) fo...  8.18 us

profile of v9, /device:TPU:0, one launch (start us, length us, event | category | flops | bytes accessed | tf_op | source)
XLA Modules:
  0.0 138.9 jit_solution(15434670817046105663)
XLA Ops:
  1.3 129.2 %layer.1 = (bf16[1024,384]{1,0:T(8,128)(2,1)}, bf16[1024,384]{1,0:T(8,128)(2,1)}, bf16[48,32,768]{2,1,0:T(8,128)(2,1)}, bf16[48,16,1536]{2,1,0:T(8,128)(2,1)}, b...) custom-call(bf16[1024,384]{1,0:T(8,128)(2,1)} %refs_0_.1, ...), custom_call_target="tpu_custom_call" | custom-call | tf_op jit(solution)/shard_map/layer/pallas_call | solution.py:685
  130.5 8.2 %widen.1 = (f32[1536,768]{1,0:T(8,128)}, f32[768,1536]{1,0:T(8,128)}, f32[384,768]{1,0:T(8,128)}, f32[3,768,384]{2,1,0:T(8,128)}, f32[768]{0:T(1024)}, /*index=5...) custom-call(bf16[48,32,768]{2,1,0:T(8,128)(2,1)} %get-tuple-element., ...), custom_call_target="tpu_custom_call" | custom-call | tf_op jit(solution)/shard_map/widen/pallas_call | solution.py:768
